TPU v7x, 32 devices: a whole 2x2x4 slice. The times are simulated.
32 devices in a mesh: grp: 4 (over x, core), pts: 8 (over z, y).
Axes of the slice: x: 2, y: 2, z: 4, core: 2. Of those that a mesh axis runs over, the one named last changes fastest.
Arguments:
- points: float32 [8192, 2048], P(('grp', 'pts')), may hold values from -2 to 2
- log_factor: float32 [8192, 256], P(('grp', 'pts')), may hold values from -40 to 320
- masses: float32 [8192], P(('grp', 'pts')), may hold values from 0.1 to 12
Outputs:
- factors: float32 [8192, 256], P(('grp', 'pts'))
All inputs are finite; a program needn't handle non-finite values. Where the computation divides by a largest or mean magnitude, that divisor is 1e-20 or more.
Results may differ from a plain program's by a relative error of at most 0.0003.
Values sent between devices are 32-bit elements; how exact they have to be, the bound alone decides.
No kernel may reach another device: no remote copies, remote signals or barrier semaphores. Data moves between devices by JAX's collectives and lax.ppermute only.
A program may use at most 64 MiB of HBM per device.

v0:
```python
import functools

import jax
import jax.numpy as jnp
from jax import lax
from jax.experimental import pallas as pl
from jax.experimental.pallas import tpu as pltpu
from jax.sharding import Mesh, PartitionSpec as P


ITERS = 2

step_scale = 4.0
highest = lax.Precision.HIGHEST
PAD = 8


def swap(value, axis):
    return lax.ppermute(value, axis, [(0, 1), (1, 0)])


def together(*values):
    return lax.optimization_barrier(values)


def contract_rows(left, right):
    return lax.dot_general(
        left,
        right,
        (((0,), (0,)), ((), ())),
        precision=highest,
        preferred_element_type=jnp.float32,
    )


def times(left, right):
    return jnp.dot(left, right, precision=highest, preferred_element_type=jnp.float32)


def own_place(bits):
    place = lax.axis_index("core")
    for axis in bits:
        place = 2 * place + lax.axis_index(axis)
    return place


def column_copies(source, begin, parts, place, sems):
    count = sems.shape[0]
    width = source.shape[1] // count
    rows = parts[0].shape[0]
    copies = []
    for i in range(count):
        column = pl.multiple_of((i ^ place) * width, width)
        copies.append(
            pltpu.make_async_copy(
                source.at[pl.ds(begin, rows), pl.ds(column, width)],
                parts[2 * i // count].at[:, pl.ds(i % (count // 2) * width, width)],
                sems.at[i],
            )
        )
    return copies


def put_rows(parts, targets, top, sems):
    rows = parts[0].shape[0]
    copies = [
        pltpu.make_async_copy(parts[i], targets[i].at[pl.ds(top, rows), :], sems.at[i])
        for i in range(2)
    ]
    for copy in copies:
        copy.start()
    for copy in copies:
        copy.wait()


def base_kernel(bits, points, near, far, near_part, far_part, sems, out_sems):
    parts = near_part, far_part
    copies = column_copies(points, 0, parts, own_place(bits), sems)
    for copy in copies:
        copy.start()
    for copy in copies:
        copy.wait()
    put_rows(parts, (near, far), 0, out_sems)


def extra_kernel(
    bits, points, first, second, near_in, far_in, near, far, near_part, far_part, sems, out_sems
):
    del near_in, far_in
    parts = near_part, far_part
    place = own_place(bits)
    group = 2 * lax.axis_index("side") + lax.axis_index("core")
    half = first.shape[0]

    @pl.when((group == 0) | (group == 2))
    def _():
        for copy in column_copies(first, 0, parts, place, sems):
            copy.start()

    @pl.when(group == 1)
    def _():
        for copy in column_copies(second, 0, parts, place, sems):
            copy.start()

    @pl.when(group == 3)
    def _():
        for copy in column_copies(points, half, parts, place, sems):
            copy.start()

    for copy in column_copies(first, 0, parts, place, sems):
        copy.wait()
    put_rows(parts, (near, far), points.shape[0], out_sems)


def arrange_base(points, bits):
    rows, width = points.shape
    blocks = 2 ** (1 + len(bits))
    if (width // blocks) % 128:
        order = jnp.arange(blocks) ^ own_place(bits)
        whole = points.reshape(rows, blocks, -1)[:, order].reshape(rows, width)
        return whole[:, : width // 2], whole[:, width // 2 :]
    return arrange_call(base_kernel, points, rows, bits, {})(points)


def arrange_extra(points, first, second, near, far, bits):
    rows, width = points.shape
    blocks = 2 ** (1 + len(bits))
    half = rows // 2
    if (width // blocks) % 128:
        group = 2 * lax.axis_index("side") + lax.axis_index("core")
        extra = jnp.where(group == 1, second, jnp.where(group == 3, points[half:], first))
        extra = arrange_base(extra, bits)
        return tuple(jnp.concatenate(pair, axis=0) for pair in zip((near, far), extra))
    return arrange_call(extra_kernel, points, half, bits, {3: 0, 4: 1})(
        points, first, second, near, far
    )


def arrange_call(kernel, points, count, bits, aliases):
    rows, width = points.shape
    anywhere = pl.BlockSpec(memory_space=pl.ANY)
    shape = jax.ShapeDtypeStruct((rows + rows // 2, width // 2), points.dtype)
    part = pltpu.VMEM((count, width // 2), points.dtype)
    return pl.pallas_call(
        functools.partial(kernel, bits),
        out_shape=(shape, shape),
        in_specs=[anywhere] * (5 if aliases else 1),
        out_specs=(anywhere, anywhere),
        scratch_shapes=[
            part,
            part,
            pltpu.SemaphoreType.DMA((2 ** (1 + len(bits)),)),
            pltpu.SemaphoreType.DMA((2,)),
        ],
        input_output_aliases=aliases,
    )


def move(own):
    half = own.shape[0] // 2
    own, head = together(own, own[:half])
    first = lax.ppermute(head, ("side", "core"), [(2, 0), (3, 2)])
    second = lax.ppermute(own[half:], ("side", "core"), [(2, 1)])
    return first, second


def from_side(base, extra):
    group = 2 * lax.axis_index("side") + lax.axis_index("core")
    half = extra.shape[0]
    first = lax.ppermute(extra, ("side", "core"), [(0, 2), (2, 3)])
    second = lax.ppermute(extra, ("side", "core"), [(1, 2)])
    top = jnp.where(group < 2, base[:half], first)
    bottom = jnp.where(group < 2, base[half:], jnp.where(group == 2, second, extra))
    return jnp.concatenate([top, bottom], axis=0)


def outer_halves(value):
    half = value.shape[0] // 2
    return value[:half], value[half:]


def inner_halves(value):
    rows, columns = value.shape
    value = value.reshape(2, 2, rows // 4, columns)
    return value[:, 0].reshape(-1, columns), value[:, 1].reshape(-1, columns)


def join_inner(mine, got):
    rows, columns = mine.shape
    blocks = [v.reshape(2, 1, rows // 2, columns) for v in (mine, got)]
    return jnp.concatenate(blocks, axis=1).reshape(2 * rows, columns)


def across(value, axis, flip):
    pairs = [(i, (i ^ 2) ^ flip) for i in range(4)]
    return lax.ppermute(value, ("side", axis), pairs)


def stage_axes(bits, stage):
    if stage < 2:
        return bits[stage], bits[1 - stage]
    return bits[stage], bits[stage]


def halve(parts, stats, bits):
    parts, stats = list(parts), list(stats)
    for stage in range(len(bits) - 1):
        axes = stage_axes(bits, stage)
        kept, sent = [None, None], [None, None]
        for i in range(2):
            inner = i == 1 and stage == 0
            kept[i], sent[i] = (inner_halves if inner else outer_halves)(parts[i])
            sent[i] = jnp.concatenate([sent[i], stats[i]], axis=0)
        sent = together(*sent)
        got = [swap(sent[i], axes[i]) for i in range(2)]
        got = together(*got)
        for i in range(2):
            rows = kept[i].shape[0]
            parts[i] = kept[i] + got[i][:rows]
            stats[i] = stats[i] + got[i][rows:]
    return parts, stats


def last_messages(part, stats):
    kept, sent = outer_halves(part)
    return jnp.concatenate([kept, stats], axis=0), jnp.concatenate([sent, stats], axis=0)


def reduce_moment(held, statistics, bits):
    half = held.shape[1] // 2
    parts, stats = halve(
        (held[:, :half], held[:, half:]),
        (statistics[:, :half], statistics[:, half:]),
        bits,
    )
    statistics = jnp.concatenate(stats, axis=1)
    kept, sent = together(*last_messages(jnp.concatenate(parts, axis=1), statistics))
    straight, crossed = together(across(kept, bits[-1], 0), across(sent, bits[-1], 1))
    return statistics, straight + crossed


def reduce_mixed(crossing, staying, cross_stats, stay_stats, bits):
    parts, stats = halve((crossing, staying), (cross_stats, stay_stats), bits)
    kept, sent = last_messages(parts[0], stats[0])
    stay_kept, stay_sent = last_messages(parts[1], stats[1])
    kept, sent, stay_sent = together(kept, sent, stay_sent)
    got = (
        across(kept, bits[-1], 0),
        across(sent, bits[-1], 1),
        swap(stay_sent, bits[-1]),
    )
    straight, crossed, got = together(*got)
    second = lax.axis_index("side") == 1
    return straight + crossed + jnp.where(second, stay_kept + got, 0.0)


def gather_moment(own, facing, bits):
    rows = facing.shape[0] - PAD
    chunk, facing = facing[:rows], facing[rows:]
    if own is None:
        chunk, facing = together(chunk, facing)
        got, own = together(swap(chunk, bits[-1]), swap(facing, "side"))
    else:
        got = swap(jnp.concatenate([chunk, own], axis=0), bits[-1])
        got, own = got[:rows], own + got[rows:]
    both = jnp.concatenate([own, facing], axis=0)
    value = jnp.concatenate([chunk, got], axis=0)
    half = value.shape[1] // 2
    parts = [value[:, :half], value[:, half:]]
    for stage in reversed(range(len(bits) - 1)):
        axes = stage_axes(bits, stage)
        if stage == 0:
            *parts, both = together(*parts, both)
            got = [swap(parts[i], axes[i]) for i in range(2)]
            *got, peer = together(*got, swap(both, "core"))
        else:
            parts = together(*parts)
            got = together(*(swap(parts[i], axes[i]) for i in range(2)))
        joined = []
        for i in range(2):
            if i == 1 and stage == 0:
                joined.append(join_inner(parts[i], got[i]))
            else:
                joined.append(jnp.concatenate([parts[i], got[i]], axis=0))
        parts = joined
    both = both + peer
    return jnp.concatenate(parts, axis=1), both[:PAD], both[PAD:]


def weigh(logits, mass, squares):
    scaled = jax.nn.softmax(logits, axis=1) * mass
    columns = jnp.sum(scaled, axis=0, keepdims=True)
    rank = scaled.shape[1]
    return scaled, jnp.concatenate(
        [
            jnp.sum(scaled * squares, axis=0, keepdims=True),
            columns,
            jnp.broadcast_to(jnp.sum(columns, axis=1, keepdims=True), columns.shape),
            jnp.zeros((PAD - 3, rank), jnp.float32),
        ],
        axis=0,
    )


def make_body(axes):
    bits = axes[2:][::-1]

    def body(points, log_factor, masses):
        return steps(points, log_factor, masses)

    def steps(points, log_factor, masses):
        source = lax.axis_index("side") == 0
        group = 2 * lax.axis_index("side") + lax.axis_index("core")
        rows, _ = points.shape
        rank = log_factor.shape[1]
        half = rows // 2
        devices = 1
        for axis in axes:
            devices *= lax.axis_size(axis)

        moved = move(points)
        squares = jnp.sum(points * points, axis=1, keepdims=True)
        mass = masses[:, None]
        near, far = arrange_base(points, bits)
        lanes = lax.broadcasted_iota(jnp.int32, (rows, 128), 1)
        packed = jnp.concatenate(
            [log_factor, jnp.where(lanes < 64, mass, squares)], axis=1
        )

        second_core = lax.axis_index("core") == 1
        scaled, statistics = weigh(log_factor, mass, squares)
        stay_stats = jnp.where(group == 2, statistics, 0.0)
        statistics = jnp.where(group == 2, 0.0, statistics)
        other = swap(contract_rows(far[:rows], scaled), "core")
        held, other = together(contract_rows(near[:rows], scaled), other)
        crossing = jnp.where(
            source, held + other, jnp.where(second_core, held, other)
        )
        staying = jnp.where(second_core, other, held)
        facing = reduce_mixed(crossing, staying, statistics, stay_stats, bits)
        moment, own, facing = gather_moment(None, facing, bits)

        first, second = move(packed)
        extra = jnp.where(group == 1, second, jnp.where(group == 3, packed[half:], first))
        near, far = arrange_extra(points, *moved, near, far, bits)
        logits = jnp.concatenate([log_factor, extra[:, :rank]], axis=0)
        mass = jnp.concatenate(
            [jnp.where(source, mass, 0.0), extra[:, rank : rank + 1]], axis=0
        )
        squares = jnp.concatenate([squares, extra[:, rank + 64 : rank + 65]], axis=0)
        real = source | (lax.broadcasted_iota(jnp.int32, (logits.shape[0], 1), 0) >= rows)

        for iteration in range(ITERS):
            if iteration:
                scaled, statistics = weigh(logits, mass, squares)
                other = swap(contract_rows(far, scaled), "core")
                held, other = together(contract_rows(near, scaled), other)
                own, facing = reduce_moment(held + other, statistics, bits)
                moment, own, facing = gather_moment(own, facing, bits)
            cross, other = together(times(near, moment), swap(moment, "core"))
            cross = cross + times(far, other)
            share = facing[1:2] / facing[2:3]
            marginal = 0.5 * (own[1:2] / own[2:3] + share)
            gradient = (
                squares * share - 2.0 * (cross / facing[2:3]) + facing[0:1] / facing[2:3]
            ) / marginal
            centred = gradient - jnp.mean(gradient, axis=1, keepdims=True)
            largest = jnp.max(jnp.where(real, jnp.abs(centred), 0.0))
            spread = jnp.full((devices, 128), largest, jnp.float32)
            largest = jnp.max(lax.all_to_all(spread, axes, 0, 0, tiled=True))
            logits = logits - step_scale / (largest + 1e-06) * gradient
        factors = rank * jax.nn.softmax(logits, axis=1)
        return from_side(factors[:rows], factors[rows:])

    return body


def solution(mesh):
    pts = mesh.shape["pts"]
    count = pts.bit_length() - 1
    axes = ("side", "core") + tuple(f"bit{i}" for i in reversed(range(count)))
    split = Mesh(mesh.devices.reshape((2,) * len(axes)), axes)
    in_specs = (P(axes, None), P(axes, None), P(axes))
    return jax.shard_map(
        make_body(axes), mesh=split, in_specs=in_specs, out_specs=P(axes, None), check_vma=False
    )
```

profile of v0, /device:TPU:1, one launch (start us, length us, event | category | flops | bytes accessed | tf_op | source)
XLA Modules:
  0.0 207.4 jit_solution(4055356138326592041)
XLA Ops:
  1.8 3.1 %shard_map.37 = (f32[384,1024]{1,0:T(8,128)}, f32[384,1024]{1,0:T(8,128)}) custom-call(f32[256,2048]{1,0:T(8,128)} %points.3), custom_call_target="tpu_custom_call" | custom-call | tf_op jit(solution)/shard_map/pallas_call | solution.py:122
  6.1 4.0 %convolution_bitcast_fusion = f32[1024,256]{1,0:T(8,128)} fusion(f32[256,256]{1,0:T(8,128)S(1)} %get-tuple-element.156, f32[384,1024]{1,0:T(8,128)} %get-tuple-element.74.far_in), kind=kOutput, calls=%fused_computation.1 | convolution fusion | flops 805306368 | bytes 2359296 | tf_op jit(solution)/shard_map/dot_general | solution.py:27
  11.0 1.8 convolution_bitcast_fusion.1
  13.4 2.6 %collective-permute-start.3 = (f32[520,256]{1,0:T(8,128)S(1)}, f32[520,256]{1,0:T(8,128)S(1)}, u32[]{:S(2)}, u32[]{:S(2)}) collective-permute-start(f32[520,256]{1,0:T(8,128)S(1)} %get-tuple-element.77), channel_id=1, source_target_pairs={{0,1},{1,0},{2,3},{3,2},{4,5},{5,4},{6,7},{7,6},{8,9},{9,8},{10,11... | collective-permute-start | bytes 1597448 | tf_op jit(solution)/shard_map/ppermute | solution.py:19
  17.3 11.0 %collective-permute-done.3 = f32[520,256]{1,0:T(8,128)S(1)} collective-permute-done((f32[520,256]{1,0:T(8,128)S(1)}, f32[520,256]{1,0:T(8,128)S(1)}, u32[]{:S(2)}, u32[]{:S(2)}) %collective-permute-start.3) | collective-permute-done | bytes 532512 | tf_op jit(solution)/shard_map/ppermute | solution.py:19
  31.3 5.2 %collective-permute-done.5 = f32[264,256]{1,0:T(8,128)S(1)} collective-permute-done((f32[264,256]{1,0:T(8,128)S(1)}, f32[264,256]{1,0:T(8,128)S(1)}, u32[]{:S(2)}, u32[]{:S(2)}) %collective-permute-start.5) | collective-permute-done | bytes 270368 | tf_op jit(solution)/shard_map/ppermute | solution.py:19
  38.9 2.3 %collective-permute-start.8 = (f32[136,256]{1,0:T(8,128)S(1)}, f32[136,256]{1,0:T(8,128)S(1)}, u32[]{:S(2)}, u32[]{:S(2)}) collective-permute-start(f32[136,256]{1,0:T(8,128)S(1)} %get-tuple-element.86), channel_id=1, source_target_pairs={{0,20},{4,16},{16,4},{20,0},{1,21},{5,17},{17,5},{21,1},{2,22},{6,... | collective-permute-start | bytes 417800 | tf_op jit(solution)/shard_map/ppermute | solution.py:196
  41.6 9.8 %collective-permute-done.8 = f32[136,256]{1,0:T(8,128)S(1)} collective-permute-done((f32[136,256]{1,0:T(8,128)S(1)}, f32[136,256]{1,0:T(8,128)S(1)}, u32[]{:S(2)}, u32[]{:S(2)}) %collective-permute-start.8) | collective-permute-done | bytes 139296 | tf_op jit(solution)/shard_map/ppermute | solution.py:196
  51.5 2.1 collective-permute-done.9
  58.7 3.3 %collective-permute-start.11 = (f32[8,256]{1,0:T(8,128)S(1)}, f32[8,256]{1,0:T(8,128)S(1)}, u32[]{:S(2)}, u32[]{:S(2)}) collective-permute-start(f32[8,256]{1,0:T(8,128)S(1)} %slice.339), channel_id=1, source_target_pairs={{0,16},{16,0},{1,17},{17,1},{2,18},{18,2},{3,19},{19,3},{4,20},{20... | collective-permute-start | bytes 24584 | tf_op jit(solution)/shard_map/ppermute | solution.py:19
  63.6 2.9 %collective-permute-start.12 = (f32[256,128]{1,0:T(8,128)S(1)}, f32[256,128]{1,0:T(8,128)S(1)}, u32[]{:S(2)}, u32[]{:S(2)}) collective-permute-start(f32[256,128]{1,0:T(8,128)S(1)} %get-tuple-element.94), channel_id=1, source_target_pairs={{0,2},{2,0},{1,3},{3,1},{4,6},{6,4},{5,7},{7,5},{8,10},{10,8},{9,1... | collective-permute-start | bytes 393224 | tf_op jit(solution)/shard_map/ppermute | solution.py:19
  66.9 2.4 %collective-permute-done.12 = f32[256,128]{1,0:T(8,128)S(1)} collective-permute-done((f32[256,128]{1,0:T(8,128)S(1)}, f32[256,128]{1,0:T(8,128)S(1)}, u32[]{:S(2)}, u32[]{:S(2)}) %collective-permute-start.12) | collective-permute-done | bytes 131104 | tf_op jit(solution)/shard_map/ppermute | solution.py:19
  71.4 22.2 %collective-permute-start.16 = (f32[16,256]{1,0:T(8,128)S(1)}, f32[16,256]{1,0:T(8,128)S(1)}, u32[]{:S(2)}, u32[]{:S(2)}) collective-permute-start(f32[16,256]{1,0:T(8,128)S(1)} %pad_maximum_fusion.25), channel_id=1, source_target_pairs={{0,8},{8,0},{1,9},{9,1},{2,10},{10,2},{3,11},{11,3},{4,12},{12,4},... | collective-permute-start | bytes 49160 | tf_op jit(solution)/shard_map/ppermute | solution.py:19
  97.6 3.9 %collective-permute-start.19 = (f32[1024,256]{1,0:T(8,128)}, f32[1024,256]{1,0:T(8,128)}, u32[]{:S(2)}, u32[]{:S(2)}) collective-permute-start(f32[1024,256]{1,0:T(8,128)} %pad_maximum_fusion), channel_id=1, source_target_pairs={{0,8},{8,0},{1,9},{9,1},{2,10},{10,2},{3,11},{11,3},{4,12},{12,4},... | collective-permute-start | bytes 3145736 | tf_op jit(solution)/shard_map/ppermute | solution.py:19
  102.8 2.4 %shard_map.38 = (f32[384,1024]{1,0:T(8,128)}, f32[384,1024]{1,0:T(8,128)}) custom-call(f32[256,2048]{1,0:T(8,128)} %points.3, f32[128,2048]{1,0:T(8,128)} %collective-permute-done.17.first, f32[128,2048]{1,0:T(8,128)} %copy-done.5, f32[384,1024]{1,0:T(8,128)} %get-tuple-element.73.near_in, ...), custom_call_target="tpu_custom_call", output_to_operand_aliasing={{0}: (3, {}), {1}: (4, {})} | custom-call | tf_op jit(solution)/shard_map/pallas_call | solution.py:134
  105.2 2.9 %fusion.25 = f32[384,256]{1,0:T(8,128)S(1)} fusion(f32[384,1024]{1,0:T(8,128)} %get-tuple-element.105, f32[1024,128]{1,0:T(8,128)S(1)} %bitcast.49, f32[512,128]{1,0:T(8,128)S(1)} %collective-permute-done.14, f32[512,128]{1,0:T(8,128)S(1)} %pad_maximum_fusion.11), kind=kOutput, calls=%fused_computation.116 | convolution fusion | flops 1208483840 | bytes 3014656 | tf_op jit(solution)/shard_map/dot_general | solution.py:37
  108.2 2.6 %fusion.41 = f32[384,256]{1,0:T(8,128)S(1)} fusion(f32[384,1024]{1,0:T(8,128)S(1)} %copy-done.2, f32[1024,256]{1,0:T(8,128)} %collective-permute-done.19), kind=kOutput, calls=%fused_computation.132 | convolution fusion | flops 1207959552 | bytes 3014656 | tf_op jit(solution)/shard_map/dot_general | solution.py:37
  113.2 7.2 %all-to-all-start = ((f32[32,1,128]{2,1,0:T(1,128)}), f32[32,1,128]{2,1,0:T(1,128)S(1)}, u32[]{:S(2)}, u32[]{:S(2)}) async-start(f32[32,1,128]{2,1,0:T(1,128)} %broadcast_in_dim.98), calls=%async_computation | async-start | bytes 32768 | tf_op jit(solution)/shard_map/all_to_all | solution.py:370
  120.5 6.7 %all-to-all-done = f32[32,1,128]{2,1,0:T(1,128)S(1)} async-done(((f32[32,1,128]{2,1,0:T(1,128)}), f32[32,1,128]{2,1,0:T(1,128)S(1)}, u32[]{:S(2)}, u32[]{:S(2)}) %all-to-all-start) | async-done | bytes 16416 | tf_op jit(solution)/shard_map/all_to_all | solution.py:370
  129.8 2.6 %fusion.43 = f32[1024,256]{1,0:T(8,128)S(1)} fusion(f32[384,1024]{1,0:T(8,128)S(1)} %copy-done.2, f32[384,256]{1,0:T(8,128)S(1)} %get-tuple-element.149), kind=kOutput, calls=%fused_computation.134 | convolution fusion | flops 1207959552 | bytes 3014656 | tf_op jit(solution)/shard_map/dot_general | solution.py:27
  134.0 2.6 %fusion.42 = f32[1024,256]{1,0:T(8,128)S(1)} fusion(f32[384,1024]{1,0:T(8,128)S(1)} %copy-done.1, f32[384,256]{1,0:T(8,128)S(1)} %get-tuple-element.149), kind=kOutput, calls=%fused_computation.133 | convolution fusion | flops 1207959552 | bytes 3014656 | tf_op jit(solution)/shard_map/dot_general | solution.py:27
  137.6 7.3 %collective-permute-done.21 = f32[520,128]{1,0:T(8,128)S(1)} collective-permute-done((f32[520,128]{1,0:T(8,128)S(1)}, f32[520,128]{1,0:T(8,128)S(1)}, u32[]{:S(2)}, u32[]{:S(2)}) %collective-permute-start.21) | collective-permute-done | bytes 266272 | tf_op jit(solution)/shard_map/ppermute | solution.py:19
  146.6 2.5 %collective-permute-done.23 = f32[264,128]{1,0:T(8,128)S(1)} collective-permute-done((f32[264,128]{1,0:T(8,128)S(1)}, f32[264,128]{1,0:T(8,128)S(1)}, u32[]{:S(2)}, u32[]{:S(2)}) %collective-permute-start.23) | collective-permute-done | bytes 135200 | tf_op jit(solution)/shard_map/ppermute | solution.py:19
  151.3 2.4 %collective-permute-done.25 = f32[136,256]{1,0:T(8,128)S(1)} collective-permute-done((f32[136,256]{1,0:T(8,128)S(1)}, f32[136,256]{1,0:T(8,128)S(1)}, u32[]{:S(2)}, u32[]{:S(2)}) %collective-permute-start.25) | collective-permute-done | bytes 139296 | tf_op jit(solution)/shard_map/ppermute | solution.py:196
  153.7 3.6 %collective-permute-done.26 = f32[136,256]{1,0:T(8,128)S(1)} collective-permute-done((f32[136,256]{1,0:T(8,128)S(1)}, f32[136,256]{1,0:T(8,128)S(1)}, u32[]{:S(2)}, u32[]{:S(2)}) %collective-permute-start.26) | collective-permute-done | bytes 139296 | tf_op jit(solution)/shard_map/ppermute | solution.py:196
  157.5 5.9 %collective-permute-done.27 = f32[136,256]{1,0:T(8,128)S(1)} collective-permute-done((f32[136,256]{1,0:T(8,128)S(1)}, f32[136,256]{1,0:T(8,128)S(1)}, u32[]{:S(2)}, u32[]{:S(2)}) %collective-permute-start.27) | collective-permute-done | bytes 139296 | tf_op jit(solution)/shard_map/ppermute | solution.py:19
  164.7 4.0 %collective-permute-done.28 = f32[256,128]{1,0:T(8,128)S(1)} collective-permute-done((f32[256,128]{1,0:T(8,128)S(1)}, f32[256,128]{1,0:T(8,128)S(1)}, u32[]{:S(2)}, u32[]{:S(2)}) %collective-permute-start.28) | collective-permute-done | bytes 131104 | tf_op jit(solution)/shard_map/ppermute | solution.py:19
  170.0 8.0 %collective-permute-start.32 = (f32[16,256]{1,0:T(8,128)S(1)}, f32[16,256]{1,0:T(8,128)S(1)}, u32[]{:S(2)}, u32[]{:S(2)}) collective-permute-start(f32[16,256]{1,0:T(8,128)S(1)} %pad_maximum_fusion.26), channel_id=1, source_target_pairs={{0,8},{8,0},{1,9},{9,1},{2,10},{10,2},{3,11},{11,3},{4,12},{12,4},... | collective-permute-start | bytes 49160 | tf_op jit(solution)/shard_map/ppermute | solution.py:19
  179.0 3.9 %collective-permute-start.33 = (f32[1024,256]{1,0:T(8,128)S(1)}, f32[1024,256]{1,0:T(8,128)S(1)}, u32[]{:S(2)}, u32[]{:S(2)}) collective-permute-start(f32[1024,256]{1,0:T(8,128)S(1)} %pad_maximum_fusion.1), channel_id=1, source_target_pairs={{0,8},{8,0},{1,9},{9,1},{2,10},{10,2},{3,11},{11,3},{4,12},{12,4},... | collective-permute-start | bytes 3145736 | tf_op jit(solution)/shard_map/ppermute | solution.py:19
  188.3 9.7 %all_to_all.12 = f32[32,1,128]{2,1,0:T(1,128)S(1)} all-to-all(f32[32,1,128]{2,1,0:T(1,128)S(1)} %broadcast_in_dim.103), channel_id=1, replica_groups=mesh['side'=2,'core'=2,'bit2'=2,'bit1'=2,'bit0'=2] {'side','core','bit2'..., dimensions={0} | all-to-all | bytes 32768 | tf_op jit(solution)/shard_map/all_to_all | solution.py:370
  200.6 4.0 %collective-permute-start.35 = (f32[128,256]{1,0:T(8,128)S(1)}, f32[128,256]{1,0:T(8,128)S(1)}, u32[]{:S(2)}, u32[]{:S(2)}) collective-permute-start(f32[128,256]{1,0:T(8,128)S(1)} %slice.373), channel_id=1, source_target_pairs={{8,16},{9,17},{10,18},{11,19},{12,20},{13,21},{14,22},{15,23}} | collective-permute-start | bytes 393224 | tf_op jit(solution)/shard_map/ppermute | solution.py:171
  204.7 1.9 collective-permute-done.35
  (180 shorter events, 48.1 us)
Async XLA Ops:
  13.4 15.0 %collective-permute-start.3 = (f32[520,256]{1,0:T(8,128)S(1)}, f32[520,256]{1,0:T(8,128)S(1)}, u32[]{:S(2)}, u32[]{:S(2)}) collective-permute-start(f32[520,256]{1,0:T(8,128)S(1)} %get-tuple-element.77), channel_id=1, source_target_pairs={{0,1},{1,0},{2,3},{3,2},{4,5},{5,4},{6,7},{7,6},{8,9},{9,8},{10,11... | collective-permute-start | bytes 1597448 | tf_op jit(solution)/shard_map/ppermute | solution.py:19
  16.0 13.2 %collective-permute-start.4 = (f32[520,256]{1,0:T(8,128)S(1)}, f32[520,256]{1,0:T(8,128)S(1)}, u32[]{:S(2)}, u32[]{:S(2)}) collective-permute-start(f32[520,256]{1,0:T(8,128)S(1)} %get-tuple-element.78), channel_id=1, source_target_pairs={{0,2},{2,0},{1,3},{3,1},{4,6},{6,4},{5,7},{7,5},{8,10},{10,8},{9,1... | collective-permute-start | bytes 1597448 | tf_op jit(solution)/shard_map/ppermute | solution.py:19
  29.6 6.8 %collective-permute-start.5 = (f32[264,256]{1,0:T(8,128)S(1)}, f32[264,256]{1,0:T(8,128)S(1)}, u32[]{:S(2)}, u32[]{:S(2)}) collective-permute-start(f32[264,256]{1,0:T(8,128)S(1)} %pad_maximum_fusion.7), channel_id=1, source_target_pairs={{0,2},{2,0},{1,3},{3,1},{4,6},{6,4},{5,7},{7,5},{8,10},{10,8},{9,1... | collective-permute-start | bytes 811016 | tf_op jit(solution)/shard_map/ppermute | solution.py:19
  31.0 6.5 %collective-permute-start.6 = (f32[264,256]{1,0:T(8,128)S(1)}, f32[264,256]{1,0:T(8,128)S(1)}, u32[]{:S(2)}, u32[]{:S(2)}) collective-permute-start(f32[264,256]{1,0:T(8,128)S(1)} %pad_maximum_fusion.8), channel_id=1, source_target_pairs={{0,1},{1,0},{2,3},{3,2},{4,5},{5,4},{6,7},{7,6},{8,9},{9,8},{10,11... | collective-permute-start | bytes 811016 | tf_op jit(solution)/shard_map/ppermute | solution.py:19
  38.9 12.5 %collective-permute-start.8 = (f32[136,256]{1,0:T(8,128)S(1)}, f32[136,256]{1,0:T(8,128)S(1)}, u32[]{:S(2)}, u32[]{:S(2)}) collective-permute-start(f32[136,256]{1,0:T(8,128)S(1)} %get-tuple-element.86), channel_id=1, source_target_pairs={{0,20},{4,16},{16,4},{20,0},{1,21},{5,17},{17,5},{21,1},{2,22},{6,... | collective-permute-start | bytes 417800 | tf_op jit(solution)/shard_map/ppermute | solution.py:196
  41.2 12.3 %collective-permute-start.9 = (f32[136,256]{1,0:T(8,128)S(1)}, f32[136,256]{1,0:T(8,128)S(1)}, u32[]{:S(2)}, u32[]{:S(2)}) collective-permute-start(f32[136,256]{1,0:T(8,128)S(1)} %pad_maximum_fusion.19), channel_id=1, source_target_pairs={{0,4},{4,0},{1,5},{5,1},{2,6},{6,2},{3,7},{7,3},{8,12},{12,8},{9,1... | collective-permute-start | bytes 417800 | tf_op jit(solution)/shard_map/ppermute | solution.py:19
  53.6 9.9 %collective-permute-start.10 = (f32[128,256]{1,0:T(8,128)S(1)}, f32[128,256]{1,0:T(8,128)S(1)}, u32[]{:S(2)}, u32[]{:S(2)}) collective-permute-start(f32[128,256]{1,0:T(8,128)S(1)} %slice.338), channel_id=1, source_target_pairs={{0,4},{4,0},{1,5},{5,1},{2,6},{6,2},{3,7},{7,3},{8,12},{12,8},{9,1... | collective-permute-start | bytes 393224 | tf_op jit(solution)/shard_map/ppermute | solution.py:19
  54.8 47.0 %collective-permute-start.17 = (f32[128,2048]{1,0:T(8,128)}, f32[128,2048]{1,0:T(8,128)}, u32[]{:S(2)}, u32[]{:S(2)}) collective-permute-start(f32[128,2048]{1,0:T(8,128)} %slice.279), channel_id=1, source_target_pairs={{16,0},{24,16},{17,1},{25,17},{18,2},{26,18},{19,3},{27,19},{20,4}... | collective-permute-start | bytes 3145736 | tf_op jit(solution)/shard_map/ppermute | solution.py:162
  57.5 44.3 %collective-permute-start.18 = (f32[128,2048]{1,0:T(8,128)}, f32[128,2048]{1,0:T(8,128)S(1)}, u32[]{:S(2)}, u32[]{:S(2)}) collective-permute-start(f32[128,2048]{1,0:T(8,128)} %slice.280), channel_id=1, source_target_pairs={{16,8},{17,9},{18,10},{19,11},{20,12},{21,13},{22,14},{23,15}} | collective-permute-start | bytes 3145736 | tf_op jit(solution)/shard_map/ppermute | solution.py:163
  58.7 4.8 %collective-permute-start.11 = (f32[8,256]{1,0:T(8,128)S(1)}, f32[8,256]{1,0:T(8,128)S(1)}, u32[]{:S(2)}, u32[]{:S(2)}) collective-permute-start(f32[8,256]{1,0:T(8,128)S(1)} %slice.339), channel_id=1, source_target_pairs={{0,16},{16,0},{1,17},{17,1},{2,18},{18,2},{3,19},{19,3},{4,20},{20... | collective-permute-start | bytes 24584 | tf_op jit(solution)/shard_map/ppermute | solution.py:19
  63.6 5.7 %collective-permute-start.12 = (f32[256,128]{1,0:T(8,128)S(1)}, f32[256,128]{1,0:T(8,128)S(1)}, u32[]{:S(2)}, u32[]{:S(2)}) collective-permute-start(f32[256,128]{1,0:T(8,128)S(1)} %get-tuple-element.94), channel_id=1, source_target_pairs={{0,2},{2,0},{1,3},{3,1},{4,6},{6,4},{5,7},{7,5},{8,10},{10,8},{9,1... | collective-permute-start | bytes 393224 | tf_op jit(solution)/shard_map/ppermute | solution.py:19
  66.5 4.2 %collective-permute-start.13 = (f32[256,128]{1,0:T(8,128)S(1)}, f32[256,128]{1,0:T(8,128)S(1)}, u32[]{:S(2)}, u32[]{:S(2)}) collective-permute-start(f32[256,128]{1,0:T(8,128)S(1)} %get-tuple-element.95), channel_id=1, source_target_pairs={{0,1},{1,0},{2,3},{3,2},{4,5},{5,4},{6,7},{7,6},{8,9},{9,8},{10,11... | collective-permute-start | bytes 393224 | tf_op jit(solution)/shard_map/ppermute | solution.py:19
  70.8 25.0 %collective-permute-start.14 = (f32[512,128]{1,0:T(8,128)S(1)}, f32[512,128]{1,0:T(8,128)S(1)}, u32[]{:S(2)}, u32[]{:S(2)}) collective-permute-start(f32[512,128]{1,0:T(8,128)S(1)} %pad_maximum_fusion.11), channel_id=1, source_target_pairs={{0,1},{1,0},{2,3},{3,2},{4,5},{5,4},{6,7},{7,6},{8,9},{9,8},{10,11... | collective-permute-start | bytes 786440 | tf_op jit(solution)/shard_map/ppermute | solution.py:19
  71.2 25.3 %collective-permute-start.15 = (f32[512,128]{1,0:T(8,128)S(1)}, f32[512,128]{1,0:T(8,128)S(1)}, u32[]{:S(2)}, u32[]{:S(2)}) collective-permute-start(f32[512,128]{1,0:T(8,128)S(1)} %pad_maximum_fusion.12), channel_id=1, source_target_pairs={{0,2},{2,0},{1,3},{3,1},{4,6},{6,4},{5,7},{7,5},{8,10},{10,8},{9,1... | collective-permute-start | bytes 786440 | tf_op jit(solution)/shard_map/ppermute | solution.py:19
  71.4 23.0 %collective-permute-start.16 = (f32[16,256]{1,0:T(8,128)S(1)}, f32[16,256]{1,0:T(8,128)S(1)}, u32[]{:S(2)}, u32[]{:S(2)}) collective-permute-start(f32[16,256]{1,0:T(8,128)S(1)} %pad_maximum_fusion.25), channel_id=1, source_target_pairs={{0,8},{8,0},{1,9},{9,1},{2,10},{10,2},{3,11},{11,3},{4,12},{12,4},... | collective-permute-start | bytes 49160 | tf_op jit(solution)/shard_map/ppermute | solution.py:19
  94.5 7.1 %collective-permute-start = (f32[128,384]{1,0:T(8,128)S(1)}, f32[128,384]{1,0:T(8,128)S(1)}, u32[]{:S(2)}, u32[]{:S(2)}) collective-permute-start(f32[128,384]{1,0:T(8,128)S(1)} %slice.247), channel_id=1, source_target_pairs={{16,8},{17,9},{18,10},{19,11},{20,12},{21,13},{22,14},{23,15}} | collective-permute-start | bytes 589832 | tf_op jit(solution)/shard_map/ppermute | solution.py:163
  95.8 5.8 %collective-permute-start.1 = (f32[128,384]{1,0:T(8,128)S(1)}, f32[128,384]{1,0:T(8,128)S(1)}, u32[]{:S(2)}, u32[]{:S(2)}) collective-permute-start(f32[128,384]{1,0:T(8,128)S(1)} %fusion.5), channel_id=1, source_target_pairs={{16,0},{24,16},{17,1},{25,17},{18,2},{26,18},{19,3},{27,19},{20,4}... | collective-permute-start | bytes 589832 | tf_op jit(solution)/shard_map/ppermute | solution.py:162
  97.6 10.5 %collective-permute-start.19 = (f32[1024,256]{1,0:T(8,128)}, f32[1024,256]{1,0:T(8,128)}, u32[]{:S(2)}, u32[]{:S(2)}) collective-permute-start(f32[1024,256]{1,0:T(8,128)} %pad_maximum_fusion), channel_id=1, source_target_pairs={{0,8},{8,0},{1,9},{9,1},{2,10},{10,2},{3,11},{11,3},{4,12},{12,4},... | collective-permute-start | bytes 3145736 | tf_op jit(solution)/shard_map/ppermute | solution.py:19
  113.2 14.0 %all-to-all-start = ((f32[32,1,128]{2,1,0:T(1,128)}), f32[32,1,128]{2,1,0:T(1,128)S(1)}, u32[]{:S(2)}, u32[]{:S(2)}) async-start(f32[32,1,128]{2,1,0:T(1,128)} %broadcast_in_dim.98), calls=%async_computation | async-start | bytes 32768 | tf_op jit(solution)/shard_map/all_to_all | solution.py:370
  132.4 4.2 %collective-permute-start.20 = (f32[1024,256]{1,0:T(8,128)S(1)}, f32[1024,256]{1,0:T(8,128)S(1)}, u32[]{:S(2)}, u32[]{:S(2)}) collective-permute-start(f32[1024,256]{1,0:T(8,128)S(1)} %fusion.43), channel_id=1, source_target_pairs={{0,8},{8,0},{1,9},{9,1},{2,10},{10,2},{3,11},{11,3},{4,12},{12,4},... | collective-permute-start | bytes 3145736 | tf_op jit(solution)/shard_map/ppermute | solution.py:19
  136.9 8.0 %collective-permute-start.21 = (f32[520,128]{1,0:T(8,128)S(1)}, f32[520,128]{1,0:T(8,128)S(1)}, u32[]{:S(2)}, u32[]{:S(2)}) collective-permute-start(f32[520,128]{1,0:T(8,128)S(1)} %pad_maximum_fusion.9), channel_id=1, source_target_pairs={{0,1},{1,0},{2,3},{3,2},{4,5},{5,4},{6,7},{7,6},{8,9},{9,8},{10,11... | collective-permute-start | bytes 798728 | tf_op jit(solution)/shard_map/ppermute | solution.py:19
  137.4 7.7 %collective-permute-start.22 = (f32[520,128]{1,0:T(8,128)S(1)}, f32[520,128]{1,0:T(8,128)S(1)}, u32[]{:S(2)}, u32[]{:S(2)}) collective-permute-start(f32[520,128]{1,0:T(8,128)S(1)} %pad_maximum_fusion.10), channel_id=1, source_target_pairs={{0,2},{2,0},{1,3},{3,1},{4,6},{6,4},{5,7},{7,5},{8,10},{10,8},{9,1... | collective-permute-start | bytes 798728 | tf_op jit(solution)/shard_map/ppermute | solution.py:19
  150.1 7.2 %collective-permute-start.26 = (f32[136,256]{1,0:T(8,128)S(1)}, f32[136,256]{1,0:T(8,128)S(1)}, u32[]{:S(2)}, u32[]{:S(2)}) collective-permute-start(f32[136,256]{1,0:T(8,128)S(1)} %get-tuple-element.122), channel_id=1, source_target_pairs={{0,20},{4,16},{16,4},{20,0},{1,21},{5,17},{17,5},{21,1},{2,22},{6,... | collective-permute-start | bytes 417800 | tf_op jit(solution)/shard_map/ppermute | solution.py:196
  157.4 6.0 %collective-permute-start.27 = (f32[136,256]{1,0:T(8,128)S(1)}, f32[136,256]{1,0:T(8,128)S(1)}, u32[]{:S(2)}, u32[]{:S(2)}) collective-permute-start(f32[136,256]{1,0:T(8,128)S(1)} %fusion.13), channel_id=1, source_target_pairs={{0,4},{4,0},{1,5},{5,1},{2,6},{6,2},{3,7},{7,3},{8,12},{12,8},{9,1... | collective-permute-start | bytes 417800 | tf_op jit(solution)/shard_map/ppermute | solution.py:19
  163.4 5.3 %collective-permute-start.28 = (f32[256,128]{1,0:T(8,128)S(1)}, f32[256,128]{1,0:T(8,128)S(1)}, u32[]{:S(2)}, u32[]{:S(2)}) collective-permute-start(f32[256,128]{1,0:T(8,128)S(1)} %get-tuple-element.125), channel_id=1, source_target_pairs={{0,2},{2,0},{1,3},{3,1},{4,6},{6,4},{5,7},{7,5},{8,10},{10,8},{9,1... | collective-permute-start | bytes 393224 | tf_op jit(solution)/shard_map/ppermute | solution.py:19
  163.5 5.2 %collective-permute-start.29 = (f32[256,128]{1,0:T(8,128)S(1)}, f32[256,128]{1,0:T(8,128)S(1)}, u32[]{:S(2)}, u32[]{:S(2)}) collective-permute-start(f32[256,128]{1,0:T(8,128)S(1)} %get-tuple-element.126), channel_id=1, source_target_pairs={{0,1},{1,0},{2,3},{3,2},{4,5},{5,4},{6,7},{7,6},{8,9},{9,8},{10,11... | collective-permute-start | bytes 393224 | tf_op jit(solution)/shard_map/ppermute | solution.py:19
  168.8 10.1 %collective-permute-start.30 = (f32[512,128]{1,0:T(8,128)S(1)}, f32[512,128]{1,0:T(8,128)S(1)}, u32[]{:S(2)}, u32[]{:S(2)}) collective-permute-start(f32[512,128]{1,0:T(8,128)S(1)} %pad_maximum_fusion.13), channel_id=1, source_target_pairs={{0,1},{1,0},{2,3},{3,2},{4,5},{5,4},{6,7},{7,6},{8,9},{9,8},{10,11... | collective-permute-start | bytes 786440 | tf_op jit(solution)/shard_map/ppermute | solution.py:19
  170.0 8.9 %collective-permute-start.31 = (f32[512,128]{1,0:T(8,128)S(1)}, f32[512,128]{1,0:T(8,128)S(1)}, u32[]{:S(2)}, u32[]{:S(2)}) collective-permute-start(f32[512,128]{1,0:T(8,128)S(1)} %pad_maximum_fusion.14), channel_id=1, source_target_pairs={{0,2},{2,0},{1,3},{3,1},{4,6},{6,4},{5,7},{7,5},{8,10},{10,8},{9,1... | collective-permute-start | bytes 786440 | tf_op jit(solution)/shard_map/ppermute | solution.py:19
  170.0 8.8 %collective-permute-start.32 = (f32[16,256]{1,0:T(8,128)S(1)}, f32[16,256]{1,0:T(8,128)S(1)}, u32[]{:S(2)}, u32[]{:S(2)}) collective-permute-start(f32[16,256]{1,0:T(8,128)S(1)} %pad_maximum_fusion.26), channel_id=1, source_target_pairs={{0,8},{8,0},{1,9},{9,1},{2,10},{10,2},{3,11},{11,3},{4,12},{12,4},... | collective-permute-start | bytes 49160 | tf_op jit(solution)/shard_map/ppermute | solution.py:19
  179.0 6.2 %collective-permute-start.33 = (f32[1024,256]{1,0:T(8,128)S(1)}, f32[1024,256]{1,0:T(8,128)S(1)}, u32[]{:S(2)}, u32[]{:S(2)}) collective-permute-start(f32[1024,256]{1,0:T(8,128)S(1)} %pad_maximum_fusion.1), channel_id=1, source_target_pairs={{0,8},{8,0},{1,9},{9,1},{2,10},{10,2},{3,11},{11,3},{4,12},{12,4},... | collective-permute-start | bytes 3145736 | tf_op jit(solution)/shard_map/ppermute | solution.py:19
  199.9 4.7 %collective-permute-start.34 = (f32[128,256]{1,0:T(8,128)S(1)}, f32[128,256]{1,0:T(8,128)S(1)}, u32[]{:S(2)}, u32[]{:S(2)}) collective-permute-start(f32[128,256]{1,0:T(8,128)S(1)} %slice.373), channel_id=1, source_target_pairs={{0,16},{16,24},{1,17},{17,25},{2,18},{18,26},{3,19},{19,27},{4,20}... | collective-permute-start | bytes 393224 | tf_op jit(solution)/shard_map/ppermute | solution.py:170
  200.6 6.0 %collective-permute-start.35 = (f32[128,256]{1,0:T(8,128)S(1)}, f32[128,256]{1,0:T(8,128)S(1)}, u32[]{:S(2)}, u32[]{:S(2)}) collective-permute-start(f32[128,256]{1,0:T(8,128)S(1)} %slice.373), channel_id=1, source_target_pairs={{8,16},{9,17},{10,18},{11,19},{12,20},{13,21},{14,22},{15,23}} | collective-permute-start | bytes 393224 | tf_op jit(solution)/shard_map/ppermute | solution.py:171
  (12 other events, 55.8 us)
where the time goes:
time: 208 us; the launch traced here: 207 us
  starting transfers between devices  78.1 us (38%)
  waiting for transfers between devices  73.3 us (35%)
  matrix products  19.5 us (9%)
  other arithmetic  11.7 us (6%)
  blocking collectives  9.72 us (5%)
  local copies, waits for them, and re-layouts  7.3 us (4%)
  Pallas kernels  5.51 us (3%)
  between operations  2.2 us (1%)
    ppermute x26, starting transfers between devices, swap(): return lax.ppermute(value, axis, [(0, 1), (1, 0)])  56.2 us
    ppermute x26, waiting for transfers between devices, swap(): return lax.ppermute(value, axis, [(0, 1), (1, 0)])  48.5 us
    ppermute x4, waiting for transfers between devices, across(): return lax.ppermute(value, ('side', axis), pairs)  16.2 us
    dot_general x4, matrix products, contract_rows(): lax.dot_general(left, right, (((0,), (0,)), ((), ())), precision=highest,...  11.1 us
    all_to_all x1, blocking collectives, steps(): largest = jnp.max(lax.all_to_all(spread, axes, 0, 0, tiled=True))  9.72 us
    dot_general x4, matrix products, times(): jnp.dot(left, right, precision=highest, preferred_element_type=jnp.float32)  8.37 us
    all_to_all x1, starting transfers between devices, steps(): largest = jnp.max(lax.all_to_all(spread, axes, 0, 0, tiled=True))  7.21 us
    all_to_all x1, waiting for transfers between devices, steps(): largest = jnp.max(lax.all_to_all(spread, axes, 0, 0, tiled=True))  6.66 us
  transfers between devices with their start and end apart: 37, of which 24 were waited for; matrix products, arithmetic and copies ran while one was open for 7% of the time, Pallas kernels for 1%

commit v1 on v0

--- a/solution.py
+++ b/solution.py
@@ -61,26 +61,32 @@
     return copies
 
 
-def put_rows(parts, targets, top, sems):
+def row_copies(parts, targets, top, sems):
     rows = parts[0].shape[0]
-    copies = [
+    return [
         pltpu.make_async_copy(parts[i], targets[i].at[pl.ds(top, rows), :], sems.at[i])
         for i in range(2)
     ]
-    for copy in copies:
-        copy.start()
-    for copy in copies:
-        copy.wait()
-
-
-def base_kernel(bits, points, near, far, near_part, far_part, sems, out_sems):
+
+
+def base_kernel(bits, points, near, far, squares, near_part, far_part, sems, out_sems):
     parts = near_part, far_part
     copies = column_copies(points, 0, parts, own_place(bits), sems)
     for copy in copies:
         copy.start()
     for copy in copies:
         copy.wait()
-    put_rows(parts, (near, far), 0, out_sems)
+    copies = row_copies(parts, (near, far), 0, out_sems)
+    for copy in copies:
+        copy.start()
+    total = jnp.zeros_like(squares)
+    for part in parts:
+        for begin in range(0, part.shape[1], 128):
+            block = part[:, begin : begin + 128]
+            total = total + block * block
+    squares[...] = total
+    for copy in copies:
+        copy.wait()
 
 
 def extra_kernel(
@@ -109,17 +115,29 @@
 
     for copy in column_copies(first, 0, parts, place, sems):
         copy.wait()
-    put_rows(parts, (near, far), points.shape[0], out_sems)
+    copies = row_copies(parts, (near, far), points.shape[0], out_sems)
+    for copy in copies:
+        copy.start()
+    for copy in copies:
+        copy.wait()
 
 
 def arrange_base(points, bits):
     rows, width = points.shape
     blocks = 2 ** (1 + len(bits))
     if (width // blocks) % 128:
-        order = jnp.arange(blocks) ^ own_place(bits)
-        whole = points.reshape(rows, blocks, -1)[:, order].reshape(rows, width)
-        return whole[:, : width // 2], whole[:, width // 2 :]
-    return arrange_call(base_kernel, points, rows, bits, {})(points)
+        near, far = reorder(points, bits)
+        return near, far, jnp.sum(points * points, axis=1, keepdims=True)
+    near, far, sums = arrange_call(base_kernel, points, rows, bits, {})(points)
+    return near, far, jnp.sum(sums, axis=1, keepdims=True)
+
+
+def reorder(points, bits):
+    rows, width = points.shape
+    blocks = 2 ** (1 + len(bits))
+    order = jnp.arange(blocks) ^ own_place(bits)
+    whole = points.reshape(rows, blocks, -1)[:, order].reshape(rows, width)
+    return whole[:, : width // 2], whole[:, width // 2 :]
 
 
 def arrange_extra(points, first, second, near, far, bits):
@@ -129,7 +147,7 @@
     if (width // blocks) % 128:
         group = 2 * lax.axis_index("side") + lax.axis_index("core")
         extra = jnp.where(group == 1, second, jnp.where(group == 3, points[half:], first))
-        extra = arrange_base(extra, bits)
+        extra = reorder(extra, bits)
         return tuple(jnp.concatenate(pair, axis=0) for pair in zip((near, far), extra))
     return arrange_call(extra_kernel, points, half, bits, {3: 0, 4: 1})(
         points, first, second, near, far
@@ -141,11 +159,15 @@
     anywhere = pl.BlockSpec(memory_space=pl.ANY)
     shape = jax.ShapeDtypeStruct((rows + rows // 2, width // 2), points.dtype)
     part = pltpu.VMEM((count, width // 2), points.dtype)
+    shapes, specs = (shape, shape), (anywhere, anywhere)
+    if not aliases:
+        shapes += (jax.ShapeDtypeStruct((count, 128), points.dtype),)
+        specs += (pl.BlockSpec(memory_space=pltpu.VMEM),)
     return pl.pallas_call(
         functools.partial(kernel, bits),
-        out_shape=(shape, shape),
+        out_shape=shapes,
         in_specs=[anywhere] * (5 if aliases else 1),
-        out_specs=(anywhere, anywhere),
+        out_specs=specs,
         scratch_shapes=[
             part,
             part,
@@ -287,19 +309,15 @@
     return jnp.concatenate(parts, axis=1), both[:PAD], both[PAD:]
 
 
-def weigh(logits, mass, squares):
+def weigh(logits, mass, squares, totals):
     scaled = jax.nn.softmax(logits, axis=1) * mass
     columns = jnp.sum(scaled, axis=0, keepdims=True)
-    rank = scaled.shape[1]
-    return scaled, jnp.concatenate(
-        [
-            jnp.sum(scaled * squares, axis=0, keepdims=True),
-            columns,
-            jnp.broadcast_to(jnp.sum(columns, axis=1, keepdims=True), columns.shape),
-            jnp.zeros((PAD - 3, rank), jnp.float32),
-        ],
-        axis=0,
-    )
+    sums = [jnp.sum(scaled * squares, axis=0, keepdims=True), columns]
+    if totals:
+        total = jnp.sum(columns, axis=1, keepdims=True)
+        sums.append(jnp.broadcast_to(total, columns.shape))
+    rest = PAD - len(sums)
+    return scaled, jnp.concatenate([*sums, jnp.zeros((rest, columns.shape[1]))], axis=0)
 
 
 def make_body(axes):
@@ -319,16 +337,15 @@
             devices *= lax.axis_size(axis)
 
         moved = move(points)
-        squares = jnp.sum(points * points, axis=1, keepdims=True)
         mass = masses[:, None]
-        near, far = arrange_base(points, bits)
+        near, far, squares = arrange_base(points, bits)
         lanes = lax.broadcasted_iota(jnp.int32, (rows, 128), 1)
         packed = jnp.concatenate(
             [log_factor, jnp.where(lanes < 64, mass, squares)], axis=1
         )
 
         second_core = lax.axis_index("core") == 1
-        scaled, statistics = weigh(log_factor, mass, squares)
+        scaled, statistics = weigh(log_factor, mass, squares, True)
         stay_stats = jnp.where(group == 2, statistics, 0.0)
         statistics = jnp.where(group == 2, 0.0, statistics)
         other = swap(contract_rows(far[:rows], scaled), "core")
@@ -350,25 +367,27 @@
         squares = jnp.concatenate([squares, extra[:, rank + 64 : rank + 65]], axis=0)
         real = source | (lax.broadcasted_iota(jnp.int32, (logits.shape[0], 1), 0) >= rows)
 
+        own_mass, mass_total = own[2:3], facing[2:3]
         for iteration in range(ITERS):
             if iteration:
-                scaled, statistics = weigh(logits, mass, squares)
+                scaled, statistics = weigh(logits, mass, squares, False)
                 other = swap(contract_rows(far, scaled), "core")
                 held, other = together(contract_rows(near, scaled), other)
                 own, facing = reduce_moment(held + other, statistics, bits)
                 moment, own, facing = gather_moment(own, facing, bits)
             cross, other = together(times(near, moment), swap(moment, "core"))
             cross = cross + times(far, other)
-            share = facing[1:2] / facing[2:3]
-            marginal = 0.5 * (own[1:2] / own[2:3] + share)
+            share = facing[1:2] / mass_total
+            marginal = 0.5 * (own[1:2] / own_mass + share)
             gradient = (
-                squares * share - 2.0 * (cross / facing[2:3]) + facing[0:1] / facing[2:3]
+                squares * share - 2.0 * (cross / mass_total) + facing[0:1] / mass_total
             ) / marginal
             centred = gradient - jnp.mean(gradient, axis=1, keepdims=True)
             largest = jnp.max(jnp.where(real, jnp.abs(centred), 0.0))
             spread = jnp.full((devices, 128), largest, jnp.float32)
-            largest = jnp.max(lax.all_to_all(spread, axes, 0, 0, tiled=True))
-            logits = logits - step_scale / (largest + 1e-06) * gradient
+            largest = jnp.max(lax.all_to_all(spread, axes, 0, 0, tiled=True), axis=0)
+            rate = jnp.tile(step_scale / (largest + 1e-06), rank // 128)
+            logits = logits - rate[None, :] * gradient
         factors = rank * jax.nn.softmax(logits, axis=1)
         return from_side(factors[:rows], factors[rows:])
 

time: 208 us -> 204 us (0.981)
  other arithmetic: 11.7 us -> 9.28 us
where the time goes in v1:
time: 204 us
  starting transfers between devices  78.1 us (38%)
  waiting for transfers between devices  73.3 us (36%)
  matrix products  19.5 us (10%)
  blocking collectives  9.71 us (5%)
  other arithmetic  9.28 us (5%)
  local copies, waits for them, and re-layouts  6.64 us (3%)
  Pallas kernels  6.17 us (3%)
    ppermute x26, starting transfers between devices, swap(): return lax.ppermute(value, axis, [(0, 1), (1, 0)])  56.2 us
    ppermute x26, waiting for transfers between devices, swap(): return lax.ppermute(value, axis, [(0, 1), (1, 0)])  48.5 us
    ppermute x4, waiting for transfers between devices, across(): return lax.ppermute(value, ('side', axis), pairs)  16.2 us
    dot_general x4, matrix products, contract_rows(): lax.dot_general(left, right, (((0,), (0,)), ((), ())), precision=highest,...  11.2 us
    all_to_all x1, blocking collectives, steps(): largest = jnp.max(lax.all_to_all(spread, axes, 0, 0, tiled=True), axis=0)  9.71 us
    dot_general x4, matrix products, times(): jnp.dot(left, right, precision=highest, preferred_element_type=jnp.float32)  8.36 us
    all_to_all x1, starting transfers between devices, steps(): largest = jnp.max(lax.all_to_all(spread, axes, 0, 0, tiled=True), axis=0)  7.23 us
    all_to_all x1, waiting for transfers between devices, steps(): largest = jnp.max(lax.all_to_all(spread, axes, 0, 0, tiled=True), axis=0)  6.66 us
  transfers between devices with their start and end apart: 37, of which 24 were waited for; matrix products, arithmetic and copies ran while one was open for 7% of the time, Pallas kernels for 1%

profile of v1, /device:TPU:1, one launch (start us, length us, event | category | flops | bytes accessed | tf_op | source)
XLA Modules:
  0.0 203.6 jit_solution(589734479505531643)
XLA Ops:
  0.0 3.8 %shard_map.37 = (f32[384,1024]{1,0:T(8,128)}, f32[384,1024]{1,0:T(8,128)}, f32[256,128]{1,0:T(8,128)}) custom-call(f32[256,2048]{1,0:T(8,128)} %points.3), custom_call_target="tpu_custom_call" | custom-call | tf_op jit(solution)/shard_map/pallas_call | solution.py:131
  6.1 4.0 %convolution_bitcast_fusion = f32[1024,256]{1,0:T(8,128)} fusion(f32[256,256]{1,0:T(8,128)S(1)} %get-tuple-element.157, f32[384,1024]{1,0:T(8,128)} %get-tuple-element.76.far_in), kind=kOutput, calls=%fused_computation | convolution fusion | flops 805306368 | bytes 2359296 | tf_op jit(solution)/shard_map/dot_general | solution.py:27
  11.0 1.8 convolution_bitcast_fusion.1
  13.4 2.6 %collective-permute-start.3 = (f32[520,256]{1,0:T(8,128)S(1)}, f32[520,256]{1,0:T(8,128)S(1)}, u32[]{:S(2)}, u32[]{:S(2)}) collective-permute-start(f32[520,256]{1,0:T(8,128)S(1)} %get-tuple-element.79), channel_id=1, source_target_pairs={{0,1},{1,0},{2,3},{3,2},{4,5},{5,4},{6,7},{7,6},{8,9},{9,8},{10,11... | collective-permute-start | bytes 1597448 | tf_op jit(solution)/shard_map/ppermute | solution.py:19
  17.3 11.0 %collective-permute-done.3 = f32[520,256]{1,0:T(8,128)S(1)} collective-permute-done((f32[520,256]{1,0:T(8,128)S(1)}, f32[520,256]{1,0:T(8,128)S(1)}, u32[]{:S(2)}, u32[]{:S(2)}) %collective-permute-start.3) | collective-permute-done | bytes 532512 | tf_op jit(solution)/shard_map/ppermute | solution.py:19
  31.2 5.2 %collective-permute-done.5 = f32[264,256]{1,0:T(8,128)S(1)} collective-permute-done((f32[264,256]{1,0:T(8,128)S(1)}, f32[264,256]{1,0:T(8,128)S(1)}, u32[]{:S(2)}, u32[]{:S(2)}) %collective-permute-start.5) | collective-permute-done | bytes 270368 | tf_op jit(solution)/shard_map/ppermute | solution.py:19
  38.9 2.3 %collective-permute-start.8 = (f32[136,256]{1,0:T(8,128)S(1)}, f32[136,256]{1,0:T(8,128)S(1)}, u32[]{:S(2)}, u32[]{:S(2)}) collective-permute-start(f32[136,256]{1,0:T(8,128)S(1)} %get-tuple-element.88), channel_id=1, source_target_pairs={{0,20},{4,16},{16,4},{20,0},{1,21},{5,17},{17,5},{21,1},{2,22},{6,... | collective-permute-start | bytes 417800 | tf_op jit(solution)/shard_map/ppermute | solution.py:218
  41.6 9.8 %collective-permute-done.8 = f32[136,256]{1,0:T(8,128)S(1)} collective-permute-done((f32[136,256]{1,0:T(8,128)S(1)}, f32[136,256]{1,0:T(8,128)S(1)}, u32[]{:S(2)}, u32[]{:S(2)}) %collective-permute-start.8) | collective-permute-done | bytes 139296 | tf_op jit(solution)/shard_map/ppermute | solution.py:218
  51.4 2.1 %collective-permute-done.9 = f32[136,256]{1,0:T(8,128)S(1)} collective-permute-done((f32[136,256]{1,0:T(8,128)S(1)}, f32[136,256]{1,0:T(8,128)S(1)}, u32[]{:S(2)}, u32[]{:S(2)}) %collective-permute-start.9) | collective-permute-done | bytes 139296 | tf_op jit(solution)/shard_map/ppermute | solution.py:19
  58.7 3.3 %collective-permute-start.11 = (f32[8,256]{1,0:T(8,128)S(1)}, f32[8,256]{1,0:T(8,128)S(1)}, u32[]{:S(2)}, u32[]{:S(2)}) collective-permute-start(f32[8,256]{1,0:T(8,128)S(1)} %slice.325), channel_id=1, source_target_pairs={{0,16},{16,0},{1,17},{17,1},{2,18},{18,2},{3,19},{19,3},{4,20},{20... | collective-permute-start | bytes 24584 | tf_op jit(solution)/shard_map/ppermute | solution.py:19
  63.6 2.9 %collective-permute-start.12 = (f32[256,128]{1,0:T(8,128)S(1)}, f32[256,128]{1,0:T(8,128)S(1)}, u32[]{:S(2)}, u32[]{:S(2)}) collective-permute-start(f32[256,128]{1,0:T(8,128)S(1)} %get-tuple-element.96), channel_id=1, source_target_pairs={{0,2},{2,0},{1,3},{3,1},{4,6},{6,4},{5,7},{7,5},{8,10},{10,8},{9,1... | collective-permute-start | bytes 393224 | tf_op jit(solution)/shard_map/ppermute | solution.py:19
  66.8 2.4 %collective-permute-done.12 = f32[256,128]{1,0:T(8,128)S(1)} collective-permute-done((f32[256,128]{1,0:T(8,128)S(1)}, f32[256,128]{1,0:T(8,128)S(1)}, u32[]{:S(2)}, u32[]{:S(2)}) %collective-permute-start.12) | collective-permute-done | bytes 131104 | tf_op jit(solution)/shard_map/ppermute | solution.py:19
  71.4 22.2 %collective-permute-start.16 = (f32[16,256]{1,0:T(8,128)S(1)}, f32[16,256]{1,0:T(8,128)S(1)}, u32[]{:S(2)}, u32[]{:S(2)}) collective-permute-start(f32[16,256]{1,0:T(8,128)S(1)} %pad_maximum_fusion.25), channel_id=1, source_target_pairs={{0,8},{8,0},{1,9},{9,1},{2,10},{10,2},{3,11},{11,3},{4,12},{12,4},... | collective-permute-start | bytes 49160 | tf_op jit(solution)/shard_map/ppermute | solution.py:19
  97.6 3.9 %collective-permute-start.19 = (f32[1024,256]{1,0:T(8,128)}, f32[1024,256]{1,0:T(8,128)}, u32[]{:S(2)}, u32[]{:S(2)}) collective-permute-start(f32[1024,256]{1,0:T(8,128)} %pad_maximum_fusion), channel_id=1, source_target_pairs={{0,8},{8,0},{1,9},{9,1},{2,10},{10,2},{3,11},{11,3},{4,12},{12,4},... | collective-permute-start | bytes 3145736 | tf_op jit(solution)/shard_map/ppermute | solution.py:19
  102.8 2.4 %shard_map.38 = (f32[384,1024]{1,0:T(8,128)}, f32[384,1024]{1,0:T(8,128)}) custom-call(f32[256,2048]{1,0:T(8,128)} %points.3, f32[128,2048]{1,0:T(8,128)} %collective-permute-done.17.first, f32[128,2048]{1,0:T(8,128)} %copy-done.5, f32[384,1024]{1,0:T(8,128)} %get-tuple-element.75.near_in, ...), custom_call_target="tpu_custom_call", output_to_operand_aliasing={{0}: (3, {}), {1}: (4, {})} | custom-call | tf_op jit(solution)/shard_map/pallas_call | solution.py:152
  105.2 2.9 %fusion.25 = f32[384,256]{1,0:T(8,128)S(1)} fusion(f32[384,1024]{1,0:T(8,128)} %get-tuple-element.107, f32[1024,128]{1,0:T(8,128)S(1)} %bitcast.51, f32[512,128]{1,0:T(8,128)S(1)} %collective-permute-done.14, f32[512,128]{1,0:T(8,128)S(1)} %pad_maximum_fusion.11), kind=kOutput, calls=%fused_computation.119 | convolution fusion | flops 1208483840 | bytes 3014656 | tf_op jit(solution)/shard_map/dot_general | solution.py:37
  108.2 2.6 %fusion.38 = f32[384,256]{1,0:T(8,128)S(1)} fusion(f32[384,1024]{1,0:T(8,128)S(1)} %copy-done.2, f32[1024,256]{1,0:T(8,128)} %collective-permute-done.19), kind=kOutput, calls=%fused_computation.132 | convolution fusion | flops 1207959552 | bytes 3014656 | tf_op jit(solution)/shard_map/dot_general | solution.py:37
  113.1 7.2 %all-to-all-start = ((f32[32,1,128]{2,1,0:T(1,128)}), f32[32,1,128]{2,1,0:T(1,128)S(1)}, u32[]{:S(2)}, u32[]{:S(2)}) async-start(f32[32,1,128]{2,1,0:T(1,128)} %broadcast_in_dim.99), calls=%async_computation | async-start | bytes 32768 | tf_op jit(solution)/shard_map/all_to_all | solution.py:388
  120.5 6.7 %all-to-all-done = f32[32,1,128]{2,1,0:T(1,128)S(1)} async-done(((f32[32,1,128]{2,1,0:T(1,128)}), f32[32,1,128]{2,1,0:T(1,128)S(1)}, u32[]{:S(2)}, u32[]{:S(2)}) %all-to-all-start) | async-done | bytes 16416 | tf_op jit(solution)/shard_map/all_to_all | solution.py:388
  127.9 2.6 %fusion.40 = f32[1024,256]{1,0:T(8,128)S(1)} fusion(f32[384,1024]{1,0:T(8,128)S(1)} %copy-done.2, f32[384,256]{1,0:T(8,128)S(1)} %get-tuple-element.150), kind=kOutput, calls=%fused_computation.134 | convolution fusion | flops 1207959552 | bytes 3014656 | tf_op jit(solution)/shard_map/dot_general | solution.py:27
  131.4 2.6 %fusion.39 = f32[1024,256]{1,0:T(8,128)S(1)} fusion(f32[384,1024]{1,0:T(8,128)S(1)} %copy-done.1, f32[384,256]{1,0:T(8,128)S(1)} %get-tuple-element.150), kind=kOutput, calls=%fused_computation.133 | convolution fusion | flops 1207959552 | bytes 3014656 | tf_op jit(solution)/shard_map/dot_general | solution.py:27
  135.1 7.3 %collective-permute-done.21 = f32[520,128]{1,0:T(8,128)S(1)} collective-permute-done((f32[520,128]{1,0:T(8,128)S(1)}, f32[520,128]{1,0:T(8,128)S(1)}, u32[]{:S(2)}, u32[]{:S(2)}) %collective-permute-start.21) | collective-permute-done | bytes 266272 | tf_op jit(solution)/shard_map/ppermute | solution.py:19
  144.1 2.5 %collective-permute-done.23 = f32[264,128]{1,0:T(8,128)S(1)} collective-permute-done((f32[264,128]{1,0:T(8,128)S(1)}, f32[264,128]{1,0:T(8,128)S(1)}, u32[]{:S(2)}, u32[]{:S(2)}) %collective-permute-start.23) | collective-permute-done | bytes 135200 | tf_op jit(solution)/shard_map/ppermute | solution.py:19
  148.8 2.4 %collective-permute-done.25 = f32[136,256]{1,0:T(8,128)S(1)} collective-permute-done((f32[136,256]{1,0:T(8,128)S(1)}, f32[136,256]{1,0:T(8,128)S(1)}, u32[]{:S(2)}, u32[]{:S(2)}) %collective-permute-start.25) | collective-permute-done | bytes 139296 | tf_op jit(solution)/shard_map/ppermute | solution.py:218
  151.2 3.6 %collective-permute-done.26 = f32[136,256]{1,0:T(8,128)S(1)} collective-permute-done((f32[136,256]{1,0:T(8,128)S(1)}, f32[136,256]{1,0:T(8,128)S(1)}, u32[]{:S(2)}, u32[]{:S(2)}) %collective-permute-start.26) | collective-permute-done | bytes 139296 | tf_op jit(solution)/shard_map/ppermute | solution.py:218
  154.9 5.9 %collective-permute-done.27 = f32[136,256]{1,0:T(8,128)S(1)} collective-permute-done((f32[136,256]{1,0:T(8,128)S(1)}, f32[136,256]{1,0:T(8,128)S(1)}, u32[]{:S(2)}, u32[]{:S(2)}) %collective-permute-start.27) | collective-permute-done | bytes 139296 | tf_op jit(solution)/shard_map/ppermute | solution.py:19
  162.2 4.0 %collective-permute-done.28 = f32[256,128]{1,0:T(8,128)S(1)} collective-permute-done((f32[256,128]{1,0:T(8,128)S(1)}, f32[256,128]{1,0:T(8,128)S(1)}, u32[]{:S(2)}, u32[]{:S(2)}) %collective-permute-start.28) | collective-permute-done | bytes 131104 | tf_op jit(solution)/shard_map/ppermute | solution.py:19
  167.5 8.0 %collective-permute-start.32 = (f32[16,256]{1,0:T(8,128)S(1)}, f32[16,256]{1,0:T(8,128)S(1)}, u32[]{:S(2)}, u32[]{:S(2)}) collective-permute-start(f32[16,256]{1,0:T(8,128)S(1)} %pad_maximum_fusion.26), channel_id=1, source_target_pairs={{0,8},{8,0},{1,9},{9,1},{2,10},{10,2},{3,11},{11,3},{4,12},{12,4},... | collective-permute-start | bytes 49160 | tf_op jit(solution)/shard_map/ppermute | solution.py:19
  176.5 3.9 %collective-permute-start.33 = (f32[1024,256]{1,0:T(8,128)S(1)}, f32[1024,256]{1,0:T(8,128)S(1)}, u32[]{:S(2)}, u32[]{:S(2)}) collective-permute-start(f32[1024,256]{1,0:T(8,128)S(1)} %pad_maximum_fusion.1), channel_id=1, source_target_pairs={{0,8},{8,0},{1,9},{9,1},{2,10},{10,2},{3,11},{11,3},{4,12},{12,4},... | collective-permute-start | bytes 3145736 | tf_op jit(solution)/shard_map/ppermute | solution.py:19
  185.8 9.7 %all_to_all.12 = f32[32,1,128]{2,1,0:T(1,128)S(1)} all-to-all(f32[32,1,128]{2,1,0:T(1,128)S(1)} %broadcast_in_dim.104), channel_id=1, replica_groups=mesh['side'=2,'core'=2,'bit2'=2,'bit1'=2,'bit0'=2] {'side','core','bit2'..., dimensions={0} | all-to-all | bytes 32768 | tf_op jit(solution)/shard_map/all_to_all | solution.py:388
  196.8 4.0 %collective-permute-start.35 = (f32[128,256]{1,0:T(8,128)S(1)}, f32[128,256]{1,0:T(8,128)S(1)}, u32[]{:S(2)}, u32[]{:S(2)}) collective-permute-start(f32[128,256]{1,0:T(8,128)S(1)} %slice.357), channel_id=1, source_target_pairs={{8,16},{9,17},{10,18},{11,19},{12,20},{13,21},{14,22},{15,23}} | collective-permute-start | bytes 393224 | tf_op jit(solution)/shard_map/ppermute | solution.py:193
  200.9 1.9 collective-permute-done.35
  (185 shorter events, 45.0 us)
Async XLA Ops:
  13.4 15.0 %collective-permute-start.3 = (f32[520,256]{1,0:T(8,128)S(1)}, f32[520,256]{1,0:T(8,128)S(1)}, u32[]{:S(2)}, u32[]{:S(2)}) collective-permute-start(f32[520,256]{1,0:T(8,128)S(1)} %get-tuple-element.79), channel_id=1, source_target_pairs={{0,1},{1,0},{2,3},{3,2},{4,5},{5,4},{6,7},{7,6},{8,9},{9,8},{10,11... | collective-permute-start | bytes 1597448 | tf_op jit(solution)/shard_map/ppermute | solution.py:19
  16.0 13.2 %collective-permute-start.4 = (f32[520,256]{1,0:T(8,128)S(1)}, f32[520,256]{1,0:T(8,128)S(1)}, u32[]{:S(2)}, u32[]{:S(2)}) collective-permute-start(f32[520,256]{1,0:T(8,128)S(1)} %get-tuple-element.80), channel_id=1, source_target_pairs={{0,2},{2,0},{1,3},{3,1},{4,6},{6,4},{5,7},{7,5},{8,10},{10,8},{9,1... | collective-permute-start | bytes 1597448 | tf_op jit(solution)/shard_map/ppermute | solution.py:19
  29.6 6.8 %collective-permute-start.5 = (f32[264,256]{1,0:T(8,128)S(1)}, f32[264,256]{1,0:T(8,128)S(1)}, u32[]{:S(2)}, u32[]{:S(2)}) collective-permute-start(f32[264,256]{1,0:T(8,128)S(1)} %pad_maximum_fusion.7), channel_id=1, source_target_pairs={{0,2},{2,0},{1,3},{3,1},{4,6},{6,4},{5,7},{7,5},{8,10},{10,8},{9,1... | collective-permute-start | bytes 811016 | tf_op jit(solution)/shard_map/ppermute | solution.py:19
  31.0 6.5 %collective-permute-start.6 = (f32[264,256]{1,0:T(8,128)S(1)}, f32[264,256]{1,0:T(8,128)S(1)}, u32[]{:S(2)}, u32[]{:S(2)}) collective-permute-start(f32[264,256]{1,0:T(8,128)S(1)} %pad_maximum_fusion.8), channel_id=1, source_target_pairs={{0,1},{1,0},{2,3},{3,2},{4,5},{5,4},{6,7},{7,6},{8,9},{9,8},{10,11... | collective-permute-start | bytes 811016 | tf_op jit(solution)/shard_map/ppermute | solution.py:19
  38.9 12.5 %collective-permute-start.8 = (f32[136,256]{1,0:T(8,128)S(1)}, f32[136,256]{1,0:T(8,128)S(1)}, u32[]{:S(2)}, u32[]{:S(2)}) collective-permute-start(f32[136,256]{1,0:T(8,128)S(1)} %get-tuple-element.88), channel_id=1, source_target_pairs={{0,20},{4,16},{16,4},{20,0},{1,21},{5,17},{17,5},{21,1},{2,22},{6,... | collective-permute-start | bytes 417800 | tf_op jit(solution)/shard_map/ppermute | solution.py:218
  41.2 12.3 %collective-permute-start.9 = (f32[136,256]{1,0:T(8,128)S(1)}, f32[136,256]{1,0:T(8,128)S(1)}, u32[]{:S(2)}, u32[]{:S(2)}) collective-permute-start(f32[136,256]{1,0:T(8,128)S(1)} %pad_maximum_fusion.19), channel_id=1, source_target_pairs={{0,4},{4,0},{1,5},{5,1},{2,6},{6,2},{3,7},{7,3},{8,12},{12,8},{9,1... | collective-permute-start | bytes 417800 | tf_op jit(solution)/shard_map/ppermute | solution.py:19
  53.6 10.0 %collective-permute-start.10 = (f32[128,256]{1,0:T(8,128)S(1)}, f32[128,256]{1,0:T(8,128)S(1)}, u32[]{:S(2)}, u32[]{:S(2)}) collective-permute-start(f32[128,256]{1,0:T(8,128)S(1)} %slice.324), channel_id=1, source_target_pairs={{0,4},{4,0},{1,5},{5,1},{2,6},{6,2},{3,7},{7,3},{8,12},{12,8},{9,1... | collective-permute-start | bytes 393224 | tf_op jit(solution)/shard_map/ppermute | solution.py:19
  54.7 47.0 %collective-permute-start.17 = (f32[128,2048]{1,0:T(8,128)}, f32[128,2048]{1,0:T(8,128)}, u32[]{:S(2)}, u32[]{:S(2)}) collective-permute-start(f32[128,2048]{1,0:T(8,128)} %slice.267), channel_id=1, source_target_pairs={{16,0},{24,16},{17,1},{25,17},{18,2},{26,18},{19,3},{27,19},{20,4}... | collective-permute-start | bytes 3145736 | tf_op jit(solution)/shard_map/ppermute | solution.py:184
  57.5 44.3 %collective-permute-start.18 = (f32[128,2048]{1,0:T(8,128)}, f32[128,2048]{1,0:T(8,128)S(1)}, u32[]{:S(2)}, u32[]{:S(2)}) collective-permute-start(f32[128,2048]{1,0:T(8,128)} %slice.268), channel_id=1, source_target_pairs={{16,8},{17,9},{18,10},{19,11},{20,12},{21,13},{22,14},{23,15}} | collective-permute-start | bytes 3145736 | tf_op jit(solution)/shard_map/ppermute | solution.py:185
  58.7 4.8 %collective-permute-start.11 = (f32[8,256]{1,0:T(8,128)S(1)}, f32[8,256]{1,0:T(8,128)S(1)}, u32[]{:S(2)}, u32[]{:S(2)}) collective-permute-start(f32[8,256]{1,0:T(8,128)S(1)} %slice.325), channel_id=1, source_target_pairs={{0,16},{16,0},{1,17},{17,1},{2,18},{18,2},{3,19},{19,3},{4,20},{20... | collective-permute-start | bytes 24584 | tf_op jit(solution)/shard_map/ppermute | solution.py:19
  63.6 5.7 %collective-permute-start.12 = (f32[256,128]{1,0:T(8,128)S(1)}, f32[256,128]{1,0:T(8,128)S(1)}, u32[]{:S(2)}, u32[]{:S(2)}) collective-permute-start(f32[256,128]{1,0:T(8,128)S(1)} %get-tuple-element.96), channel_id=1, source_target_pairs={{0,2},{2,0},{1,3},{3,1},{4,6},{6,4},{5,7},{7,5},{8,10},{10,8},{9,1... | collective-permute-start | bytes 393224 | tf_op jit(solution)/shard_map/ppermute | solution.py:19
  66.5 4.2 %collective-permute-start.13 = (f32[256,128]{1,0:T(8,128)S(1)}, f32[256,128]{1,0:T(8,128)S(1)}, u32[]{:S(2)}, u32[]{:S(2)}) collective-permute-start(f32[256,128]{1,0:T(8,128)S(1)} %get-tuple-element.97), channel_id=1, source_target_pairs={{0,1},{1,0},{2,3},{3,2},{4,5},{5,4},{6,7},{7,6},{8,9},{9,8},{10,11... | collective-permute-start | bytes 393224 | tf_op jit(solution)/shard_map/ppermute | solution.py:19
  70.8 25.0 %collective-permute-start.14 = (f32[512,128]{1,0:T(8,128)S(1)}, f32[512,128]{1,0:T(8,128)S(1)}, u32[]{:S(2)}, u32[]{:S(2)}) collective-permute-start(f32[512,128]{1,0:T(8,128)S(1)} %pad_maximum_fusion.11), channel_id=1, source_target_pairs={{0,1},{1,0},{2,3},{3,2},{4,5},{5,4},{6,7},{7,6},{8,9},{9,8},{10,11... | collective-permute-start | bytes 786440 | tf_op jit(solution)/shard_map/ppermute | solution.py:19
  71.2 25.3 %collective-permute-start.15 = (f32[512,128]{1,0:T(8,128)S(1)}, f32[512,128]{1,0:T(8,128)S(1)}, u32[]{:S(2)}, u32[]{:S(2)}) collective-permute-start(f32[512,128]{1,0:T(8,128)S(1)} %pad_maximum_fusion.12), channel_id=1, source_target_pairs={{0,2},{2,0},{1,3},{3,1},{4,6},{6,4},{5,7},{7,5},{8,10},{10,8},{9,1... | collective-permute-start | bytes 786440 | tf_op jit(solution)/shard_map/ppermute | solution.py:19
  71.4 23.0 %collective-permute-start.16 = (f32[16,256]{1,0:T(8,128)S(1)}, f32[16,256]{1,0:T(8,128)S(1)}, u32[]{:S(2)}, u32[]{:S(2)}) collective-permute-start(f32[16,256]{1,0:T(8,128)S(1)} %pad_maximum_fusion.25), channel_id=1, source_target_pairs={{0,8},{8,0},{1,9},{9,1},{2,10},{10,2},{3,11},{11,3},{4,12},{12,4},... | collective-permute-start | bytes 49160 | tf_op jit(solution)/shard_map/ppermute | solution.py:19
  94.5 7.1 %collective-permute-start = (f32[128,384]{1,0:T(8,128)S(1)}, f32[128,384]{1,0:T(8,128)S(1)}, u32[]{:S(2)}, u32[]{:S(2)}) collective-permute-start(f32[128,384]{1,0:T(8,128)S(1)} %slice.235), channel_id=1, source_target_pairs={{16,8},{17,9},{18,10},{19,11},{20,12},{21,13},{22,14},{23,15}} | collective-permute-start | bytes 589832 | tf_op jit(solution)/shard_map/ppermute | solution.py:185
  95.8 5.8 %collective-permute-start.1 = (f32[128,384]{1,0:T(8,128)S(1)}, f32[128,384]{1,0:T(8,128)S(1)}, u32[]{:S(2)}, u32[]{:S(2)}) collective-permute-start(f32[128,384]{1,0:T(8,128)S(1)} %fusion.5), channel_id=1, source_target_pairs={{16,0},{24,16},{17,1},{25,17},{18,2},{26,18},{19,3},{27,19},{20,4}... | collective-permute-start | bytes 589832 | tf_op jit(solution)/shard_map/ppermute | solution.py:184
  97.6 10.5 %collective-permute-start.19 = (f32[1024,256]{1,0:T(8,128)}, f32[1024,256]{1,0:T(8,128)}, u32[]{:S(2)}, u32[]{:S(2)}) collective-permute-start(f32[1024,256]{1,0:T(8,128)} %pad_maximum_fusion), channel_id=1, source_target_pairs={{0,8},{8,0},{1,9},{9,1},{2,10},{10,2},{3,11},{11,3},{4,12},{12,4},... | collective-permute-start | bytes 3145736 | tf_op jit(solution)/shard_map/ppermute | solution.py:19
  113.1 14.0 %all-to-all-start = ((f32[32,1,128]{2,1,0:T(1,128)}), f32[32,1,128]{2,1,0:T(1,128)S(1)}, u32[]{:S(2)}, u32[]{:S(2)}) async-start(f32[32,1,128]{2,1,0:T(1,128)} %broadcast_in_dim.99), calls=%async_computation | async-start | bytes 32768 | tf_op jit(solution)/shard_map/all_to_all | solution.py:388
  134.4 8.0 %collective-permute-start.21 = (f32[520,128]{1,0:T(8,128)S(1)}, f32[520,128]{1,0:T(8,128)S(1)}, u32[]{:S(2)}, u32[]{:S(2)}) collective-permute-start(f32[520,128]{1,0:T(8,128)S(1)} %pad_maximum_fusion.9), channel_id=1, source_target_pairs={{0,1},{1,0},{2,3},{3,2},{4,5},{5,4},{6,7},{7,6},{8,9},{9,8},{10,11... | collective-permute-start | bytes 798728 | tf_op jit(solution)/shard_map/ppermute | solution.py:19
  134.8 7.7 %collective-permute-start.22 = (f32[520,128]{1,0:T(8,128)S(1)}, f32[520,128]{1,0:T(8,128)S(1)}, u32[]{:S(2)}, u32[]{:S(2)}) collective-permute-start(f32[520,128]{1,0:T(8,128)S(1)} %pad_maximum_fusion.10), channel_id=1, source_target_pairs={{0,2},{2,0},{1,3},{3,1},{4,6},{6,4},{5,7},{7,5},{8,10},{10,8},{9,1... | collective-permute-start | bytes 798728 | tf_op jit(solution)/shard_map/ppermute | solution.py:19
  143.0 4.2 %collective-permute-start.24 = (f32[264,128]{1,0:T(8,128)S(1)}, f32[264,128]{1,0:T(8,128)S(1)}, u32[]{:S(2)}, u32[]{:S(2)}) collective-permute-start(f32[264,128]{1,0:T(8,128)S(1)} %pad_maximum_fusion.23), channel_id=1, source_target_pairs={{0,1},{1,0},{2,3},{3,2},{4,5},{5,4},{6,7},{7,6},{8,9},{9,8},{10,11... | collective-permute-start | bytes 405512 | tf_op jit(solution)/shard_map/ppermute | solution.py:19
  147.6 7.2 %collective-permute-start.26 = (f32[136,256]{1,0:T(8,128)S(1)}, f32[136,256]{1,0:T(8,128)S(1)}, u32[]{:S(2)}, u32[]{:S(2)}) collective-permute-start(f32[136,256]{1,0:T(8,128)S(1)} %get-tuple-element.124), channel_id=1, source_target_pairs={{0,20},{4,16},{16,4},{20,0},{1,21},{5,17},{17,5},{21,1},{2,22},{6,... | collective-permute-start | bytes 417800 | tf_op jit(solution)/shard_map/ppermute | solution.py:218
  154.8 6.0 %collective-permute-start.27 = (f32[136,256]{1,0:T(8,128)S(1)}, f32[136,256]{1,0:T(8,128)S(1)}, u32[]{:S(2)}, u32[]{:S(2)}) collective-permute-start(f32[136,256]{1,0:T(8,128)S(1)} %fusion.13), channel_id=1, source_target_pairs={{0,4},{4,0},{1,5},{5,1},{2,6},{6,2},{3,7},{7,3},{8,12},{12,8},{9,1... | collective-permute-start | bytes 417800 | tf_op jit(solution)/shard_map/ppermute | solution.py:19
  160.9 5.3 %collective-permute-start.28 = (f32[256,128]{1,0:T(8,128)S(1)}, f32[256,128]{1,0:T(8,128)S(1)}, u32[]{:S(2)}, u32[]{:S(2)}) collective-permute-start(f32[256,128]{1,0:T(8,128)S(1)} %get-tuple-element.127), channel_id=1, source_target_pairs={{0,2},{2,0},{1,3},{3,1},{4,6},{6,4},{5,7},{7,5},{8,10},{10,8},{9,1... | collective-permute-start | bytes 393224 | tf_op jit(solution)/shard_map/ppermute | solution.py:19
  161.0 5.2 %collective-permute-start.29 = (f32[256,128]{1,0:T(8,128)S(1)}, f32[256,128]{1,0:T(8,128)S(1)}, u32[]{:S(2)}, u32[]{:S(2)}) collective-permute-start(f32[256,128]{1,0:T(8,128)S(1)} %get-tuple-element.128), channel_id=1, source_target_pairs={{0,1},{1,0},{2,3},{3,2},{4,5},{5,4},{6,7},{7,6},{8,9},{9,8},{10,11... | collective-permute-start | bytes 393224 | tf_op jit(solution)/shard_map/ppermute | solution.py:19
  166.2 10.1 %collective-permute-start.30 = (f32[512,128]{1,0:T(8,128)S(1)}, f32[512,128]{1,0:T(8,128)S(1)}, u32[]{:S(2)}, u32[]{:S(2)}) collective-permute-start(f32[512,128]{1,0:T(8,128)S(1)} %pad_maximum_fusion.13), channel_id=1, source_target_pairs={{0,1},{1,0},{2,3},{3,2},{4,5},{5,4},{6,7},{7,6},{8,9},{9,8},{10,11... | collective-permute-start | bytes 786440 | tf_op jit(solution)/shard_map/ppermute | solution.py:19
  167.4 8.9 %collective-permute-start.31 = (f32[512,128]{1,0:T(8,128)S(1)}, f32[512,128]{1,0:T(8,128)S(1)}, u32[]{:S(2)}, u32[]{:S(2)}) collective-permute-start(f32[512,128]{1,0:T(8,128)S(1)} %pad_maximum_fusion.14), channel_id=1, source_target_pairs={{0,2},{2,0},{1,3},{3,1},{4,6},{6,4},{5,7},{7,5},{8,10},{10,8},{9,1... | collective-permute-start | bytes 786440 | tf_op jit(solution)/shard_map/ppermute | solution.py:19
  167.5 8.8 %collective-permute-start.32 = (f32[16,256]{1,0:T(8,128)S(1)}, f32[16,256]{1,0:T(8,128)S(1)}, u32[]{:S(2)}, u32[]{:S(2)}) collective-permute-start(f32[16,256]{1,0:T(8,128)S(1)} %pad_maximum_fusion.26), channel_id=1, source_target_pairs={{0,8},{8,0},{1,9},{9,1},{2,10},{10,2},{3,11},{11,3},{4,12},{12,4},... | collective-permute-start | bytes 49160 | tf_op jit(solution)/shard_map/ppermute | solution.py:19
  176.5 6.2 %collective-permute-start.33 = (f32[1024,256]{1,0:T(8,128)S(1)}, f32[1024,256]{1,0:T(8,128)S(1)}, u32[]{:S(2)}, u32[]{:S(2)}) collective-permute-start(f32[1024,256]{1,0:T(8,128)S(1)} %pad_maximum_fusion.1), channel_id=1, source_target_pairs={{0,8},{8,0},{1,9},{9,1},{2,10},{10,2},{3,11},{11,3},{4,12},{12,4},... | collective-permute-start | bytes 3145736 | tf_op jit(solution)/shard_map/ppermute | solution.py:19
  196.1 4.7 %collective-permute-start.34 = (f32[128,256]{1,0:T(8,128)S(1)}, f32[128,256]{1,0:T(8,128)S(1)}, u32[]{:S(2)}, u32[]{:S(2)}) collective-permute-start(f32[128,256]{1,0:T(8,128)S(1)} %slice.357), channel_id=1, source_target_pairs={{0,16},{16,24},{1,17},{17,25},{2,18},{18,26},{3,19},{19,27},{4,20}... | collective-permute-start | bytes 393224 | tf_op jit(solution)/shard_map/ppermute | solution.py:192
  196.8 6.0 %collective-permute-start.35 = (f32[128,256]{1,0:T(8,128)S(1)}, f32[128,256]{1,0:T(8,128)S(1)}, u32[]{:S(2)}, u32[]{:S(2)}) collective-permute-start(f32[128,256]{1,0:T(8,128)S(1)} %slice.357), channel_id=1, source_target_pairs={{8,16},{9,17},{10,18},{11,19},{12,20},{13,21},{14,22},{15,23}} | collective-permute-start | bytes 393224 | tf_op jit(solution)/shard_map/ppermute | solution.py:193
  (12 other events, 58.0 us)

commit v2 on v1

--- a/solution.py
+++ b/solution.py
@@ -21,6 +21,10 @@
 
 def together(*values):
     return lax.optimization_barrier(values)
+
+
+def in_lanes(column, lanes):
+    return lax.optimization_barrier(jnp.broadcast_to(column, (column.shape[0], lanes)))
 
 
 def contract_rows(left, right):
@@ -69,7 +73,7 @@
     ]
 
 
-def base_kernel(bits, points, near, far, squares, near_part, far_part, sems, out_sems):
+def base_kernel(bits, points, near, far, near_part, far_part, squares, sems, out_sems):
     parts = near_part, far_part
     copies = column_copies(points, 0, parts, own_place(bits), sems)
     for copy in copies:
@@ -127,9 +131,21 @@
     blocks = 2 ** (1 + len(bits))
     if (width // blocks) % 128:
         near, far = reorder(points, bits)
-        return near, far, jnp.sum(points * points, axis=1, keepdims=True)
-    near, far, sums = arrange_call(base_kernel, points, rows, bits, {})(points)
-    return near, far, jnp.sum(sums, axis=1, keepdims=True)
+        return near, far, near, far, jnp.sum(points * points, axis=1, keepdims=True)
+    anywhere = pl.BlockSpec(memory_space=pl.ANY)
+    inside = pl.BlockSpec(memory_space=pltpu.VMEM)
+    whole = pltpu.HBM((rows + rows // 2, width // 2), points.dtype)
+    part = pltpu.VMEM((rows, width // 2), points.dtype)
+    *arrays, sums = pl.pallas_call(
+        functools.partial(base_kernel, bits),
+        out_shape=(whole, whole, part, part, pltpu.VMEM((rows, 128), points.dtype)),
+        in_specs=[anywhere],
+        out_specs=(anywhere, anywhere, inside, inside, inside),
+        scratch_shapes=[pltpu.SemaphoreType.DMA((blocks,)), pltpu.SemaphoreType.DMA((2,))],
+        compiler_params=pltpu.CompilerParams(vmem_limit_bytes=4 << 20),
+        name="base_rows",
+    )(pltpu.with_memory_space_constraint(points, pltpu.HBM))
+    return *arrays, jnp.sum(sums, axis=1, keepdims=True)
 
 
 def reorder(points, bits):
@@ -150,7 +166,7 @@
         extra = reorder(extra, bits)
         return tuple(jnp.concatenate(pair, axis=0) for pair in zip((near, far), extra))
     return arrange_call(extra_kernel, points, half, bits, {3: 0, 4: 1})(
-        points, first, second, near, far
+        pltpu.with_memory_space_constraint(points, pltpu.HBM), first, second, near, far
     )
 
 
@@ -159,15 +175,11 @@
     anywhere = pl.BlockSpec(memory_space=pl.ANY)
     shape = jax.ShapeDtypeStruct((rows + rows // 2, width // 2), points.dtype)
     part = pltpu.VMEM((count, width // 2), points.dtype)
-    shapes, specs = (shape, shape), (anywhere, anywhere)
-    if not aliases:
-        shapes += (jax.ShapeDtypeStruct((count, 128), points.dtype),)
-        specs += (pl.BlockSpec(memory_space=pltpu.VMEM),)
     return pl.pallas_call(
         functools.partial(kernel, bits),
-        out_shape=shapes,
-        in_specs=[anywhere] * (5 if aliases else 1),
-        out_specs=specs,
+        out_shape=(shape, shape),
+        in_specs=[anywhere] * 5,
+        out_specs=(anywhere, anywhere),
         scratch_shapes=[
             part,
             part,
@@ -314,8 +326,8 @@
     columns = jnp.sum(scaled, axis=0, keepdims=True)
     sums = [jnp.sum(scaled * squares, axis=0, keepdims=True), columns]
     if totals:
-        total = jnp.sum(columns, axis=1, keepdims=True)
-        sums.append(jnp.broadcast_to(total, columns.shape))
+        total = in_lanes(jnp.sum(scaled, axis=1, keepdims=True), columns.shape[1])
+        sums.append(jnp.sum(total, axis=0, keepdims=True))
     rest = PAD - len(sums)
     return scaled, jnp.concatenate([*sums, jnp.zeros((rest, columns.shape[1]))], axis=0)
 
@@ -338,7 +350,7 @@
 
         moved = move(points)
         mass = masses[:, None]
-        near, far, squares = arrange_base(points, bits)
+        near, far, near_base, far_base, squares = arrange_base(points, bits)
         lanes = lax.broadcasted_iota(jnp.int32, (rows, 128), 1)
         packed = jnp.concatenate(
             [log_factor, jnp.where(lanes < 64, mass, squares)], axis=1
@@ -348,8 +360,8 @@
         scaled, statistics = weigh(log_factor, mass, squares, True)
         stay_stats = jnp.where(group == 2, statistics, 0.0)
         statistics = jnp.where(group == 2, 0.0, statistics)
-        other = swap(contract_rows(far[:rows], scaled), "core")
-        held, other = together(contract_rows(near[:rows], scaled), other)
+        other = swap(contract_rows(far_base, scaled), "core")
+        held, other = together(contract_rows(near_base, scaled), other)
         crossing = jnp.where(
             source, held + other, jnp.where(second_core, held, other)
         )
@@ -383,8 +395,9 @@
                 squares * share - 2.0 * (cross / mass_total) + facing[0:1] / mass_total
             ) / marginal
             centred = gradient - jnp.mean(gradient, axis=1, keepdims=True)
-            largest = jnp.max(jnp.where(real, jnp.abs(centred), 0.0))
-            spread = jnp.full((devices, 128), largest, jnp.float32)
+            largest = jnp.max(jnp.where(real, jnp.abs(centred), 0.0), axis=1, keepdims=True)
+            largest = jnp.max(in_lanes(largest, 128), axis=0, keepdims=True)
+            spread = jnp.broadcast_to(largest, (devices, 128))
             largest = jnp.max(lax.all_to_all(spread, axes, 0, 0, tiled=True), axis=0)
             rate = jnp.tile(step_scale / (largest + 1e-06), rank // 128)
             logits = logits - rate[None, :] * gradient

time: 204 us -> 200 us (0.980)
  no operation moved by 1% of the time
where the time goes in v2:
time: 200 us; the launch traced here: 199 us
  starting transfers between devices  77.5 us (39%)
  waiting for transfers between devices  72.9 us (36%)
  matrix products  18.3 us (9%)
  blocking collectives  9.71 us (5%)
  other arithmetic  9.33 us (5%)
  Pallas kernels  5.49 us (3%)
  local copies, waits for them, and re-layouts  4.98 us (2%)
    ppermute x26, starting transfers between devices, swap(): return lax.ppermute(value, axis, [(0, 1), (1, 0)])  56 us
    ppermute x26, waiting for transfers between devices, swap(): return lax.ppermute(value, axis, [(0, 1), (1, 0)])  48.1 us
    ppermute x4, waiting for transfers between devices, across(): return lax.ppermute(value, ('side', axis), pairs)  16.2 us
    dot_general x4, matrix products, contract_rows(): lax.dot_general(left, right, (((0,), (0,)), ((), ())), precision=highest,...  9.91 us
    all_to_all x1, blocking collectives, steps(): largest = jnp.max(lax.all_to_all(spread, axes, 0, 0, tiled=True), axis=0)  9.71 us
    dot_general x4, matrix products, times(): jnp.dot(left, right, precision=highest, preferred_element_type=jnp.float32)  8.37 us
    all_to_all x1, starting transfers between devices, steps(): largest = jnp.max(lax.all_to_all(spread, axes, 0, 0, tiled=True), axis=0)  6.84 us
    all_to_all x1, waiting for transfers between devices, steps(): largest = jnp.max(lax.all_to_all(spread, axes, 0, 0, tiled=True), axis=0)  6.65 us
  transfers between devices with their start and end apart: 37, of which 24 were waited for; matrix products, arithmetic and copies ran while one was open for 7% of the time, Pallas kernels for 1%

profile of v2, /device:TPU:1, one launch (start us, length us, event | category | flops | bytes accessed | tf_op | source)
XLA Modules:
  0.0 199.1 jit_solution(7395809988667575387)
XLA Ops:
  0.0 3.1 %base_rows.1 = (f32[384,1024]{1,0:T(8,128)}, f32[384,1024]{1,0:T(8,128)}, f32[256,1024]{1,0:T(8,128)S(1)}, f32[256,1024]{1,0:T(8,128)S(1)}, f32[256,128]{1,0:T(8,128)S(1)}) custom-call(f32[256,2048]{1,0:T(8,128)} %points.3), custom_call_target="tpu_custom_call" | custom-call | tf_op jit(solution)/shard_map/base_rows/pallas_call | solution.py:139
  3.9 2.8 %convolution_bitcast_fusion = f32[1024,256]{1,0:T(8,128)} fusion(f32[256,256]{1,0:T(8,128)S(1)} %get-tuple-element.161, f32[256,1024]{1,0:T(8,128)S(1)} %get-tuple-element.78), kind=kOutput, calls=%fused_computation | convolution fusion | flops 805306368 | bytes 2359296 | tf_op jit(solution)/shard_map/dot_general | solution.py:31
  7.0 1.8 convolution_bitcast_fusion.1
  11.3 2.4 %collective-permute-start.3 = (f32[520,256]{1,0:T(8,128)S(1)}, f32[520,256]{1,0:T(8,128)S(1)}, u32[]{:S(2)}, u32[]{:S(2)}) collective-permute-start(f32[520,256]{1,0:T(8,128)S(1)} %get-tuple-element.81), channel_id=1, source_target_pairs={{0,1},{1,0},{2,3},{3,2},{4,5},{5,4},{6,7},{7,6},{8,9},{9,8},{10,11... | collective-permute-start | bytes 1597448 | tf_op jit(solution)/shard_map/ppermute | solution.py:19
  15.0 10.8 %collective-permute-done.3 = f32[520,256]{1,0:T(8,128)S(1)} collective-permute-done((f32[520,256]{1,0:T(8,128)S(1)}, f32[520,256]{1,0:T(8,128)S(1)}, u32[]{:S(2)}, u32[]{:S(2)}) %collective-permute-start.3) | collective-permute-done | bytes 532512 | tf_op jit(solution)/shard_map/ppermute | solution.py:19
  28.7 4.9 %collective-permute-done.5 = f32[264,256]{1,0:T(8,128)S(1)} collective-permute-done((f32[264,256]{1,0:T(8,128)S(1)}, f32[264,256]{1,0:T(8,128)S(1)}, u32[]{:S(2)}, u32[]{:S(2)}) %collective-permute-start.5) | collective-permute-done | bytes 270368 | tf_op jit(solution)/shard_map/ppermute | solution.py:19
  36.1 2.3 %collective-permute-start.8 = (f32[136,256]{1,0:T(8,128)S(1)}, f32[136,256]{1,0:T(8,128)S(1)}, u32[]{:S(2)}, u32[]{:S(2)}) collective-permute-start(f32[136,256]{1,0:T(8,128)S(1)} %get-tuple-element.90), channel_id=1, source_target_pairs={{0,20},{4,16},{16,4},{20,0},{1,21},{5,17},{17,5},{21,1},{2,22},{6,... | collective-permute-start | bytes 417800 | tf_op jit(solution)/shard_map/ppermute | solution.py:230
  38.8 9.8 %collective-permute-done.8 = f32[136,256]{1,0:T(8,128)S(1)} collective-permute-done((f32[136,256]{1,0:T(8,128)S(1)}, f32[136,256]{1,0:T(8,128)S(1)}, u32[]{:S(2)}, u32[]{:S(2)}) %collective-permute-start.8) | collective-permute-done | bytes 139296 | tf_op jit(solution)/shard_map/ppermute | solution.py:230
  48.7 2.1 %collective-permute-done.9 = f32[136,256]{1,0:T(8,128)S(1)} collective-permute-done((f32[136,256]{1,0:T(8,128)S(1)}, f32[136,256]{1,0:T(8,128)S(1)}, u32[]{:S(2)}, u32[]{:S(2)}) %collective-permute-start.9) | collective-permute-done | bytes 139296 | tf_op jit(solution)/shard_map/ppermute | solution.py:19
  56.0 3.3 %collective-permute-start.11 = (f32[8,256]{1,0:T(8,128)S(1)}, f32[8,256]{1,0:T(8,128)S(1)}, u32[]{:S(2)}, u32[]{:S(2)}) collective-permute-start(f32[8,256]{1,0:T(8,128)S(1)} %slice.317), channel_id=1, source_target_pairs={{0,16},{16,0},{1,17},{17,1},{2,18},{18,2},{3,19},{19,3},{4,20},{20... | collective-permute-start | bytes 24584 | tf_op jit(solution)/shard_map/ppermute | solution.py:19
  60.8 2.9 %collective-permute-start.12 = (f32[256,128]{1,0:T(8,128)S(1)}, f32[256,128]{1,0:T(8,128)S(1)}, u32[]{:S(2)}, u32[]{:S(2)}) collective-permute-start(f32[256,128]{1,0:T(8,128)S(1)} %get-tuple-element.98), channel_id=1, source_target_pairs={{0,2},{2,0},{1,3},{3,1},{4,6},{6,4},{5,7},{7,5},{8,10},{10,8},{9,1... | collective-permute-start | bytes 393224 | tf_op jit(solution)/shard_map/ppermute | solution.py:19
  64.1 2.4 %collective-permute-done.12 = f32[256,128]{1,0:T(8,128)S(1)} collective-permute-done((f32[256,128]{1,0:T(8,128)S(1)}, f32[256,128]{1,0:T(8,128)S(1)}, u32[]{:S(2)}, u32[]{:S(2)}) %collective-permute-start.12) | collective-permute-done | bytes 131104 | tf_op jit(solution)/shard_map/ppermute | solution.py:19
  68.7 22.2 %collective-permute-start.16 = (f32[16,256]{1,0:T(8,128)S(1)}, f32[16,256]{1,0:T(8,128)S(1)}, u32[]{:S(2)}, u32[]{:S(2)}) collective-permute-start(f32[16,256]{1,0:T(8,128)S(1)} %pad_maximum_fusion.25), channel_id=1, source_target_pairs={{0,8},{8,0},{1,9},{9,1},{2,10},{10,2},{3,11},{11,3},{4,12},{12,4},... | collective-permute-start | bytes 49160 | tf_op jit(solution)/shard_map/ppermute | solution.py:19
  94.9 3.9 %collective-permute-start.19 = (f32[1024,256]{1,0:T(8,128)}, f32[1024,256]{1,0:T(8,128)}, u32[]{:S(2)}, u32[]{:S(2)}) collective-permute-start(f32[1024,256]{1,0:T(8,128)} %pad_maximum_fusion), channel_id=1, source_target_pairs={{0,8},{8,0},{1,9},{9,1},{2,10},{10,2},{3,11},{11,3},{4,12},{12,4},... | collective-permute-start | bytes 3145736 | tf_op jit(solution)/shard_map/ppermute | solution.py:19
  100.6 2.4 %shard_map.37 = (f32[384,1024]{1,0:T(8,128)}, f32[384,1024]{1,0:T(8,128)}) custom-call(f32[256,2048]{1,0:T(8,128)} %points.3, f32[128,2048]{1,0:T(8,128)} %collective-permute-done.17.first, f32[128,2048]{1,0:T(8,128)} %copy-done.4, f32[384,1024]{1,0:T(8,128)} %get-tuple-element.109.near_in, ...), custom_call_target="tpu_custom_call", output_to_operand_aliasing={{0}: (3, {}), {1}: (4, {})} | custom-call | tf_op jit(solution)/shard_map/pallas_call | solution.py:168
  103.0 2.9 %fusion.23 = f32[384,256]{1,0:T(8,128)S(1)} fusion(f32[384,1024]{1,0:T(8,128)} %get-tuple-element.111, f32[1024,128]{1,0:T(8,128)S(1)} %bitcast.53, f32[512,128]{1,0:T(8,128)S(1)} %collective-permute-done.14, f32[512,128]{1,0:T(8,128)S(1)} %pad_maximum_fusion.11), kind=kOutput, calls=%fused_computation.117 | convolution fusion | flops 1208483840 | bytes 3014656 | tf_op jit(solution)/shard_map/dot_general | solution.py:41
  106.0 2.6 %fusion.35 = f32[384,256]{1,0:T(8,128)S(1)} fusion(f32[384,1024]{1,0:T(8,128)S(1)} %copy-done.1, f32[1024,256]{1,0:T(8,128)} %collective-permute-done.19), kind=kOutput, calls=%fused_computation.129 | convolution fusion | flops 1207959552 | bytes 3014656 | tf_op jit(solution)/shard_map/dot_general | solution.py:41
  110.0 6.8 %all-to-all-start = ((f32[32,1,128]{2,1,0:T(1,128)}), f32[32,1,128]{2,1,0:T(1,128)S(1)}, u32[]{:S(2)}, u32[]{:S(2)}) async-start(f32[32,1,128]{2,1,0:T(1,128)} %broadcast_in_dim.122), calls=%async_computation | async-start | bytes 32768 | tf_op jit(solution)/shard_map/all_to_all | solution.py:401
  117.0 6.6 %all-to-all-done = f32[32,1,128]{2,1,0:T(1,128)S(1)} async-done(((f32[32,1,128]{2,1,0:T(1,128)}), f32[32,1,128]{2,1,0:T(1,128)S(1)}, u32[]{:S(2)}, u32[]{:S(2)}) %all-to-all-start) | async-done | bytes 16416 | tf_op jit(solution)/shard_map/all_to_all | solution.py:401
  124.4 2.6 %fusion.37 = f32[1024,256]{1,0:T(8,128)S(1)} fusion(f32[384,1024]{1,0:T(8,128)S(1)} %copy-done.1, f32[384,256]{1,0:T(8,128)S(1)} %get-tuple-element.154), kind=kOutput, calls=%fused_computation.131 | convolution fusion | flops 1207959552 | bytes 3014656 | tf_op jit(solution)/shard_map/dot_general | solution.py:31
  127.9 2.6 %fusion.36 = f32[1024,256]{1,0:T(8,128)S(1)} fusion(f32[384,1024]{1,0:T(8,128)S(1)} %copy-done, f32[384,256]{1,0:T(8,128)S(1)} %get-tuple-element.154), kind=kOutput, calls=%fused_computation.130 | convolution fusion | flops 1207959552 | bytes 3014656 | tf_op jit(solution)/shard_map/dot_general | solution.py:31
  131.6 7.3 %collective-permute-done.21 = f32[520,128]{1,0:T(8,128)S(1)} collective-permute-done((f32[520,128]{1,0:T(8,128)S(1)}, f32[520,128]{1,0:T(8,128)S(1)}, u32[]{:S(2)}, u32[]{:S(2)}) %collective-permute-start.21) | collective-permute-done | bytes 266272 | tf_op jit(solution)/shard_map/ppermute | solution.py:19
  140.6 2.5 %collective-permute-done.23 = f32[264,128]{1,0:T(8,128)S(1)} collective-permute-done((f32[264,128]{1,0:T(8,128)S(1)}, f32[264,128]{1,0:T(8,128)S(1)}, u32[]{:S(2)}, u32[]{:S(2)}) %collective-permute-start.23) | collective-permute-done | bytes 135200 | tf_op jit(solution)/shard_map/ppermute | solution.py:19
  145.3 2.4 %collective-permute-done.25 = f32[136,256]{1,0:T(8,128)S(1)} collective-permute-done((f32[136,256]{1,0:T(8,128)S(1)}, f32[136,256]{1,0:T(8,128)S(1)}, u32[]{:S(2)}, u32[]{:S(2)}) %collective-permute-start.25) | collective-permute-done | bytes 139296 | tf_op jit(solution)/shard_map/ppermute | solution.py:230
  147.7 3.6 %collective-permute-done.26 = f32[136,256]{1,0:T(8,128)S(1)} collective-permute-done((f32[136,256]{1,0:T(8,128)S(1)}, f32[136,256]{1,0:T(8,128)S(1)}, u32[]{:S(2)}, u32[]{:S(2)}) %collective-permute-start.26) | collective-permute-done | bytes 139296 | tf_op jit(solution)/shard_map/ppermute | solution.py:230
  151.4 5.9 %collective-permute-done.27 = f32[136,256]{1,0:T(8,128)S(1)} collective-permute-done((f32[136,256]{1,0:T(8,128)S(1)}, f32[136,256]{1,0:T(8,128)S(1)}, u32[]{:S(2)}, u32[]{:S(2)}) %collective-permute-start.27) | collective-permute-done | bytes 139296 | tf_op jit(solution)/shard_map/ppermute | solution.py:19
  158.7 4.0 %collective-permute-done.28 = f32[256,128]{1,0:T(8,128)S(1)} collective-permute-done((f32[256,128]{1,0:T(8,128)S(1)}, f32[256,128]{1,0:T(8,128)S(1)}, u32[]{:S(2)}, u32[]{:S(2)}) %collective-permute-start.28) | collective-permute-done | bytes 131104 | tf_op jit(solution)/shard_map/ppermute | solution.py:19
  164.0 8.0 %collective-permute-start.32 = (f32[16,256]{1,0:T(8,128)S(1)}, f32[16,256]{1,0:T(8,128)S(1)}, u32[]{:S(2)}, u32[]{:S(2)}) collective-permute-start(f32[16,256]{1,0:T(8,128)S(1)} %pad_maximum_fusion.26), channel_id=1, source_target_pairs={{0,8},{8,0},{1,9},{9,1},{2,10},{10,2},{3,11},{11,3},{4,12},{12,4},... | collective-permute-start | bytes 49160 | tf_op jit(solution)/shard_map/ppermute | solution.py:19
  173.0 3.9 %collective-permute-start.33 = (f32[1024,256]{1,0:T(8,128)S(1)}, f32[1024,256]{1,0:T(8,128)S(1)}, u32[]{:S(2)}, u32[]{:S(2)}) collective-permute-start(f32[1024,256]{1,0:T(8,128)S(1)} %pad_maximum_fusion.1), channel_id=1, source_target_pairs={{0,8},{8,0},{1,9},{9,1},{2,10},{10,2},{3,11},{11,3},{4,12},{12,4},... | collective-permute-start | bytes 3145736 | tf_op jit(solution)/shard_map/ppermute | solution.py:19
  181.3 9.7 %all_to_all.12 = f32[32,1,128]{2,1,0:T(1,128)S(1)} all-to-all(f32[32,1,128]{2,1,0:T(1,128)S(1)} %broadcast_in_dim.128), channel_id=1, replica_groups=mesh['side'=2,'core'=2,'bit2'=2,'bit1'=2,'bit0'=2] {'side','core','bit2'..., dimensions={0} | all-to-all | bytes 32768 | tf_op jit(solution)/shard_map/all_to_all | solution.py:401
  192.3 4.0 %collective-permute-start.35 = (f32[128,256]{1,0:T(8,128)S(1)}, f32[128,256]{1,0:T(8,128)S(1)}, u32[]{:S(2)}, u32[]{:S(2)}) collective-permute-start(f32[128,256]{1,0:T(8,128)S(1)} %slice.349), channel_id=1, source_target_pairs={{8,16},{9,17},{10,18},{11,19},{12,20},{13,21},{14,22},{15,23}} | collective-permute-start | bytes 393224 | tf_op jit(solution)/shard_map/ppermute | solution.py:205
  196.4 1.9 collective-permute-done.35
  (200 shorter events, 43.4 us)
Async XLA Ops:
  11.3 14.5 %collective-permute-start.3 = (f32[520,256]{1,0:T(8,128)S(1)}, f32[520,256]{1,0:T(8,128)S(1)}, u32[]{:S(2)}, u32[]{:S(2)}) collective-permute-start(f32[520,256]{1,0:T(8,128)S(1)} %get-tuple-element.81), channel_id=1, source_target_pairs={{0,1},{1,0},{2,3},{3,2},{4,5},{5,4},{6,7},{7,6},{8,9},{9,8},{10,11... | collective-permute-start | bytes 1597448 | tf_op jit(solution)/shard_map/ppermute | solution.py:19
  13.7 13.0 %collective-permute-start.4 = (f32[520,256]{1,0:T(8,128)S(1)}, f32[520,256]{1,0:T(8,128)S(1)}, u32[]{:S(2)}, u32[]{:S(2)}) collective-permute-start(f32[520,256]{1,0:T(8,128)S(1)} %get-tuple-element.82), channel_id=1, source_target_pairs={{0,2},{2,0},{1,3},{3,1},{4,6},{6,4},{5,7},{7,5},{8,10},{10,8},{9,1... | collective-permute-start | bytes 1597448 | tf_op jit(solution)/shard_map/ppermute | solution.py:19
  27.0 6.6 %collective-permute-start.5 = (f32[264,256]{1,0:T(8,128)S(1)}, f32[264,256]{1,0:T(8,128)S(1)}, u32[]{:S(2)}, u32[]{:S(2)}) collective-permute-start(f32[264,256]{1,0:T(8,128)S(1)} %pad_maximum_fusion.7), channel_id=1, source_target_pairs={{0,2},{2,0},{1,3},{3,1},{4,6},{6,4},{5,7},{7,5},{8,10},{10,8},{9,1... | collective-permute-start | bytes 811016 | tf_op jit(solution)/shard_map/ppermute | solution.py:19
  28.4 6.2 %collective-permute-start.6 = (f32[264,256]{1,0:T(8,128)S(1)}, f32[264,256]{1,0:T(8,128)S(1)}, u32[]{:S(2)}, u32[]{:S(2)}) collective-permute-start(f32[264,256]{1,0:T(8,128)S(1)} %pad_maximum_fusion.8), channel_id=1, source_target_pairs={{0,1},{1,0},{2,3},{3,2},{4,5},{5,4},{6,7},{7,6},{8,9},{9,8},{10,11... | collective-permute-start | bytes 811016 | tf_op jit(solution)/shard_map/ppermute | solution.py:19
  36.1 12.5 %collective-permute-start.8 = (f32[136,256]{1,0:T(8,128)S(1)}, f32[136,256]{1,0:T(8,128)S(1)}, u32[]{:S(2)}, u32[]{:S(2)}) collective-permute-start(f32[136,256]{1,0:T(8,128)S(1)} %get-tuple-element.90), channel_id=1, source_target_pairs={{0,20},{4,16},{16,4},{20,0},{1,21},{5,17},{17,5},{21,1},{2,22},{6,... | collective-permute-start | bytes 417800 | tf_op jit(solution)/shard_map/ppermute | solution.py:230
  38.4 12.3 %collective-permute-start.9 = (f32[136,256]{1,0:T(8,128)S(1)}, f32[136,256]{1,0:T(8,128)S(1)}, u32[]{:S(2)}, u32[]{:S(2)}) collective-permute-start(f32[136,256]{1,0:T(8,128)S(1)} %pad_maximum_fusion.19), channel_id=1, source_target_pairs={{0,4},{4,0},{1,5},{5,1},{2,6},{6,2},{3,7},{7,3},{8,12},{12,8},{9,1... | collective-permute-start | bytes 417800 | tf_op jit(solution)/shard_map/ppermute | solution.py:19
  50.8 9.9 %collective-permute-start.10 = (f32[128,256]{1,0:T(8,128)S(1)}, f32[128,256]{1,0:T(8,128)S(1)}, u32[]{:S(2)}, u32[]{:S(2)}) collective-permute-start(f32[128,256]{1,0:T(8,128)S(1)} %slice.316), channel_id=1, source_target_pairs={{0,4},{4,0},{1,5},{5,1},{2,6},{6,2},{3,7},{7,3},{8,12},{12,8},{9,1... | collective-permute-start | bytes 393224 | tf_op jit(solution)/shard_map/ppermute | solution.py:19
  52.0 47.6 %collective-permute-start.17 = (f32[128,2048]{1,0:T(8,128)}, f32[128,2048]{1,0:T(8,128)}, u32[]{:S(2)}, u32[]{:S(2)}) collective-permute-start(f32[128,2048]{1,0:T(8,128)} %slice.259), channel_id=1, source_target_pairs={{16,0},{24,16},{17,1},{25,17},{18,2},{26,18},{19,3},{27,19},{20,4}... | collective-permute-start | bytes 3145736 | tf_op jit(solution)/shard_map/ppermute | solution.py:196
  54.7 44.9 %collective-permute-start.18 = (f32[128,2048]{1,0:T(8,128)}, f32[128,2048]{1,0:T(8,128)S(1)}, u32[]{:S(2)}, u32[]{:S(2)}) collective-permute-start(f32[128,2048]{1,0:T(8,128)} %slice.260), channel_id=1, source_target_pairs={{16,8},{17,9},{18,10},{19,11},{20,12},{21,13},{22,14},{23,15}} | collective-permute-start | bytes 3145736 | tf_op jit(solution)/shard_map/ppermute | solution.py:197
  56.0 4.8 %collective-permute-start.11 = (f32[8,256]{1,0:T(8,128)S(1)}, f32[8,256]{1,0:T(8,128)S(1)}, u32[]{:S(2)}, u32[]{:S(2)}) collective-permute-start(f32[8,256]{1,0:T(8,128)S(1)} %slice.317), channel_id=1, source_target_pairs={{0,16},{16,0},{1,17},{17,1},{2,18},{18,2},{3,19},{19,3},{4,20},{20... | collective-permute-start | bytes 24584 | tf_op jit(solution)/shard_map/ppermute | solution.py:19
  60.8 5.7 %collective-permute-start.12 = (f32[256,128]{1,0:T(8,128)S(1)}, f32[256,128]{1,0:T(8,128)S(1)}, u32[]{:S(2)}, u32[]{:S(2)}) collective-permute-start(f32[256,128]{1,0:T(8,128)S(1)} %get-tuple-element.98), channel_id=1, source_target_pairs={{0,2},{2,0},{1,3},{3,1},{4,6},{6,4},{5,7},{7,5},{8,10},{10,8},{9,1... | collective-permute-start | bytes 393224 | tf_op jit(solution)/shard_map/ppermute | solution.py:19
  63.7 4.2 %collective-permute-start.13 = (f32[256,128]{1,0:T(8,128)S(1)}, f32[256,128]{1,0:T(8,128)S(1)}, u32[]{:S(2)}, u32[]{:S(2)}) collective-permute-start(f32[256,128]{1,0:T(8,128)S(1)} %get-tuple-element.99), channel_id=1, source_target_pairs={{0,1},{1,0},{2,3},{3,2},{4,5},{5,4},{6,7},{7,6},{8,9},{9,8},{10,11... | collective-permute-start | bytes 393224 | tf_op jit(solution)/shard_map/ppermute | solution.py:19
  68.0 25.0 %collective-permute-start.14 = (f32[512,128]{1,0:T(8,128)S(1)}, f32[512,128]{1,0:T(8,128)S(1)}, u32[]{:S(2)}, u32[]{:S(2)}) collective-permute-start(f32[512,128]{1,0:T(8,128)S(1)} %pad_maximum_fusion.11), channel_id=1, source_target_pairs={{0,1},{1,0},{2,3},{3,2},{4,5},{5,4},{6,7},{7,6},{8,9},{9,8},{10,11... | collective-permute-start | bytes 786440 | tf_op jit(solution)/shard_map/ppermute | solution.py:19
  68.4 25.3 %collective-permute-start.15 = (f32[512,128]{1,0:T(8,128)S(1)}, f32[512,128]{1,0:T(8,128)S(1)}, u32[]{:S(2)}, u32[]{:S(2)}) collective-permute-start(f32[512,128]{1,0:T(8,128)S(1)} %pad_maximum_fusion.12), channel_id=1, source_target_pairs={{0,2},{2,0},{1,3},{3,1},{4,6},{6,4},{5,7},{7,5},{8,10},{10,8},{9,1... | collective-permute-start | bytes 786440 | tf_op jit(solution)/shard_map/ppermute | solution.py:19
  68.7 23.0 %collective-permute-start.16 = (f32[16,256]{1,0:T(8,128)S(1)}, f32[16,256]{1,0:T(8,128)S(1)}, u32[]{:S(2)}, u32[]{:S(2)}) collective-permute-start(f32[16,256]{1,0:T(8,128)S(1)} %pad_maximum_fusion.25), channel_id=1, source_target_pairs={{0,8},{8,0},{1,9},{9,1},{2,10},{10,2},{3,11},{11,3},{4,12},{12,4},... | collective-permute-start | bytes 49160 | tf_op jit(solution)/shard_map/ppermute | solution.py:19
  91.7 7.7 %collective-permute-start = (f32[128,384]{1,0:T(8,128)S(1)}, f32[128,384]{1,0:T(8,128)S(1)}, u32[]{:S(2)}, u32[]{:S(2)}) collective-permute-start(f32[128,384]{1,0:T(8,128)S(1)} %slice.229), channel_id=1, source_target_pairs={{16,8},{17,9},{18,10},{19,11},{20,12},{21,13},{22,14},{23,15}} | collective-permute-start | bytes 589832 | tf_op jit(solution)/shard_map/ppermute | solution.py:197
  93.0 6.4 %collective-permute-start.1 = (f32[128,384]{1,0:T(8,128)}, f32[128,384]{1,0:T(8,128)S(1)}, u32[]{:S(2)}, u32[]{:S(2)}) collective-permute-start(f32[128,384]{1,0:T(8,128)} %fusion.3), channel_id=1, source_target_pairs={{16,0},{24,16},{17,1},{25,17},{18,2},{26,18},{19,3},{27,19},{20,4}... | collective-permute-start | bytes 589832 | tf_op jit(solution)/shard_map/ppermute | solution.py:196
  94.9 11.1 %collective-permute-start.19 = (f32[1024,256]{1,0:T(8,128)}, f32[1024,256]{1,0:T(8,128)}, u32[]{:S(2)}, u32[]{:S(2)}) collective-permute-start(f32[1024,256]{1,0:T(8,128)} %pad_maximum_fusion), channel_id=1, source_target_pairs={{0,8},{8,0},{1,9},{9,1},{2,10},{10,2},{3,11},{11,3},{4,12},{12,4},... | collective-permute-start | bytes 3145736 | tf_op jit(solution)/shard_map/ppermute | solution.py:19
  110.0 13.6 %all-to-all-start = ((f32[32,1,128]{2,1,0:T(1,128)}), f32[32,1,128]{2,1,0:T(1,128)S(1)}, u32[]{:S(2)}, u32[]{:S(2)}) async-start(f32[32,1,128]{2,1,0:T(1,128)} %broadcast_in_dim.122), calls=%async_computation | async-start | bytes 32768 | tf_op jit(solution)/shard_map/all_to_all | solution.py:401
  130.9 8.0 %collective-permute-start.21 = (f32[520,128]{1,0:T(8,128)S(1)}, f32[520,128]{1,0:T(8,128)S(1)}, u32[]{:S(2)}, u32[]{:S(2)}) collective-permute-start(f32[520,128]{1,0:T(8,128)S(1)} %pad_maximum_fusion.9), channel_id=1, source_target_pairs={{0,1},{1,0},{2,3},{3,2},{4,5},{5,4},{6,7},{7,6},{8,9},{9,8},{10,11... | collective-permute-start | bytes 798728 | tf_op jit(solution)/shard_map/ppermute | solution.py:19
  131.3 7.7 %collective-permute-start.22 = (f32[520,128]{1,0:T(8,128)S(1)}, f32[520,128]{1,0:T(8,128)S(1)}, u32[]{:S(2)}, u32[]{:S(2)}) collective-permute-start(f32[520,128]{1,0:T(8,128)S(1)} %pad_maximum_fusion.10), channel_id=1, source_target_pairs={{0,2},{2,0},{1,3},{3,1},{4,6},{6,4},{5,7},{7,5},{8,10},{10,8},{9,1... | collective-permute-start | bytes 798728 | tf_op jit(solution)/shard_map/ppermute | solution.py:19
  139.4 4.2 %collective-permute-start.24 = (f32[264,128]{1,0:T(8,128)S(1)}, f32[264,128]{1,0:T(8,128)S(1)}, u32[]{:S(2)}, u32[]{:S(2)}) collective-permute-start(f32[264,128]{1,0:T(8,128)S(1)} %pad_maximum_fusion.23), channel_id=1, source_target_pairs={{0,1},{1,0},{2,3},{3,2},{4,5},{5,4},{6,7},{7,6},{8,9},{9,8},{10,11... | collective-permute-start | bytes 405512 | tf_op jit(solution)/shard_map/ppermute | solution.py:19
  144.1 7.2 %collective-permute-start.26 = (f32[136,256]{1,0:T(8,128)S(1)}, f32[136,256]{1,0:T(8,128)S(1)}, u32[]{:S(2)}, u32[]{:S(2)}) collective-permute-start(f32[136,256]{1,0:T(8,128)S(1)} %get-tuple-element.128), channel_id=1, source_target_pairs={{0,20},{4,16},{16,4},{20,0},{1,21},{5,17},{17,5},{21,1},{2,22},{6,... | collective-permute-start | bytes 417800 | tf_op jit(solution)/shard_map/ppermute | solution.py:230
  151.3 6.0 %collective-permute-start.27 = (f32[136,256]{1,0:T(8,128)S(1)}, f32[136,256]{1,0:T(8,128)S(1)}, u32[]{:S(2)}, u32[]{:S(2)}) collective-permute-start(f32[136,256]{1,0:T(8,128)S(1)} %fusion.11), channel_id=1, source_target_pairs={{0,4},{4,0},{1,5},{5,1},{2,6},{6,2},{3,7},{7,3},{8,12},{12,8},{9,1... | collective-permute-start | bytes 417800 | tf_op jit(solution)/shard_map/ppermute | solution.py:19
  157.4 5.3 %collective-permute-start.28 = (f32[256,128]{1,0:T(8,128)S(1)}, f32[256,128]{1,0:T(8,128)S(1)}, u32[]{:S(2)}, u32[]{:S(2)}) collective-permute-start(f32[256,128]{1,0:T(8,128)S(1)} %get-tuple-element.131), channel_id=1, source_target_pairs={{0,2},{2,0},{1,3},{3,1},{4,6},{6,4},{5,7},{7,5},{8,10},{10,8},{9,1... | collective-permute-start | bytes 393224 | tf_op jit(solution)/shard_map/ppermute | solution.py:19
  157.5 5.2 %collective-permute-start.29 = (f32[256,128]{1,0:T(8,128)S(1)}, f32[256,128]{1,0:T(8,128)S(1)}, u32[]{:S(2)}, u32[]{:S(2)}) collective-permute-start(f32[256,128]{1,0:T(8,128)S(1)} %get-tuple-element.132), channel_id=1, source_target_pairs={{0,1},{1,0},{2,3},{3,2},{4,5},{5,4},{6,7},{7,6},{8,9},{9,8},{10,11... | collective-permute-start | bytes 393224 | tf_op jit(solution)/shard_map/ppermute | solution.py:19
  162.7 10.1 %collective-permute-start.30 = (f32[512,128]{1,0:T(8,128)S(1)}, f32[512,128]{1,0:T(8,128)S(1)}, u32[]{:S(2)}, u32[]{:S(2)}) collective-permute-start(f32[512,128]{1,0:T(8,128)S(1)} %pad_maximum_fusion.13), channel_id=1, source_target_pairs={{0,1},{1,0},{2,3},{3,2},{4,5},{5,4},{6,7},{7,6},{8,9},{9,8},{10,11... | collective-permute-start | bytes 786440 | tf_op jit(solution)/shard_map/ppermute | solution.py:19
  163.9 8.9 %collective-permute-start.31 = (f32[512,128]{1,0:T(8,128)S(1)}, f32[512,128]{1,0:T(8,128)S(1)}, u32[]{:S(2)}, u32[]{:S(2)}) collective-permute-start(f32[512,128]{1,0:T(8,128)S(1)} %pad_maximum_fusion.14), channel_id=1, source_target_pairs={{0,2},{2,0},{1,3},{3,1},{4,6},{6,4},{5,7},{7,5},{8,10},{10,8},{9,1... | collective-permute-start | bytes 786440 | tf_op jit(solution)/shard_map/ppermute | solution.py:19
  164.0 8.8 %collective-permute-start.32 = (f32[16,256]{1,0:T(8,128)S(1)}, f32[16,256]{1,0:T(8,128)S(1)}, u32[]{:S(2)}, u32[]{:S(2)}) collective-permute-start(f32[16,256]{1,0:T(8,128)S(1)} %pad_maximum_fusion.26), channel_id=1, source_target_pairs={{0,8},{8,0},{1,9},{9,1},{2,10},{10,2},{3,11},{11,3},{4,12},{12,4},... | collective-permute-start | bytes 49160 | tf_op jit(solution)/shard_map/ppermute | solution.py:19
  173.0 6.2 %collective-permute-start.33 = (f32[1024,256]{1,0:T(8,128)S(1)}, f32[1024,256]{1,0:T(8,128)S(1)}, u32[]{:S(2)}, u32[]{:S(2)}) collective-permute-start(f32[1024,256]{1,0:T(8,128)S(1)} %pad_maximum_fusion.1), channel_id=1, source_target_pairs={{0,8},{8,0},{1,9},{9,1},{2,10},{10,2},{3,11},{11,3},{4,12},{12,4},... | collective-permute-start | bytes 3145736 | tf_op jit(solution)/shard_map/ppermute | solution.py:19
  191.7 4.7 %collective-permute-start.34 = (f32[128,256]{1,0:T(8,128)S(1)}, f32[128,256]{1,0:T(8,128)S(1)}, u32[]{:S(2)}, u32[]{:S(2)}) collective-permute-start(f32[128,256]{1,0:T(8,128)S(1)} %slice.349), channel_id=1, source_target_pairs={{0,16},{16,24},{1,17},{17,25},{2,18},{18,26},{3,19},{19,27},{4,20}... | collective-permute-start | bytes 393224 | tf_op jit(solution)/shard_map/ppermute | solution.py:204
  192.3 6.0 %collective-permute-start.35 = (f32[128,256]{1,0:T(8,128)S(1)}, f32[128,256]{1,0:T(8,128)S(1)}, u32[]{:S(2)}, u32[]{:S(2)}) collective-permute-start(f32[128,256]{1,0:T(8,128)S(1)} %slice.349), channel_id=1, source_target_pairs={{8,16},{9,17},{10,18},{11,19},{12,20},{13,21},{14,22},{15,23}} | collective-permute-start | bytes 393224 | tf_op jit(solution)/shard_map/ppermute | solution.py:205
  (17 other events, 136.2 us)

commit v3 on v2

--- a/solution.py
+++ b/solution.py
@@ -73,7 +73,7 @@
     ]
 
 
-def base_kernel(bits, points, near, far, near_part, far_part, squares, sems, out_sems):
+def base_kernel(bits, points, near, far, far_part, squares, near_part, sems, out_sems):
     parts = near_part, far_part
     copies = column_copies(points, 0, parts, own_place(bits), sems)
     for copy in copies:
@@ -131,17 +131,21 @@
     blocks = 2 ** (1 + len(bits))
     if (width // blocks) % 128:
         near, far = reorder(points, bits)
-        return near, far, near, far, jnp.sum(points * points, axis=1, keepdims=True)
+        return near, far, far, jnp.sum(points * points, axis=1, keepdims=True)
     anywhere = pl.BlockSpec(memory_space=pl.ANY)
     inside = pl.BlockSpec(memory_space=pltpu.VMEM)
     whole = pltpu.HBM((rows + rows // 2, width // 2), points.dtype)
     part = pltpu.VMEM((rows, width // 2), points.dtype)
     *arrays, sums = pl.pallas_call(
         functools.partial(base_kernel, bits),
-        out_shape=(whole, whole, part, part, pltpu.VMEM((rows, 128), points.dtype)),
+        out_shape=(whole, whole, part, pltpu.VMEM((rows, 128), points.dtype)),
         in_specs=[anywhere],
-        out_specs=(anywhere, anywhere, inside, inside, inside),
-        scratch_shapes=[pltpu.SemaphoreType.DMA((blocks,)), pltpu.SemaphoreType.DMA((2,))],
+        out_specs=(anywhere, anywhere, inside, inside),
+        scratch_shapes=[
+            part,
+            pltpu.SemaphoreType.DMA((blocks,)),
+            pltpu.SemaphoreType.DMA((2,)),
+        ],
         compiler_params=pltpu.CompilerParams(vmem_limit_bytes=4 << 20),
         name="base_rows",
     )(pltpu.with_memory_space_constraint(points, pltpu.HBM))
@@ -350,7 +354,7 @@
 
         moved = move(points)
         mass = masses[:, None]
-        near, far, near_base, far_base, squares = arrange_base(points, bits)
+        near, far, far_base, squares = arrange_base(points, bits)
         lanes = lax.broadcasted_iota(jnp.int32, (rows, 128), 1)
         packed = jnp.concatenate(
             [log_factor, jnp.where(lanes < 64, mass, squares)], axis=1
@@ -361,7 +365,7 @@
         stay_stats = jnp.where(group == 2, statistics, 0.0)
         statistics = jnp.where(group == 2, 0.0, statistics)
         other = swap(contract_rows(far_base, scaled), "core")
-        held, other = together(contract_rows(near_base, scaled), other)
+        held, other = together(contract_rows(near[:rows], scaled), other)
         crossing = jnp.where(
             source, held + other, jnp.where(second_core, held, other)
         )

time: 200 us -> 198 us (0.990)
  no operation moved by 1% of the time
where the time goes in v3:
time: 198 us
  starting transfers between devices  77.8 us (39%)
  waiting for transfers between devices  73.4 us (37%)
  matrix products  18.3 us (9%)
  blocking collectives  9.72 us (5%)
  other arithmetic  7.52 us (4%)
  Pallas kernels  5.49 us (3%)
  local copies, waits for them, and re-layouts  4.98 us (3%)
    ppermute x26, starting transfers between devices, swap(): return lax.ppermute(value, axis, [(0, 1), (1, 0)])  56 us
    ppermute x26, waiting for transfers between devices, swap(): return lax.ppermute(value, axis, [(0, 1), (1, 0)])  48.6 us
    ppermute x4, waiting for transfers between devices, across(): return lax.ppermute(value, ('side', axis), pairs)  16.2 us
    dot_general x4, matrix products, contract_rows(): lax.dot_general(left, right, (((0,), (0,)), ((), ())), precision=highest,...  9.92 us
    all_to_all x1, blocking collectives, steps(): largest = jnp.max(lax.all_to_all(spread, axes, 0, 0, tiled=True), axis=0)  9.72 us
    dot_general x4, matrix products, times(): jnp.dot(left, right, precision=highest, preferred_element_type=jnp.float32)  8.37 us
    all_to_all x1, starting transfers between devices, steps(): largest = jnp.max(lax.all_to_all(spread, axes, 0, 0, tiled=True), axis=0)  7.2 us
    all_to_all x1, waiting for transfers between devices, steps(): largest = jnp.max(lax.all_to_all(spread, axes, 0, 0, tiled=True), axis=0)  6.65 us
  transfers between devices with their start and end apart: 37, of which 24 were waited for; matrix products, arithmetic and copies ran while one was open for 7% of the time, Pallas kernels for 1%

profile of v3, /device:TPU:1, one launch (start us, length us, event | category | flops | bytes accessed | tf_op | source)
XLA Modules:
  0.0 198.1 jit_solution(4948097006703606723)
XLA Ops:
  0.0 3.1 %base_rows.1 = (f32[384,1024]{1,0:T(8,128)}, f32[384,1024]{1,0:T(8,128)}, f32[256,1024]{1,0:T(8,128)S(1)}, f32[256,128]{1,0:T(8,128)S(1)}) custom-call(f32[256,2048]{1,0:T(8,128)} %points.3), custom_call_target="tpu_custom_call" | custom-call | tf_op jit(solution)/shard_map/base_rows/pallas_call | solution.py:139
  3.9 2.8 %convolution_bitcast_fusion = f32[1024,256]{1,0:T(8,128)} fusion(f32[256,256]{1,0:T(8,128)S(1)} %get-tuple-element.159, f32[256,1024]{1,0:T(8,128)S(1)} %get-tuple-element.77), kind=kOutput, calls=%fused_computation | convolution fusion | flops 805306368 | bytes 2359296 | tf_op jit(solution)/shard_map/dot_general | solution.py:31
  7.0 1.8 convolution_bitcast_fusion.1
  9.9 2.4 %collective-permute-start.3 = (f32[520,256]{1,0:T(8,128)S(1)}, f32[520,256]{1,0:T(8,128)S(1)}, u32[]{:S(2)}, u32[]{:S(2)}) collective-permute-start(f32[520,256]{1,0:T(8,128)S(1)} %get-tuple-element.80), channel_id=1, source_target_pairs={{0,1},{1,0},{2,3},{3,2},{4,5},{5,4},{6,7},{7,6},{8,9},{9,8},{10,11... | collective-permute-start | bytes 1597448 | tf_op jit(solution)/shard_map/ppermute | solution.py:19
  13.6 10.8 %collective-permute-done.3 = f32[520,256]{1,0:T(8,128)S(1)} collective-permute-done((f32[520,256]{1,0:T(8,128)S(1)}, f32[520,256]{1,0:T(8,128)S(1)}, u32[]{:S(2)}, u32[]{:S(2)}) %collective-permute-start.3) | collective-permute-done | bytes 532512 | tf_op jit(solution)/shard_map/ppermute | solution.py:19
  27.4 4.9 %collective-permute-done.5 = f32[264,256]{1,0:T(8,128)S(1)} collective-permute-done((f32[264,256]{1,0:T(8,128)S(1)}, f32[264,256]{1,0:T(8,128)S(1)}, u32[]{:S(2)}, u32[]{:S(2)}) %collective-permute-start.5) | collective-permute-done | bytes 270368 | tf_op jit(solution)/shard_map/ppermute | solution.py:19
  35.4 2.3 %collective-permute-start.8 = (f32[136,256]{1,0:T(8,128)S(1)}, f32[136,256]{1,0:T(8,128)S(1)}, u32[]{:S(2)}, u32[]{:S(2)}) collective-permute-start(f32[136,256]{1,0:T(8,128)S(1)} %get-tuple-element.89), channel_id=1, source_target_pairs={{0,20},{4,16},{16,4},{20,0},{1,21},{5,17},{17,5},{21,1},{2,22},{6,... | collective-permute-start | bytes 417800 | tf_op jit(solution)/shard_map/ppermute | solution.py:234
  38.3 9.6 %collective-permute-done.8 = f32[136,256]{1,0:T(8,128)S(1)} collective-permute-done((f32[136,256]{1,0:T(8,128)S(1)}, f32[136,256]{1,0:T(8,128)S(1)}, u32[]{:S(2)}, u32[]{:S(2)}) %collective-permute-start.8) | collective-permute-done | bytes 139296 | tf_op jit(solution)/shard_map/ppermute | solution.py:234
  47.9 2.1 %collective-permute-done.9 = f32[136,256]{1,0:T(8,128)S(1)} collective-permute-done((f32[136,256]{1,0:T(8,128)S(1)}, f32[136,256]{1,0:T(8,128)S(1)}, u32[]{:S(2)}, u32[]{:S(2)}) %collective-permute-start.9) | collective-permute-done | bytes 139296 | tf_op jit(solution)/shard_map/ppermute | solution.py:19
  55.2 3.3 %collective-permute-start.11 = (f32[8,256]{1,0:T(8,128)S(1)}, f32[8,256]{1,0:T(8,128)S(1)}, u32[]{:S(2)}, u32[]{:S(2)}) collective-permute-start(f32[8,256]{1,0:T(8,128)S(1)} %slice.321), channel_id=1, source_target_pairs={{0,16},{16,0},{1,17},{17,1},{2,18},{18,2},{3,19},{19,3},{4,20},{20... | collective-permute-start | bytes 24584 | tf_op jit(solution)/shard_map/ppermute | solution.py:19
  60.0 2.9 %collective-permute-start.12 = (f32[256,128]{1,0:T(8,128)S(1)}, f32[256,128]{1,0:T(8,128)S(1)}, u32[]{:S(2)}, u32[]{:S(2)}) collective-permute-start(f32[256,128]{1,0:T(8,128)S(1)} %get-tuple-element.97), channel_id=1, source_target_pairs={{0,2},{2,0},{1,3},{3,1},{4,6},{6,4},{5,7},{7,5},{8,10},{10,8},{9,1... | collective-permute-start | bytes 393224 | tf_op jit(solution)/shard_map/ppermute | solution.py:19
  63.3 2.4 %collective-permute-done.12 = f32[256,128]{1,0:T(8,128)S(1)} collective-permute-done((f32[256,128]{1,0:T(8,128)S(1)}, f32[256,128]{1,0:T(8,128)S(1)}, u32[]{:S(2)}, u32[]{:S(2)}) %collective-permute-start.12) | collective-permute-done | bytes 131104 | tf_op jit(solution)/shard_map/ppermute | solution.py:19
  67.9 22.2 %collective-permute-start.16 = (f32[16,256]{1,0:T(8,128)S(1)}, f32[16,256]{1,0:T(8,128)S(1)}, u32[]{:S(2)}, u32[]{:S(2)}) collective-permute-start(f32[16,256]{1,0:T(8,128)S(1)} %pad_maximum_fusion.25), channel_id=1, source_target_pairs={{0,8},{8,0},{1,9},{9,1},{2,10},{10,2},{3,11},{11,3},{4,12},{12,4},... | collective-permute-start | bytes 49160 | tf_op jit(solution)/shard_map/ppermute | solution.py:19
  94.1 3.9 %collective-permute-start.19 = (f32[1024,256]{1,0:T(8,128)}, f32[1024,256]{1,0:T(8,128)}, u32[]{:S(2)}, u32[]{:S(2)}) collective-permute-start(f32[1024,256]{1,0:T(8,128)} %pad_maximum_fusion), channel_id=1, source_target_pairs={{0,8},{8,0},{1,9},{9,1},{2,10},{10,2},{3,11},{11,3},{4,12},{12,4},... | collective-permute-start | bytes 3145736 | tf_op jit(solution)/shard_map/ppermute | solution.py:19
  99.3 2.4 %shard_map.37 = (f32[384,1024]{1,0:T(8,128)}, f32[384,1024]{1,0:T(8,128)}) custom-call(f32[256,2048]{1,0:T(8,128)} %points.3, f32[128,2048]{1,0:T(8,128)} %collective-permute-done.17.first, f32[128,2048]{1,0:T(8,128)} %copy-done.5, f32[384,1024]{1,0:T(8,128)} %get-tuple-element.76.near_in, ...), custom_call_target="tpu_custom_call", output_to_operand_aliasing={{0}: (3, {}), {1}: (4, {})} | custom-call | tf_op jit(solution)/shard_map/pallas_call | solution.py:172
  101.7 2.9 %fusion.24 = f32[384,256]{1,0:T(8,128)S(1)} fusion(f32[384,1024]{1,0:T(8,128)} %get-tuple-element.109, f32[1024,128]{1,0:T(8,128)S(1)} %bitcast.52, f32[512,128]{1,0:T(8,128)S(1)} %collective-permute-done.14, f32[512,128]{1,0:T(8,128)S(1)} %pad_maximum_fusion.11), kind=kOutput, calls=%fused_computation.118 | convolution fusion | flops 1208483840 | bytes 3014656 | tf_op jit(solution)/shard_map/dot_general | solution.py:41
  104.6 2.6 %fusion.36 = f32[384,256]{1,0:T(8,128)S(1)} fusion(f32[384,1024]{1,0:T(8,128)S(1)} %copy-done.2, f32[1024,256]{1,0:T(8,128)} %collective-permute-done.19), kind=kOutput, calls=%fused_computation.130 | convolution fusion | flops 1207959552 | bytes 3014656 | tf_op jit(solution)/shard_map/dot_general | solution.py:41
  108.6 7.2 %all-to-all-start = ((f32[32,1,128]{2,1,0:T(1,128)}), f32[32,1,128]{2,1,0:T(1,128)S(1)}, u32[]{:S(2)}, u32[]{:S(2)}) async-start(f32[32,1,128]{2,1,0:T(1,128)} %broadcast_in_dim.122), calls=%async_computation | async-start | bytes 32768 | tf_op jit(solution)/shard_map/all_to_all | solution.py:405
  116.0 6.6 %all-to-all-done = f32[32,1,128]{2,1,0:T(1,128)S(1)} async-done(((f32[32,1,128]{2,1,0:T(1,128)}), f32[32,1,128]{2,1,0:T(1,128)S(1)}, u32[]{:S(2)}, u32[]{:S(2)}) %all-to-all-start) | async-done | bytes 16416 | tf_op jit(solution)/shard_map/all_to_all | solution.py:405
  123.4 2.6 %fusion.38 = f32[1024,256]{1,0:T(8,128)S(1)} fusion(f32[384,1024]{1,0:T(8,128)S(1)} %copy-done.2, f32[384,256]{1,0:T(8,128)S(1)} %get-tuple-element.152), kind=kOutput, calls=%fused_computation.132 | convolution fusion | flops 1207959552 | bytes 3014656 | tf_op jit(solution)/shard_map/dot_general | solution.py:31
  126.9 2.6 %fusion.37 = f32[1024,256]{1,0:T(8,128)S(1)} fusion(f32[384,1024]{1,0:T(8,128)S(1)} %copy-done.1, f32[384,256]{1,0:T(8,128)S(1)} %get-tuple-element.152), kind=kOutput, calls=%fused_computation.131 | convolution fusion | flops 1207959552 | bytes 3014656 | tf_op jit(solution)/shard_map/dot_general | solution.py:31
  130.6 7.3 %collective-permute-done.21 = f32[520,128]{1,0:T(8,128)S(1)} collective-permute-done((f32[520,128]{1,0:T(8,128)S(1)}, f32[520,128]{1,0:T(8,128)S(1)}, u32[]{:S(2)}, u32[]{:S(2)}) %collective-permute-start.21) | collective-permute-done | bytes 266272 | tf_op jit(solution)/shard_map/ppermute | solution.py:19
  139.6 2.5 %collective-permute-done.23 = f32[264,128]{1,0:T(8,128)S(1)} collective-permute-done((f32[264,128]{1,0:T(8,128)S(1)}, f32[264,128]{1,0:T(8,128)S(1)}, u32[]{:S(2)}, u32[]{:S(2)}) %collective-permute-start.23) | collective-permute-done | bytes 135200 | tf_op jit(solution)/shard_map/ppermute | solution.py:19
  144.3 2.4 %collective-permute-done.25 = f32[136,256]{1,0:T(8,128)S(1)} collective-permute-done((f32[136,256]{1,0:T(8,128)S(1)}, f32[136,256]{1,0:T(8,128)S(1)}, u32[]{:S(2)}, u32[]{:S(2)}) %collective-permute-start.25) | collective-permute-done | bytes 139296 | tf_op jit(solution)/shard_map/ppermute | solution.py:234
  146.7 3.6 %collective-permute-done.26 = f32[136,256]{1,0:T(8,128)S(1)} collective-permute-done((f32[136,256]{1,0:T(8,128)S(1)}, f32[136,256]{1,0:T(8,128)S(1)}, u32[]{:S(2)}, u32[]{:S(2)}) %collective-permute-start.26) | collective-permute-done | bytes 139296 | tf_op jit(solution)/shard_map/ppermute | solution.py:234
  150.4 5.9 %collective-permute-done.27 = f32[136,256]{1,0:T(8,128)S(1)} collective-permute-done((f32[136,256]{1,0:T(8,128)S(1)}, f32[136,256]{1,0:T(8,128)S(1)}, u32[]{:S(2)}, u32[]{:S(2)}) %collective-permute-start.27) | collective-permute-done | bytes 139296 | tf_op jit(solution)/shard_map/ppermute | solution.py:19
  157.7 4.0 %collective-permute-done.28 = f32[256,128]{1,0:T(8,128)S(1)} collective-permute-done((f32[256,128]{1,0:T(8,128)S(1)}, f32[256,128]{1,0:T(8,128)S(1)}, u32[]{:S(2)}, u32[]{:S(2)}) %collective-permute-start.28) | collective-permute-done | bytes 131104 | tf_op jit(solution)/shard_map/ppermute | solution.py:19
  163.0 8.0 %collective-permute-start.32 = (f32[16,256]{1,0:T(8,128)S(1)}, f32[16,256]{1,0:T(8,128)S(1)}, u32[]{:S(2)}, u32[]{:S(2)}) collective-permute-start(f32[16,256]{1,0:T(8,128)S(1)} %pad_maximum_fusion.26), channel_id=1, source_target_pairs={{0,8},{8,0},{1,9},{9,1},{2,10},{10,2},{3,11},{11,3},{4,12},{12,4},... | collective-permute-start | bytes 49160 | tf_op jit(solution)/shard_map/ppermute | solution.py:19
  172.0 3.9 %collective-permute-start.33 = (f32[1024,256]{1,0:T(8,128)S(1)}, f32[1024,256]{1,0:T(8,128)S(1)}, u32[]{:S(2)}, u32[]{:S(2)}) collective-permute-start(f32[1024,256]{1,0:T(8,128)S(1)} %pad_maximum_fusion.1), channel_id=1, source_target_pairs={{0,8},{8,0},{1,9},{9,1},{2,10},{10,2},{3,11},{11,3},{4,12},{12,4},... | collective-permute-start | bytes 3145736 | tf_op jit(solution)/shard_map/ppermute | solution.py:19
  180.3 9.7 %all_to_all.12 = f32[32,1,128]{2,1,0:T(1,128)S(1)} all-to-all(f32[32,1,128]{2,1,0:T(1,128)S(1)} %broadcast_in_dim.128), channel_id=1, replica_groups=mesh['side'=2,'core'=2,'bit2'=2,'bit1'=2,'bit0'=2] {'side','core','bit2'..., dimensions={0} | all-to-all | bytes 32768 | tf_op jit(solution)/shard_map/all_to_all | solution.py:405
  191.4 4.0 %collective-permute-start.35 = (f32[128,256]{1,0:T(8,128)S(1)}, f32[128,256]{1,0:T(8,128)S(1)}, u32[]{:S(2)}, u32[]{:S(2)}) collective-permute-start(f32[128,256]{1,0:T(8,128)S(1)} %slice.353), channel_id=1, source_target_pairs={{8,16},{9,17},{10,18},{11,19},{12,20},{13,21},{14,22},{15,23}} | collective-permute-start | bytes 393224 | tf_op jit(solution)/shard_map/ppermute | solution.py:209
  195.4 1.9 collective-permute-done.35
  (200 shorter events, 42.3 us)
Async XLA Ops:
  9.9 14.5 %collective-permute-start.3 = (f32[520,256]{1,0:T(8,128)S(1)}, f32[520,256]{1,0:T(8,128)S(1)}, u32[]{:S(2)}, u32[]{:S(2)}) collective-permute-start(f32[520,256]{1,0:T(8,128)S(1)} %get-tuple-element.80), channel_id=1, source_target_pairs={{0,1},{1,0},{2,3},{3,2},{4,5},{5,4},{6,7},{7,6},{8,9},{9,8},{10,11... | collective-permute-start | bytes 1597448 | tf_op jit(solution)/shard_map/ppermute | solution.py:19
  12.4 13.0 %collective-permute-start.4 = (f32[520,256]{1,0:T(8,128)S(1)}, f32[520,256]{1,0:T(8,128)S(1)}, u32[]{:S(2)}, u32[]{:S(2)}) collective-permute-start(f32[520,256]{1,0:T(8,128)S(1)} %get-tuple-element.81), channel_id=1, source_target_pairs={{0,2},{2,0},{1,3},{3,1},{4,6},{6,4},{5,7},{7,5},{8,10},{10,8},{9,1... | collective-permute-start | bytes 1597448 | tf_op jit(solution)/shard_map/ppermute | solution.py:19
  25.7 6.6 %collective-permute-start.5 = (f32[264,256]{1,0:T(8,128)S(1)}, f32[264,256]{1,0:T(8,128)S(1)}, u32[]{:S(2)}, u32[]{:S(2)}) collective-permute-start(f32[264,256]{1,0:T(8,128)S(1)} %pad_maximum_fusion.7), channel_id=1, source_target_pairs={{0,2},{2,0},{1,3},{3,1},{4,6},{6,4},{5,7},{7,5},{8,10},{10,8},{9,1... | collective-permute-start | bytes 811016 | tf_op jit(solution)/shard_map/ppermute | solution.py:19
  27.1 6.2 %collective-permute-start.6 = (f32[264,256]{1,0:T(8,128)S(1)}, f32[264,256]{1,0:T(8,128)S(1)}, u32[]{:S(2)}, u32[]{:S(2)}) collective-permute-start(f32[264,256]{1,0:T(8,128)S(1)} %pad_maximum_fusion.8), channel_id=1, source_target_pairs={{0,1},{1,0},{2,3},{3,2},{4,5},{5,4},{6,7},{7,6},{8,9},{9,8},{10,11... | collective-permute-start | bytes 811016 | tf_op jit(solution)/shard_map/ppermute | solution.py:19
  35.4 12.5 %collective-permute-start.8 = (f32[136,256]{1,0:T(8,128)S(1)}, f32[136,256]{1,0:T(8,128)S(1)}, u32[]{:S(2)}, u32[]{:S(2)}) collective-permute-start(f32[136,256]{1,0:T(8,128)S(1)} %get-tuple-element.89), channel_id=1, source_target_pairs={{0,20},{4,16},{16,4},{20,0},{1,21},{5,17},{17,5},{21,1},{2,22},{6,... | collective-permute-start | bytes 417800 | tf_op jit(solution)/shard_map/ppermute | solution.py:234
  37.7 12.3 %collective-permute-start.9 = (f32[136,256]{1,0:T(8,128)S(1)}, f32[136,256]{1,0:T(8,128)S(1)}, u32[]{:S(2)}, u32[]{:S(2)}) collective-permute-start(f32[136,256]{1,0:T(8,128)S(1)} %pad_maximum_fusion.19), channel_id=1, source_target_pairs={{0,4},{4,0},{1,5},{5,1},{2,6},{6,2},{3,7},{7,3},{8,12},{12,8},{9,1... | collective-permute-start | bytes 417800 | tf_op jit(solution)/shard_map/ppermute | solution.py:19
  50.1 9.9 %collective-permute-start.10 = (f32[128,256]{1,0:T(8,128)S(1)}, f32[128,256]{1,0:T(8,128)S(1)}, u32[]{:S(2)}, u32[]{:S(2)}) collective-permute-start(f32[128,256]{1,0:T(8,128)S(1)} %slice.320), channel_id=1, source_target_pairs={{0,4},{4,0},{1,5},{5,1},{2,6},{6,2},{3,7},{7,3},{8,12},{12,8},{9,1... | collective-permute-start | bytes 393224 | tf_op jit(solution)/shard_map/ppermute | solution.py:19
  51.2 47.0 %collective-permute-start.17 = (f32[128,2048]{1,0:T(8,128)}, f32[128,2048]{1,0:T(8,128)}, u32[]{:S(2)}, u32[]{:S(2)}) collective-permute-start(f32[128,2048]{1,0:T(8,128)} %slice.263), channel_id=1, source_target_pairs={{16,0},{24,16},{17,1},{25,17},{18,2},{26,18},{19,3},{27,19},{20,4}... | collective-permute-start | bytes 3145736 | tf_op jit(solution)/shard_map/ppermute | solution.py:200
  53.9 44.4 %collective-permute-start.18 = (f32[128,2048]{1,0:T(8,128)}, f32[128,2048]{1,0:T(8,128)S(1)}, u32[]{:S(2)}, u32[]{:S(2)}) collective-permute-start(f32[128,2048]{1,0:T(8,128)} %slice.264), channel_id=1, source_target_pairs={{16,8},{17,9},{18,10},{19,11},{20,12},{21,13},{22,14},{23,15}} | collective-permute-start | bytes 3145736 | tf_op jit(solution)/shard_map/ppermute | solution.py:201
  55.2 4.8 %collective-permute-start.11 = (f32[8,256]{1,0:T(8,128)S(1)}, f32[8,256]{1,0:T(8,128)S(1)}, u32[]{:S(2)}, u32[]{:S(2)}) collective-permute-start(f32[8,256]{1,0:T(8,128)S(1)} %slice.321), channel_id=1, source_target_pairs={{0,16},{16,0},{1,17},{17,1},{2,18},{18,2},{3,19},{19,3},{4,20},{20... | collective-permute-start | bytes 24584 | tf_op jit(solution)/shard_map/ppermute | solution.py:19
  60.0 5.7 %collective-permute-start.12 = (f32[256,128]{1,0:T(8,128)S(1)}, f32[256,128]{1,0:T(8,128)S(1)}, u32[]{:S(2)}, u32[]{:S(2)}) collective-permute-start(f32[256,128]{1,0:T(8,128)S(1)} %get-tuple-element.97), channel_id=1, source_target_pairs={{0,2},{2,0},{1,3},{3,1},{4,6},{6,4},{5,7},{7,5},{8,10},{10,8},{9,1... | collective-permute-start | bytes 393224 | tf_op jit(solution)/shard_map/ppermute | solution.py:19
  63.0 4.2 %collective-permute-start.13 = (f32[256,128]{1,0:T(8,128)S(1)}, f32[256,128]{1,0:T(8,128)S(1)}, u32[]{:S(2)}, u32[]{:S(2)}) collective-permute-start(f32[256,128]{1,0:T(8,128)S(1)} %get-tuple-element.98), channel_id=1, source_target_pairs={{0,1},{1,0},{2,3},{3,2},{4,5},{5,4},{6,7},{7,6},{8,9},{9,8},{10,11... | collective-permute-start | bytes 393224 | tf_op jit(solution)/shard_map/ppermute | solution.py:19
  67.2 25.0 %collective-permute-start.14 = (f32[512,128]{1,0:T(8,128)S(1)}, f32[512,128]{1,0:T(8,128)S(1)}, u32[]{:S(2)}, u32[]{:S(2)}) collective-permute-start(f32[512,128]{1,0:T(8,128)S(1)} %pad_maximum_fusion.11), channel_id=1, source_target_pairs={{0,1},{1,0},{2,3},{3,2},{4,5},{5,4},{6,7},{7,6},{8,9},{9,8},{10,11... | collective-permute-start | bytes 786440 | tf_op jit(solution)/shard_map/ppermute | solution.py:19
  67.6 25.3 %collective-permute-start.15 = (f32[512,128]{1,0:T(8,128)S(1)}, f32[512,128]{1,0:T(8,128)S(1)}, u32[]{:S(2)}, u32[]{:S(2)}) collective-permute-start(f32[512,128]{1,0:T(8,128)S(1)} %pad_maximum_fusion.12), channel_id=1, source_target_pairs={{0,2},{2,0},{1,3},{3,1},{4,6},{6,4},{5,7},{7,5},{8,10},{10,8},{9,1... | collective-permute-start | bytes 786440 | tf_op jit(solution)/shard_map/ppermute | solution.py:19
  67.9 23.0 %collective-permute-start.16 = (f32[16,256]{1,0:T(8,128)S(1)}, f32[16,256]{1,0:T(8,128)S(1)}, u32[]{:S(2)}, u32[]{:S(2)}) collective-permute-start(f32[16,256]{1,0:T(8,128)S(1)} %pad_maximum_fusion.25), channel_id=1, source_target_pairs={{0,8},{8,0},{1,9},{9,1},{2,10},{10,2},{3,11},{11,3},{4,12},{12,4},... | collective-permute-start | bytes 49160 | tf_op jit(solution)/shard_map/ppermute | solution.py:19
  90.9 7.1 %collective-permute-start = (f32[128,384]{1,0:T(8,128)S(1)}, f32[128,384]{1,0:T(8,128)S(1)}, u32[]{:S(2)}, u32[]{:S(2)}) collective-permute-start(f32[128,384]{1,0:T(8,128)S(1)} %slice.232), channel_id=1, source_target_pairs={{16,8},{17,9},{18,10},{19,11},{20,12},{21,13},{22,14},{23,15}} | collective-permute-start | bytes 589832 | tf_op jit(solution)/shard_map/ppermute | solution.py:201
  92.2 5.8 %collective-permute-start.1 = (f32[128,384]{1,0:T(8,128)S(1)}, f32[128,384]{1,0:T(8,128)S(1)}, u32[]{:S(2)}, u32[]{:S(2)}) collective-permute-start(f32[128,384]{1,0:T(8,128)S(1)} %fusion.4), channel_id=1, source_target_pairs={{16,0},{24,16},{17,1},{25,17},{18,2},{26,18},{19,3},{27,19},{20,4}... | collective-permute-start | bytes 589832 | tf_op jit(solution)/shard_map/ppermute | solution.py:200
  94.1 10.5 %collective-permute-start.19 = (f32[1024,256]{1,0:T(8,128)}, f32[1024,256]{1,0:T(8,128)}, u32[]{:S(2)}, u32[]{:S(2)}) collective-permute-start(f32[1024,256]{1,0:T(8,128)} %pad_maximum_fusion), channel_id=1, source_target_pairs={{0,8},{8,0},{1,9},{9,1},{2,10},{10,2},{3,11},{11,3},{4,12},{12,4},... | collective-permute-start | bytes 3145736 | tf_op jit(solution)/shard_map/ppermute | solution.py:19
  108.6 14.0 %all-to-all-start = ((f32[32,1,128]{2,1,0:T(1,128)}), f32[32,1,128]{2,1,0:T(1,128)S(1)}, u32[]{:S(2)}, u32[]{:S(2)}) async-start(f32[32,1,128]{2,1,0:T(1,128)} %broadcast_in_dim.122), calls=%async_computation | async-start | bytes 32768 | tf_op jit(solution)/shard_map/all_to_all | solution.py:405
  129.9 8.0 %collective-permute-start.21 = (f32[520,128]{1,0:T(8,128)S(1)}, f32[520,128]{1,0:T(8,128)S(1)}, u32[]{:S(2)}, u32[]{:S(2)}) collective-permute-start(f32[520,128]{1,0:T(8,128)S(1)} %pad_maximum_fusion.9), channel_id=1, source_target_pairs={{0,1},{1,0},{2,3},{3,2},{4,5},{5,4},{6,7},{7,6},{8,9},{9,8},{10,11... | collective-permute-start | bytes 798728 | tf_op jit(solution)/shard_map/ppermute | solution.py:19
  130.3 7.7 %collective-permute-start.22 = (f32[520,128]{1,0:T(8,128)S(1)}, f32[520,128]{1,0:T(8,128)S(1)}, u32[]{:S(2)}, u32[]{:S(2)}) collective-permute-start(f32[520,128]{1,0:T(8,128)S(1)} %pad_maximum_fusion.10), channel_id=1, source_target_pairs={{0,2},{2,0},{1,3},{3,1},{4,6},{6,4},{5,7},{7,5},{8,10},{10,8},{9,1... | collective-permute-start | bytes 798728 | tf_op jit(solution)/shard_map/ppermute | solution.py:19
  138.4 4.2 %collective-permute-start.24 = (f32[264,128]{1,0:T(8,128)S(1)}, f32[264,128]{1,0:T(8,128)S(1)}, u32[]{:S(2)}, u32[]{:S(2)}) collective-permute-start(f32[264,128]{1,0:T(8,128)S(1)} %pad_maximum_fusion.23), channel_id=1, source_target_pairs={{0,1},{1,0},{2,3},{3,2},{4,5},{5,4},{6,7},{7,6},{8,9},{9,8},{10,11... | collective-permute-start | bytes 405512 | tf_op jit(solution)/shard_map/ppermute | solution.py:19
  143.1 7.2 %collective-permute-start.26 = (f32[136,256]{1,0:T(8,128)S(1)}, f32[136,256]{1,0:T(8,128)S(1)}, u32[]{:S(2)}, u32[]{:S(2)}) collective-permute-start(f32[136,256]{1,0:T(8,128)S(1)} %get-tuple-element.126), channel_id=1, source_target_pairs={{0,20},{4,16},{16,4},{20,0},{1,21},{5,17},{17,5},{21,1},{2,22},{6,... | collective-permute-start | bytes 417800 | tf_op jit(solution)/shard_map/ppermute | solution.py:234
  150.3 6.0 %collective-permute-start.27 = (f32[136,256]{1,0:T(8,128)S(1)}, f32[136,256]{1,0:T(8,128)S(1)}, u32[]{:S(2)}, u32[]{:S(2)}) collective-permute-start(f32[136,256]{1,0:T(8,128)S(1)} %fusion.12), channel_id=1, source_target_pairs={{0,4},{4,0},{1,5},{5,1},{2,6},{6,2},{3,7},{7,3},{8,12},{12,8},{9,1... | collective-permute-start | bytes 417800 | tf_op jit(solution)/shard_map/ppermute | solution.py:19
  156.4 5.3 %collective-permute-start.28 = (f32[256,128]{1,0:T(8,128)S(1)}, f32[256,128]{1,0:T(8,128)S(1)}, u32[]{:S(2)}, u32[]{:S(2)}) collective-permute-start(f32[256,128]{1,0:T(8,128)S(1)} %get-tuple-element.129), channel_id=1, source_target_pairs={{0,2},{2,0},{1,3},{3,1},{4,6},{6,4},{5,7},{7,5},{8,10},{10,8},{9,1... | collective-permute-start | bytes 393224 | tf_op jit(solution)/shard_map/ppermute | solution.py:19
  156.4 5.2 %collective-permute-start.29 = (f32[256,128]{1,0:T(8,128)S(1)}, f32[256,128]{1,0:T(8,128)S(1)}, u32[]{:S(2)}, u32[]{:S(2)}) collective-permute-start(f32[256,128]{1,0:T(8,128)S(1)} %get-tuple-element.130), channel_id=1, source_target_pairs={{0,1},{1,0},{2,3},{3,2},{4,5},{5,4},{6,7},{7,6},{8,9},{9,8},{10,11... | collective-permute-start | bytes 393224 | tf_op jit(solution)/shard_map/ppermute | solution.py:19
  161.7 10.1 %collective-permute-start.30 = (f32[512,128]{1,0:T(8,128)S(1)}, f32[512,128]{1,0:T(8,128)S(1)}, u32[]{:S(2)}, u32[]{:S(2)}) collective-permute-start(f32[512,128]{1,0:T(8,128)S(1)} %pad_maximum_fusion.13), channel_id=1, source_target_pairs={{0,1},{1,0},{2,3},{3,2},{4,5},{5,4},{6,7},{7,6},{8,9},{9,8},{10,11... | collective-permute-start | bytes 786440 | tf_op jit(solution)/shard_map/ppermute | solution.py:19
  162.9 8.9 %collective-permute-start.31 = (f32[512,128]{1,0:T(8,128)S(1)}, f32[512,128]{1,0:T(8,128)S(1)}, u32[]{:S(2)}, u32[]{:S(2)}) collective-permute-start(f32[512,128]{1,0:T(8,128)S(1)} %pad_maximum_fusion.14), channel_id=1, source_target_pairs={{0,2},{2,0},{1,3},{3,1},{4,6},{6,4},{5,7},{7,5},{8,10},{10,8},{9,1... | collective-permute-start | bytes 786440 | tf_op jit(solution)/shard_map/ppermute | solution.py:19
  163.0 8.8 %collective-permute-start.32 = (f32[16,256]{1,0:T(8,128)S(1)}, f32[16,256]{1,0:T(8,128)S(1)}, u32[]{:S(2)}, u32[]{:S(2)}) collective-permute-start(f32[16,256]{1,0:T(8,128)S(1)} %pad_maximum_fusion.26), channel_id=1, source_target_pairs={{0,8},{8,0},{1,9},{9,1},{2,10},{10,2},{3,11},{11,3},{4,12},{12,4},... | collective-permute-start | bytes 49160 | tf_op jit(solution)/shard_map/ppermute | solution.py:19
  172.0 6.2 %collective-permute-start.33 = (f32[1024,256]{1,0:T(8,128)S(1)}, f32[1024,256]{1,0:T(8,128)S(1)}, u32[]{:S(2)}, u32[]{:S(2)}) collective-permute-start(f32[1024,256]{1,0:T(8,128)S(1)} %pad_maximum_fusion.1), channel_id=1, source_target_pairs={{0,8},{8,0},{1,9},{9,1},{2,10},{10,2},{3,11},{11,3},{4,12},{12,4},... | collective-permute-start | bytes 3145736 | tf_op jit(solution)/shard_map/ppermute | solution.py:19
  190.7 4.7 %collective-permute-start.34 = (f32[128,256]{1,0:T(8,128)S(1)}, f32[128,256]{1,0:T(8,128)S(1)}, u32[]{:S(2)}, u32[]{:S(2)}) collective-permute-start(f32[128,256]{1,0:T(8,128)S(1)} %slice.353), channel_id=1, source_target_pairs={{0,16},{16,24},{1,17},{17,25},{2,18},{18,26},{3,19},{19,27},{4,20}... | collective-permute-start | bytes 393224 | tf_op jit(solution)/shard_map/ppermute | solution.py:208
  191.4 6.0 %collective-permute-start.35 = (f32[128,256]{1,0:T(8,128)S(1)}, f32[128,256]{1,0:T(8,128)S(1)}, u32[]{:S(2)}, u32[]{:S(2)}) collective-permute-start(f32[128,256]{1,0:T(8,128)S(1)} %slice.353), channel_id=1, source_target_pairs={{8,16},{9,17},{10,18},{11,19},{12,20},{13,21},{14,22},{15,23}} | collective-permute-start | bytes 393224 | tf_op jit(solution)/shard_map/ppermute | solution.py:209
  (17 other events, 142.5 us)

commit v4 on v3

--- a/solution.py
+++ b/solution.py
@@ -271,10 +271,16 @@
         (statistics[:, :half], statistics[:, half:]),
         bits,
     )
-    statistics = jnp.concatenate(stats, axis=1)
-    kept, sent = together(*last_messages(jnp.concatenate(parts, axis=1), statistics))
-    straight, crossed = together(across(kept, bits[-1], 0), across(sent, bits[-1], 1))
-    return statistics, straight + crossed
+    chunk = parts[0].shape[0] // 2
+    whole = jnp.concatenate(
+        [jnp.concatenate(parts, axis=1), jnp.concatenate(stats, axis=1)], axis=0
+    )
+    crossed, straight = together(across(whole, bits[-1], 1), across(whole, bits[-1], 0))
+    value = jnp.concatenate(
+        [straight[:chunk] + crossed[chunk : 2 * chunk], straight[chunk : 2 * chunk] + crossed[:chunk]],
+        axis=0,
+    )
+    return value, straight[2 * chunk :] + crossed[2 * chunk :]
 
 
 def reduce_mixed(crossing, staying, cross_stats, stay_stats, bits):
@@ -283,26 +289,24 @@
     stay_kept, stay_sent = last_messages(parts[1], stats[1])
     kept, sent, stay_sent = together(kept, sent, stay_sent)
     got = (
-        across(kept, bits[-1], 0),
         across(sent, bits[-1], 1),
         swap(stay_sent, bits[-1]),
-    )
-    straight, crossed, got = together(*got)
+        across(kept, bits[-1], 0),
+    )
+    crossed, got, straight = together(*got)
     second = lax.axis_index("side") == 1
     return straight + crossed + jnp.where(second, stay_kept + got, 0.0)
 
 
-def gather_moment(own, facing, bits):
+def gather_last(facing, bits):
     rows = facing.shape[0] - PAD
-    chunk, facing = facing[:rows], facing[rows:]
-    if own is None:
-        chunk, facing = together(chunk, facing)
-        got, own = together(swap(chunk, bits[-1]), swap(facing, "side"))
-    else:
-        got = swap(jnp.concatenate([chunk, own], axis=0), bits[-1])
-        got, own = got[:rows], own + got[rows:]
+    chunk, facing = together(facing[:rows], facing[rows:])
+    got, own = together(swap(chunk, bits[-1]), swap(facing, "side"))
+    return jnp.concatenate([chunk, got], axis=0), own, facing
+
+
+def gather_moment(value, own, facing, bits):
     both = jnp.concatenate([own, facing], axis=0)
-    value = jnp.concatenate([chunk, got], axis=0)
     half = value.shape[1] // 2
     parts = [value[:, :half], value[:, half:]]
     for stage in reversed(range(len(bits) - 1)):
@@ -371,7 +375,7 @@
         )
         staying = jnp.where(second_core, other, held)
         facing = reduce_mixed(crossing, staying, statistics, stay_stats, bits)
-        moment, own, facing = gather_moment(None, facing, bits)
+        moment, own, facing = gather_moment(*gather_last(facing, bits), bits)
 
         first, second = move(packed)
         extra = jnp.where(group == 1, second, jnp.where(group == 3, packed[half:], first))
@@ -389,8 +393,9 @@
                 scaled, statistics = weigh(logits, mass, squares, False)
                 other = swap(contract_rows(far, scaled), "core")
                 held, other = together(contract_rows(near, scaled), other)
-                own, facing = reduce_moment(held + other, statistics, bits)
-                moment, own, facing = gather_moment(own, facing, bits)
+                value, facing = reduce_moment(held + other, statistics, bits)
+                own = swap(facing, "side")
+                moment, own, facing = gather_moment(value, own, facing, bits)
             cross, other = together(times(near, moment), swap(moment, "core"))
             cross = cross + times(far, other)
             share = facing[1:2] / mass_total

time: 198 us -> 196 us (0.990)
  starting transfers between devices: 77.8 us -> 75.1 us
    ppermute x26, waiting for transfers between devices: 48.6 us -> 41.2 us  [swap(): return lax.ppermute(value, axis, [(0, 1), (1, 0)])]
    ppermute x4, waiting for transfers between devices: 16.2 us -> 23 us  [across(): return lax.ppermute(value, ('side', axis), pairs)]
    ppermute x26, starting transfers between devices: 56 us -> 53.3 us  [swap(): return lax.ppermute(value, axis, [(0, 1), (1, 0)])]
where the time goes in v4:
time: 196 us; the launch traced here: 195 us
  starting transfers between devices  75.1 us (38%)
  waiting for transfers between devices  72.8 us (37%)
  matrix products  18.3 us (9%)
  blocking collectives  10.3 us (5%)
  other arithmetic  7.51 us (4%)
  Pallas kernels  5.49 us (3%)
  local copies, waits for them, and re-layouts  4.95 us (3%)
    ppermute x26, starting transfers between devices, swap(): return lax.ppermute(value, axis, [(0, 1), (1, 0)])  53.3 us
    ppermute x26, waiting for transfers between devices, swap(): return lax.ppermute(value, axis, [(0, 1), (1, 0)])  41.2 us
    ppermute x4, waiting for transfers between devices, across(): return lax.ppermute(value, ('side', axis), pairs)  23 us
    all_to_all x1, blocking collectives, steps(): largest = jnp.max(lax.all_to_all(spread, axes, 0, 0, tiled=True), axis=0)  10.3 us
    dot_general x4, matrix products, contract_rows(): lax.dot_general(left, right, (((0,), (0,)), ((), ())), precision=highest,...  9.92 us
    dot_general x4, matrix products, times(): jnp.dot(left, right, precision=highest, preferred_element_type=jnp.float32)  8.37 us
    all_to_all x1, starting transfers between devices, steps(): largest = jnp.max(lax.all_to_all(spread, axes, 0, 0, tiled=True), axis=0)  7.2 us
    all_to_all x1, waiting for transfers between devices, steps(): largest = jnp.max(lax.all_to_all(spread, axes, 0, 0, tiled=True), axis=0)  6.65 us
  transfers between devices with their start and end apart: 37, of which 24 were waited for; matrix products, arithmetic and copies ran while one was open for 7% of the time, Pallas kernels for 1%

profile of v4, /device:TPU:1, one launch (start us, length us, event | category | flops | bytes accessed | tf_op | source)
XLA Modules:
  0.0 195.3 jit_solution(8774326896006894924)
XLA Ops:
  0.0 3.1 %base_rows.1 = (f32[384,1024]{1,0:T(8,128)}, f32[384,1024]{1,0:T(8,128)}, f32[256,1024]{1,0:T(8,128)S(1)}, f32[256,128]{1,0:T(8,128)S(1)}) custom-call(f32[256,2048]{1,0:T(8,128)} %points.3), custom_call_target="tpu_custom_call" | custom-call | tf_op jit(solution)/shard_map/base_rows/pallas_call | solution.py:139
  3.9 2.8 %convolution_bitcast_fusion = f32[1024,256]{1,0:T(8,128)} fusion(f32[256,256]{1,0:T(8,128)S(1)} %get-tuple-element.155, f32[256,1024]{1,0:T(8,128)S(1)} %get-tuple-element.75), kind=kOutput, calls=%fused_computation | convolution fusion | flops 805306368 | bytes 2359296 | tf_op jit(solution)/shard_map/dot_general | solution.py:31
  7.0 1.8 convolution_bitcast_fusion.1
  9.9 2.4 %collective-permute-start.3 = (f32[520,256]{1,0:T(8,128)S(1)}, f32[520,256]{1,0:T(8,128)S(1)}, u32[]{:S(2)}, u32[]{:S(2)}) collective-permute-start(f32[520,256]{1,0:T(8,128)S(1)} %get-tuple-element.78), channel_id=1, source_target_pairs={{0,1},{1,0},{2,3},{3,2},{4,5},{5,4},{6,7},{7,6},{8,9},{9,8},{10,11... | collective-permute-start | bytes 1597448 | tf_op jit(solution)/shard_map/ppermute | solution.py:19
  13.6 10.8 %collective-permute-done.3 = f32[520,256]{1,0:T(8,128)S(1)} collective-permute-done((f32[520,256]{1,0:T(8,128)S(1)}, f32[520,256]{1,0:T(8,128)S(1)}, u32[]{:S(2)}, u32[]{:S(2)}) %collective-permute-start.3) | collective-permute-done | bytes 532512 | tf_op jit(solution)/shard_map/ppermute | solution.py:19
  27.4 4.9 %collective-permute-done.5 = f32[264,256]{1,0:T(8,128)S(1)} collective-permute-done((f32[264,256]{1,0:T(8,128)S(1)}, f32[264,256]{1,0:T(8,128)S(1)}, u32[]{:S(2)}, u32[]{:S(2)}) %collective-permute-start.5) | collective-permute-done | bytes 270368 | tf_op jit(solution)/shard_map/ppermute | solution.py:19
  34.2 3.2 %collective-permute-start.7 = (f32[136,256]{1,0:T(8,128)}, f32[136,256]{1,0:T(8,128)S(1)}, u32[]{:S(2)}, u32[]{:S(2)}) collective-permute-start(f32[136,256]{1,0:T(8,128)} %get-tuple-element.86), channel_id=1, source_target_pairs={{0,20},{4,16},{16,4},{20,0},{1,21},{5,17},{17,5},{21,1},{2,22},{6,... | collective-permute-start | bytes 417800 | tf_op jit(solution)/shard_map/ppermute | solution.py:234
  37.7 9.4 %collective-permute-done.7 = f32[136,256]{1,0:T(8,128)S(1)} collective-permute-done((f32[136,256]{1,0:T(8,128)}, f32[136,256]{1,0:T(8,128)S(1)}, u32[]{:S(2)}, u32[]{:S(2)}) %collective-permute-start.7) | collective-permute-done | bytes 139296 | tf_op jit(solution)/shard_map/ppermute | solution.py:234
  47.1 3.0 %collective-permute-done.8 = f32[136,256]{1,0:T(8,128)S(1)} collective-permute-done((f32[136,256]{1,0:T(8,128)S(1)}, f32[136,256]{1,0:T(8,128)S(1)}, u32[]{:S(2)}, u32[]{:S(2)}) %collective-permute-start.8) | collective-permute-done | bytes 139296 | tf_op jit(solution)/shard_map/ppermute | solution.py:19
  51.4 1.6 collective-permute-start.17
  55.4 2.1 %collective-permute-start.11 = (f32[8,256]{1,0:T(8,128)S(1)}, f32[8,256]{1,0:T(8,128)S(1)}, u32[]{:S(2)}, u32[]{:S(2)}) collective-permute-start(f32[8,256]{1,0:T(8,128)S(1)} %slice.321), channel_id=1, source_target_pairs={{0,16},{16,0},{1,17},{17,1},{2,18},{18,2},{3,19},{19,3},{4,20},{20... | collective-permute-start | bytes 24584 | tf_op jit(solution)/shard_map/ppermute | solution.py:19
  57.5 1.5 collective-permute-done.11
  59.0 2.9 %collective-permute-start.12 = (f32[256,128]{1,0:T(8,128)S(1)}, f32[256,128]{1,0:T(8,128)S(1)}, u32[]{:S(2)}, u32[]{:S(2)}) collective-permute-start(f32[256,128]{1,0:T(8,128)S(1)} %get-tuple-element.95), channel_id=1, source_target_pairs={{0,2},{2,0},{1,3},{3,1},{4,6},{6,4},{5,7},{7,5},{8,10},{10,8},{9,1... | collective-permute-start | bytes 393224 | tf_op jit(solution)/shard_map/ppermute | solution.py:19
  62.3 2.4 %collective-permute-done.12 = f32[256,128]{1,0:T(8,128)S(1)} collective-permute-done((f32[256,128]{1,0:T(8,128)S(1)}, f32[256,128]{1,0:T(8,128)S(1)}, u32[]{:S(2)}, u32[]{:S(2)}) %collective-permute-start.12) | collective-permute-done | bytes 131104 | tf_op jit(solution)/shard_map/ppermute | solution.py:19
  66.9 23.2 %collective-permute-start.16 = (f32[16,256]{1,0:T(8,128)S(1)}, f32[16,256]{1,0:T(8,128)S(1)}, u32[]{:S(2)}, u32[]{:S(2)}) collective-permute-start(f32[16,256]{1,0:T(8,128)S(1)} %pad_maximum_fusion.23), channel_id=1, source_target_pairs={{0,8},{8,0},{1,9},{9,1},{2,10},{10,2},{3,11},{11,3},{4,12},{12,4},... | collective-permute-start | bytes 49160 | tf_op jit(solution)/shard_map/ppermute | solution.py:19
  94.1 3.9 %collective-permute-start.19 = (f32[1024,256]{1,0:T(8,128)}, f32[1024,256]{1,0:T(8,128)}, u32[]{:S(2)}, u32[]{:S(2)}) collective-permute-start(f32[1024,256]{1,0:T(8,128)} %pad_maximum_fusion), channel_id=1, source_target_pairs={{0,8},{8,0},{1,9},{9,1},{2,10},{10,2},{3,11},{11,3},{4,12},{12,4},... | collective-permute-start | bytes 3145736 | tf_op jit(solution)/shard_map/ppermute | solution.py:19
  99.2 2.4 %shard_map.37 = (f32[384,1024]{1,0:T(8,128)}, f32[384,1024]{1,0:T(8,128)}) custom-call(f32[256,2048]{1,0:T(8,128)} %points.3, f32[128,2048]{1,0:T(8,128)} %collective-permute-done.17.first, f32[128,2048]{1,0:T(8,128)} %copy-done.5, f32[384,1024]{1,0:T(8,128)} %get-tuple-element.74.near_in, ...), custom_call_target="tpu_custom_call", output_to_operand_aliasing={{0}: (3, {}), {1}: (4, {})} | custom-call | tf_op jit(solution)/shard_map/pallas_call | solution.py:172
  101.7 2.9 %fusion.20 = f32[384,256]{1,0:T(8,128)S(1)} fusion(f32[384,1024]{1,0:T(8,128)} %get-tuple-element.107, f32[1024,128]{1,0:T(8,128)S(1)} %bitcast.52, f32[512,128]{1,0:T(8,128)S(1)} %collective-permute-done.14, f32[512,128]{1,0:T(8,128)S(1)} %pad_maximum_fusion.11), kind=kOutput, calls=%fused_computation.113 | convolution fusion | flops 1208483840 | bytes 3014656 | tf_op jit(solution)/shard_map/dot_general | solution.py:41
  104.6 2.6 %fusion.32 = f32[384,256]{1,0:T(8,128)S(1)} fusion(f32[384,1024]{1,0:T(8,128)S(1)} %copy-done.2, f32[1024,256]{1,0:T(8,128)} %collective-permute-done.19), kind=kOutput, calls=%fused_computation.125 | convolution fusion | flops 1207959552 | bytes 3014656 | tf_op jit(solution)/shard_map/dot_general | solution.py:41
  108.6 7.2 %all-to-all-start = ((f32[32,1,128]{2,1,0:T(1,128)}), f32[32,1,128]{2,1,0:T(1,128)S(1)}, u32[]{:S(2)}, u32[]{:S(2)}) async-start(f32[32,1,128]{2,1,0:T(1,128)} %broadcast_in_dim.122), calls=%async_computation | async-start | bytes 32768 | tf_op jit(solution)/shard_map/all_to_all | solution.py:410
  115.9 6.6 %all-to-all-done = f32[32,1,128]{2,1,0:T(1,128)S(1)} async-done(((f32[32,1,128]{2,1,0:T(1,128)}), f32[32,1,128]{2,1,0:T(1,128)S(1)}, u32[]{:S(2)}, u32[]{:S(2)}) %all-to-all-start) | async-done | bytes 16416 | tf_op jit(solution)/shard_map/all_to_all | solution.py:410
  123.3 2.6 %fusion.34 = f32[1024,256]{1,0:T(8,128)S(1)} fusion(f32[384,1024]{1,0:T(8,128)S(1)} %copy-done.2, f32[384,256]{1,0:T(8,128)S(1)} %get-tuple-element.148), kind=kOutput, calls=%fused_computation.127 | convolution fusion | flops 1207959552 | bytes 3014656 | tf_op jit(solution)/shard_map/dot_general | solution.py:31
  126.9 2.6 %fusion.33 = f32[1024,256]{1,0:T(8,128)S(1)} fusion(f32[384,1024]{1,0:T(8,128)S(1)} %copy-done.1, f32[384,256]{1,0:T(8,128)S(1)} %get-tuple-element.148), kind=kOutput, calls=%fused_computation.126 | convolution fusion | flops 1207959552 | bytes 3014656 | tf_op jit(solution)/shard_map/dot_general | solution.py:31
  130.5 7.3 %collective-permute-done.21 = f32[520,128]{1,0:T(8,128)S(1)} collective-permute-done((f32[520,128]{1,0:T(8,128)S(1)}, f32[520,128]{1,0:T(8,128)S(1)}, u32[]{:S(2)}, u32[]{:S(2)}) %collective-permute-start.21) | collective-permute-done | bytes 266272 | tf_op jit(solution)/shard_map/ppermute | solution.py:19
  139.5 2.5 %collective-permute-done.23 = f32[264,128]{1,0:T(8,128)S(1)} collective-permute-done((f32[264,128]{1,0:T(8,128)S(1)}, f32[264,128]{1,0:T(8,128)S(1)}, u32[]{:S(2)}, u32[]{:S(2)}) %collective-permute-start.23) | collective-permute-done | bytes 135200 | tf_op jit(solution)/shard_map/ppermute | solution.py:19
  144.2 13.6 %collective-permute-done.25 = f32[264,256]{1,0:T(8,128)S(1)} collective-permute-done((f32[264,256]{1,0:T(8,128)S(1)}, f32[264,256]{1,0:T(8,128)S(1)}, u32[]{:S(2)}, u32[]{:S(2)}) %collective-permute-start.25) | collective-permute-done | bytes 270368 | tf_op jit(solution)/shard_map/ppermute | solution.py:234
  163.0 1.7 collective-permute-start.31
  164.7 3.1 %collective-permute-start.32 = (f32[16,256]{1,0:T(8,128)S(1)}, f32[16,256]{1,0:T(8,128)S(1)}, u32[]{:S(2)}, u32[]{:S(2)}) collective-permute-start(f32[16,256]{1,0:T(8,128)S(1)} %pad_maximum_fusion.24), channel_id=1, source_target_pairs={{0,8},{8,0},{1,9},{9,1},{2,10},{10,2},{3,11},{11,3},{4,12},{12,4},... | collective-permute-start | bytes 49160 | tf_op jit(solution)/shard_map/ppermute | solution.py:19
  168.9 3.6 %collective-permute-start.33 = (f32[1024,256]{1,0:T(8,128)S(1)}, f32[1024,256]{1,0:T(8,128)S(1)}, u32[]{:S(2)}, u32[]{:S(2)}) collective-permute-start(f32[1024,256]{1,0:T(8,128)S(1)} %pad_maximum_fusion.1), channel_id=1, source_target_pairs={{0,8},{8,0},{1,9},{9,1},{2,10},{10,2},{3,11},{11,3},{4,12},{12,4},... | collective-permute-start | bytes 3145736 | tf_op jit(solution)/shard_map/ppermute | solution.py:19
  176.9 10.3 %all_to_all.12 = f32[32,1,128]{2,1,0:T(1,128)S(1)} all-to-all(f32[32,1,128]{2,1,0:T(1,128)S(1)} %broadcast_in_dim.128), channel_id=1, replica_groups=mesh['side'=2,'core'=2,'bit2'=2,'bit1'=2,'bit0'=2] {'side','core','bit2'..., dimensions={0} | all-to-all | bytes 32768 | tf_op jit(solution)/shard_map/all_to_all | solution.py:410
  188.6 4.0 %collective-permute-start.35 = (f32[128,256]{1,0:T(8,128)S(1)}, f32[128,256]{1,0:T(8,128)S(1)}, u32[]{:S(2)}, u32[]{:S(2)}) collective-permute-start(f32[128,256]{1,0:T(8,128)S(1)} %slice.347), channel_id=1, source_target_pairs={{8,16},{9,17},{10,18},{11,19},{12,20},{13,21},{14,22},{15,23}} | collective-permute-start | bytes 393224 | tf_op jit(solution)/shard_map/ppermute | solution.py:209
  192.6 1.9 collective-permute-done.35
  (195 shorter events, 40.2 us)
Async XLA Ops:
  9.9 14.5 %collective-permute-start.3 = (f32[520,256]{1,0:T(8,128)S(1)}, f32[520,256]{1,0:T(8,128)S(1)}, u32[]{:S(2)}, u32[]{:S(2)}) collective-permute-start(f32[520,256]{1,0:T(8,128)S(1)} %get-tuple-element.78), channel_id=1, source_target_pairs={{0,1},{1,0},{2,3},{3,2},{4,5},{5,4},{6,7},{7,6},{8,9},{9,8},{10,11... | collective-permute-start | bytes 1597448 | tf_op jit(solution)/shard_map/ppermute | solution.py:19
  12.4 13.0 %collective-permute-start.4 = (f32[520,256]{1,0:T(8,128)S(1)}, f32[520,256]{1,0:T(8,128)S(1)}, u32[]{:S(2)}, u32[]{:S(2)}) collective-permute-start(f32[520,256]{1,0:T(8,128)S(1)} %get-tuple-element.79), channel_id=1, source_target_pairs={{0,2},{2,0},{1,3},{3,1},{4,6},{6,4},{5,7},{7,5},{8,10},{10,8},{9,1... | collective-permute-start | bytes 1597448 | tf_op jit(solution)/shard_map/ppermute | solution.py:19
  25.7 6.6 %collective-permute-start.5 = (f32[264,256]{1,0:T(8,128)S(1)}, f32[264,256]{1,0:T(8,128)S(1)}, u32[]{:S(2)}, u32[]{:S(2)}) collective-permute-start(f32[264,256]{1,0:T(8,128)S(1)} %pad_maximum_fusion.7), channel_id=1, source_target_pairs={{0,2},{2,0},{1,3},{3,1},{4,6},{6,4},{5,7},{7,5},{8,10},{10,8},{9,1... | collective-permute-start | bytes 811016 | tf_op jit(solution)/shard_map/ppermute | solution.py:19
  27.1 6.2 %collective-permute-start.6 = (f32[264,256]{1,0:T(8,128)S(1)}, f32[264,256]{1,0:T(8,128)S(1)}, u32[]{:S(2)}, u32[]{:S(2)}) collective-permute-start(f32[264,256]{1,0:T(8,128)S(1)} %pad_maximum_fusion.8), channel_id=1, source_target_pairs={{0,1},{1,0},{2,3},{3,2},{4,5},{5,4},{6,7},{7,6},{8,9},{9,8},{10,11... | collective-permute-start | bytes 811016 | tf_op jit(solution)/shard_map/ppermute | solution.py:19
  34.2 13.0 %collective-permute-start.7 = (f32[136,256]{1,0:T(8,128)}, f32[136,256]{1,0:T(8,128)S(1)}, u32[]{:S(2)}, u32[]{:S(2)}) collective-permute-start(f32[136,256]{1,0:T(8,128)} %get-tuple-element.86), channel_id=1, source_target_pairs={{0,20},{4,16},{16,4},{20,0},{1,21},{5,17},{17,5},{21,1},{2,22},{6,... | collective-permute-start | bytes 417800 | tf_op jit(solution)/shard_map/ppermute | solution.py:234
  37.4 12.7 %collective-permute-start.8 = (f32[136,256]{1,0:T(8,128)S(1)}, f32[136,256]{1,0:T(8,128)S(1)}, u32[]{:S(2)}, u32[]{:S(2)}) collective-permute-start(f32[136,256]{1,0:T(8,128)S(1)} %pad_maximum_fusion.19), channel_id=1, source_target_pairs={{0,4},{4,0},{1,5},{5,1},{2,6},{6,2},{3,7},{7,3},{8,12},{12,8},{9,1... | collective-permute-start | bytes 417800 | tf_op jit(solution)/shard_map/ppermute | solution.py:19
  37.5 12.7 %collective-permute-start.9 = (f32[136,256]{1,0:T(8,128)S(1)}, f32[136,256]{1,0:T(8,128)S(1)}, u32[]{:S(2)}, u32[]{:S(2)}) collective-permute-start(f32[136,256]{1,0:T(8,128)S(1)} %get-tuple-element.88), channel_id=1, source_target_pairs={{0,16},{4,20},{16,0},{20,4},{1,17},{5,21},{17,1},{21,5},{2,18},{6,... | collective-permute-start | bytes 417800 | tf_op jit(solution)/shard_map/ppermute | solution.py:234
  50.2 8.8 %collective-permute-start.10 = (f32[128,256]{1,0:T(8,128)S(1)}, f32[128,256]{1,0:T(8,128)S(1)}, u32[]{:S(2)}, u32[]{:S(2)}) collective-permute-start(f32[128,256]{1,0:T(8,128)S(1)} %slice.320), channel_id=1, source_target_pairs={{0,4},{4,0},{1,5},{5,1},{2,6},{6,2},{3,7},{7,3},{8,12},{12,8},{9,1... | collective-permute-start | bytes 393224 | tf_op jit(solution)/shard_map/ppermute | solution.py:19
  51.4 46.8 %collective-permute-start.17 = (f32[128,2048]{1,0:T(8,128)}, f32[128,2048]{1,0:T(8,128)}, u32[]{:S(2)}, u32[]{:S(2)}) collective-permute-start(f32[128,2048]{1,0:T(8,128)} %slice.263), channel_id=1, source_target_pairs={{16,0},{24,16},{17,1},{25,17},{18,2},{26,18},{19,3},{27,19},{20,4}... | collective-permute-start | bytes 3145736 | tf_op jit(solution)/shard_map/ppermute | solution.py:200
  54.1 44.1 %collective-permute-start.18 = (f32[128,2048]{1,0:T(8,128)}, f32[128,2048]{1,0:T(8,128)S(1)}, u32[]{:S(2)}, u32[]{:S(2)}) collective-permute-start(f32[128,2048]{1,0:T(8,128)} %slice.264), channel_id=1, source_target_pairs={{16,8},{17,9},{18,10},{19,11},{20,12},{21,13},{22,14},{23,15}} | collective-permute-start | bytes 3145736 | tf_op jit(solution)/shard_map/ppermute | solution.py:201
  59.0 5.7 %collective-permute-start.12 = (f32[256,128]{1,0:T(8,128)S(1)}, f32[256,128]{1,0:T(8,128)S(1)}, u32[]{:S(2)}, u32[]{:S(2)}) collective-permute-start(f32[256,128]{1,0:T(8,128)S(1)} %get-tuple-element.95), channel_id=1, source_target_pairs={{0,2},{2,0},{1,3},{3,1},{4,6},{6,4},{5,7},{7,5},{8,10},{10,8},{9,1... | collective-permute-start | bytes 393224 | tf_op jit(solution)/shard_map/ppermute | solution.py:19
  62.0 4.2 %collective-permute-start.13 = (f32[256,128]{1,0:T(8,128)S(1)}, f32[256,128]{1,0:T(8,128)S(1)}, u32[]{:S(2)}, u32[]{:S(2)}) collective-permute-start(f32[256,128]{1,0:T(8,128)S(1)} %get-tuple-element.96), channel_id=1, source_target_pairs={{0,1},{1,0},{2,3},{3,2},{4,5},{5,4},{6,7},{7,6},{8,9},{9,8},{10,11... | collective-permute-start | bytes 393224 | tf_op jit(solution)/shard_map/ppermute | solution.py:19
  66.2 26.0 %collective-permute-start.14 = (f32[512,128]{1,0:T(8,128)S(1)}, f32[512,128]{1,0:T(8,128)S(1)}, u32[]{:S(2)}, u32[]{:S(2)}) collective-permute-start(f32[512,128]{1,0:T(8,128)S(1)} %pad_maximum_fusion.11), channel_id=1, source_target_pairs={{0,1},{1,0},{2,3},{3,2},{4,5},{5,4},{6,7},{7,6},{8,9},{9,8},{10,11... | collective-permute-start | bytes 786440 | tf_op jit(solution)/shard_map/ppermute | solution.py:19
  66.6 26.2 %collective-permute-start.15 = (f32[512,128]{1,0:T(8,128)S(1)}, f32[512,128]{1,0:T(8,128)S(1)}, u32[]{:S(2)}, u32[]{:S(2)}) collective-permute-start(f32[512,128]{1,0:T(8,128)S(1)} %pad_maximum_fusion.12), channel_id=1, source_target_pairs={{0,2},{2,0},{1,3},{3,1},{4,6},{6,4},{5,7},{7,5},{8,10},{10,8},{9,1... | collective-permute-start | bytes 786440 | tf_op jit(solution)/shard_map/ppermute | solution.py:19
  66.9 24.0 %collective-permute-start.16 = (f32[16,256]{1,0:T(8,128)S(1)}, f32[16,256]{1,0:T(8,128)S(1)}, u32[]{:S(2)}, u32[]{:S(2)}) collective-permute-start(f32[16,256]{1,0:T(8,128)S(1)} %pad_maximum_fusion.23), channel_id=1, source_target_pairs={{0,8},{8,0},{1,9},{9,1},{2,10},{10,2},{3,11},{11,3},{4,12},{12,4},... | collective-permute-start | bytes 49160 | tf_op jit(solution)/shard_map/ppermute | solution.py:19
  90.9 7.1 %collective-permute-start = (f32[128,384]{1,0:T(8,128)S(1)}, f32[128,384]{1,0:T(8,128)S(1)}, u32[]{:S(2)}, u32[]{:S(2)}) collective-permute-start(f32[128,384]{1,0:T(8,128)S(1)} %slice.232), channel_id=1, source_target_pairs={{16,8},{17,9},{18,10},{19,11},{20,12},{21,13},{22,14},{23,15}} | collective-permute-start | bytes 589832 | tf_op jit(solution)/shard_map/ppermute | solution.py:201
  92.2 5.8 %collective-permute-start.1 = (f32[128,384]{1,0:T(8,128)S(1)}, f32[128,384]{1,0:T(8,128)S(1)}, u32[]{:S(2)}, u32[]{:S(2)}) collective-permute-start(f32[128,384]{1,0:T(8,128)S(1)} %fusion.4), channel_id=1, source_target_pairs={{16,0},{24,16},{17,1},{25,17},{18,2},{26,18},{19,3},{27,19},{20,4}... | collective-permute-start | bytes 589832 | tf_op jit(solution)/shard_map/ppermute | solution.py:200
  94.1 10.5 %collective-permute-start.19 = (f32[1024,256]{1,0:T(8,128)}, f32[1024,256]{1,0:T(8,128)}, u32[]{:S(2)}, u32[]{:S(2)}) collective-permute-start(f32[1024,256]{1,0:T(8,128)} %pad_maximum_fusion), channel_id=1, source_target_pairs={{0,8},{8,0},{1,9},{9,1},{2,10},{10,2},{3,11},{11,3},{4,12},{12,4},... | collective-permute-start | bytes 3145736 | tf_op jit(solution)/shard_map/ppermute | solution.py:19
  108.6 14.0 %all-to-all-start = ((f32[32,1,128]{2,1,0:T(1,128)}), f32[32,1,128]{2,1,0:T(1,128)S(1)}, u32[]{:S(2)}, u32[]{:S(2)}) async-start(f32[32,1,128]{2,1,0:T(1,128)} %broadcast_in_dim.122), calls=%async_computation | async-start | bytes 32768 | tf_op jit(solution)/shard_map/all_to_all | solution.py:410
  129.9 8.0 %collective-permute-start.21 = (f32[520,128]{1,0:T(8,128)S(1)}, f32[520,128]{1,0:T(8,128)S(1)}, u32[]{:S(2)}, u32[]{:S(2)}) collective-permute-start(f32[520,128]{1,0:T(8,128)S(1)} %pad_maximum_fusion.9), channel_id=1, source_target_pairs={{0,1},{1,0},{2,3},{3,2},{4,5},{5,4},{6,7},{7,6},{8,9},{9,8},{10,11... | collective-permute-start | bytes 798728 | tf_op jit(solution)/shard_map/ppermute | solution.py:19
  130.3 7.7 %collective-permute-start.22 = (f32[520,128]{1,0:T(8,128)S(1)}, f32[520,128]{1,0:T(8,128)S(1)}, u32[]{:S(2)}, u32[]{:S(2)}) collective-permute-start(f32[520,128]{1,0:T(8,128)S(1)} %pad_maximum_fusion.10), channel_id=1, source_target_pairs={{0,2},{2,0},{1,3},{3,1},{4,6},{6,4},{5,7},{7,5},{8,10},{10,8},{9,1... | collective-permute-start | bytes 798728 | tf_op jit(solution)/shard_map/ppermute | solution.py:19
  138.1 3.9 %collective-permute-start.23 = (f32[264,128]{1,0:T(8,128)S(1)}, f32[264,128]{1,0:T(8,128)S(1)}, u32[]{:S(2)}, u32[]{:S(2)}) collective-permute-start(f32[264,128]{1,0:T(8,128)S(1)} %pad_maximum_fusion.20), channel_id=1, source_target_pairs={{0,2},{2,0},{1,3},{3,1},{4,6},{6,4},{5,7},{7,5},{8,10},{10,8},{9,1... | collective-permute-start | bytes 405512 | tf_op jit(solution)/shard_map/ppermute | solution.py:19
  138.4 4.2 %collective-permute-start.24 = (f32[264,128]{1,0:T(8,128)S(1)}, f32[264,128]{1,0:T(8,128)S(1)}, u32[]{:S(2)}, u32[]{:S(2)}) collective-permute-start(f32[264,128]{1,0:T(8,128)S(1)} %pad_maximum_fusion.21), channel_id=1, source_target_pairs={{0,1},{1,0},{2,3},{3,2},{4,5},{5,4},{6,7},{7,6},{8,9},{9,8},{10,11... | collective-permute-start | bytes 405512 | tf_op jit(solution)/shard_map/ppermute | solution.py:19
  142.7 15.1 %collective-permute-start.25 = (f32[264,256]{1,0:T(8,128)S(1)}, f32[264,256]{1,0:T(8,128)S(1)}, u32[]{:S(2)}, u32[]{:S(2)}) collective-permute-start(f32[264,256]{1,0:T(8,128)S(1)} %maximum_maximum_fusion), channel_id=1, source_target_pairs={{0,20},{4,16},{16,4},{20,0},{1,21},{5,17},{17,5},{21,1},{2,22},{6,... | collective-permute-start | bytes 811016 | tf_op jit(solution)/shard_map/ppermute | solution.py:234
  143.0 14.8 %collective-permute-start.26 = (f32[264,256]{1,0:T(8,128)S(1)}, f32[264,256]{1,0:T(8,128)S(1)}, u32[]{:S(2)}, u32[]{:S(2)}) collective-permute-start(f32[264,256]{1,0:T(8,128)S(1)} %maximum_maximum_fusion), channel_id=1, source_target_pairs={{0,16},{4,20},{16,0},{20,4},{1,17},{5,21},{17,1},{21,5},{2,18},{6,... | collective-permute-start | bytes 811016 | tf_op jit(solution)/shard_map/ppermute | solution.py:234
  157.9 3.9 %collective-permute-start.27 = (f32[256,128]{1,0:T(8,128)S(1)}, f32[256,128]{1,0:T(8,128)S(1)}, u32[]{:S(2)}, u32[]{:S(2)}) collective-permute-start(f32[256,128]{1,0:T(8,128)S(1)} %get-tuple-element.125), channel_id=1, source_target_pairs={{0,2},{2,0},{1,3},{3,1},{4,6},{6,4},{5,7},{7,5},{8,10},{10,8},{9,1... | collective-permute-start | bytes 393224 | tf_op jit(solution)/shard_map/ppermute | solution.py:19
  161.9 6.8 %collective-permute-start.30 = (f32[512,128]{1,0:T(8,128)S(1)}, f32[512,128]{1,0:T(8,128)S(1)}, u32[]{:S(2)}, u32[]{:S(2)}) collective-permute-start(f32[512,128]{1,0:T(8,128)S(1)} %pad_maximum_fusion.13), channel_id=1, source_target_pairs={{0,1},{1,0},{2,3},{3,2},{4,5},{5,4},{6,7},{7,6},{8,9},{9,8},{10,11... | collective-permute-start | bytes 786440 | tf_op jit(solution)/shard_map/ppermute | solution.py:19
  163.0 5.7 %collective-permute-start.31 = (f32[512,128]{1,0:T(8,128)S(1)}, f32[512,128]{1,0:T(8,128)S(1)}, u32[]{:S(2)}, u32[]{:S(2)}) collective-permute-start(f32[512,128]{1,0:T(8,128)S(1)} %pad_maximum_fusion.14), channel_id=1, source_target_pairs={{0,2},{2,0},{1,3},{3,1},{4,6},{6,4},{5,7},{7,5},{8,10},{10,8},{9,1... | collective-permute-start | bytes 786440 | tf_op jit(solution)/shard_map/ppermute | solution.py:19
  164.7 4.0 %collective-permute-start.32 = (f32[16,256]{1,0:T(8,128)S(1)}, f32[16,256]{1,0:T(8,128)S(1)}, u32[]{:S(2)}, u32[]{:S(2)}) collective-permute-start(f32[16,256]{1,0:T(8,128)S(1)} %pad_maximum_fusion.24), channel_id=1, source_target_pairs={{0,8},{8,0},{1,9},{9,1},{2,10},{10,2},{3,11},{11,3},{4,12},{12,4},... | collective-permute-start | bytes 49160 | tf_op jit(solution)/shard_map/ppermute | solution.py:19
  168.9 5.8 %collective-permute-start.33 = (f32[1024,256]{1,0:T(8,128)S(1)}, f32[1024,256]{1,0:T(8,128)S(1)}, u32[]{:S(2)}, u32[]{:S(2)}) collective-permute-start(f32[1024,256]{1,0:T(8,128)S(1)} %pad_maximum_fusion.1), channel_id=1, source_target_pairs={{0,8},{8,0},{1,9},{9,1},{2,10},{10,2},{3,11},{11,3},{4,12},{12,4},... | collective-permute-start | bytes 3145736 | tf_op jit(solution)/shard_map/ppermute | solution.py:19
  187.9 4.7 %collective-permute-start.34 = (f32[128,256]{1,0:T(8,128)S(1)}, f32[128,256]{1,0:T(8,128)S(1)}, u32[]{:S(2)}, u32[]{:S(2)}) collective-permute-start(f32[128,256]{1,0:T(8,128)S(1)} %slice.347), channel_id=1, source_target_pairs={{0,16},{16,24},{1,17},{17,25},{2,18},{18,26},{3,19},{19,27},{4,20}... | collective-permute-start | bytes 393224 | tf_op jit(solution)/shard_map/ppermute | solution.py:208
  188.6 6.0 %collective-permute-start.35 = (f32[128,256]{1,0:T(8,128)S(1)}, f32[128,256]{1,0:T(8,128)S(1)}, u32[]{:S(2)}, u32[]{:S(2)}) collective-permute-start(f32[128,256]{1,0:T(8,128)S(1)} %slice.347), channel_id=1, source_target_pairs={{8,16},{9,17},{10,18},{11,19},{12,20},{13,21},{14,22},{15,23}} | collective-permute-start | bytes 393224 | tf_op jit(solution)/shard_map/ppermute | solution.py:209
  (17 other events, 139.7 us)
